TPU v7x, 128 devices: a whole 4x4x4 slice. The times are simulated.
128 devices in a mesh: lon: 16 (over x, y_lo, core), lat: 8 (over z, y_hi).
Axes of the slice: x: 4, y: 4 (y_hi: 2, y_lo: 2; y = y_hi * 2 + y_lo), z: 4, core: 2. Of those that a mesh axis runs over, the one named last changes fastest.
Arguments:
- heat_content_field: float32 [12, 768, 2048], P(None, 'lat', 'lon'), may hold values from -6 to 6
- saltiness_field: float32 [12, 768, 2048], P(None, 'lat', 'lon'), may hold values from -6 to 6
- eastward_cfl_number: float32 [12, 768, 2048], P(None, 'lat', 'lon'), may hold values from -0.4 to 0.4
- northward_cfl_number: float32 [12, 768, 2048], P(None, 'lat', 'lon'), may hold values from -0.4 to 0.4
- seawater_indicator: int32 [768, 2048], P('lat', 'lon'), may hold values 0 or 1
- submerged_layer_total: int32 [768, 2048], P('lat', 'lon'), may hold values from 1 to 12
- seam_partner_index: int32 [2048], replicated, may hold values from 0 to 2047, as said below
Outputs:
- new_temperature: float32 [12, 768, 2048], P(None, 'lat', 'lon')
- new_salinity: float32 [12, 768, 2048], P(None, 'lat', 'lon')
Inputs may be any that keep to these rules, and one draw needn't show every extreme that they name: Each column appears once; the map is a reflection of the columns about a pivot, seam_partner_index[i] = (s - i) mod 2048.
All inputs are finite; a program needn't handle non-finite values. No bound on the sum of `seawater_indicator` on one device may be relied on, other than what follows from the above.
Results may differ from a plain program's by a relative error of at most 0.0003.
Values sent between devices are 32-bit elements; how exact they have to be, the bound alone decides.
A program may use at most 192 MiB of HBM per device.

v0:
```python
from functools import reduce

import jax
import jax.numpy as jnp
from jax import lax
from jax.sharding import PartitionSpec as P

RATIO_FLOOR = 0.05
SLOPE_FLOOR = 0.5
SLOPE_LIMIT = 2.0
DIFFUSIVITY = 0.1
THERMAL_COEF = 0.2
HALINE_COEF = 0.8
STATE_SIGNS = (1.0, 1.0, -1.0, -1.0, 1.0)


def extended(cells, sides, width, closed):
    for axis, dim in sides:
        count = lax.axis_size(axis)
        ends = count if closed else count - 1
        head = lax.slice_in_dim(cells, 0, width, axis=dim)
        tail = lax.slice_in_dim(cells, cells.shape[dim] - width, cells.shape[dim], axis=dim)
        cells = jnp.concatenate(
            [
                lax.ppermute(tail, axis, [(i, (i + 1) % count) for i in range(ends)]),
                cells,
                lax.ppermute(head, axis, [((i + 1) % count, i) for i in range(ends)]),
            ],
            axis=dim,
        )
    return cells


def sign_column(values):
    return jnp.array(values, jnp.float32).reshape(len(values), 1, 1, 1)


def sided(core, west_col, east_col, south_row, north_row):
    width = core.shape[-1]
    height = core.shape[-2]
    lane = lax.broadcasted_iota(jnp.int32, core.shape, core.ndim - 1)
    level = lax.broadcasted_iota(jnp.int32, core.shape, core.ndim - 2)
    at_east = jnp.where(lane == width - 1, east_col, jnp.roll(core, -1, axis=-1))
    at_west = jnp.where(lane == 0, west_col, jnp.roll(core, 1, axis=-1))
    at_north = jnp.where(level == height - 1, north_row, jnp.roll(core, -1, axis=-2))
    at_south = jnp.where(level == 0, south_row, jnp.roll(core, 1, axis=-2))
    return (core, at_east, at_west, at_north, at_south)


def low_order(tracer, zonal, meridional, wet_sides):
    value_centre, value_east, value_west, value_north, value_south = tracer
    speed_centre, speed_west = (zonal[0], zonal[2])
    flow_centre, flow_south = (meridional[0], meridional[4])
    wet_centre, wet_east, wet_west, wet_north, wet_south = wet_sides
    face_east = wet_centre * wet_east
    face_west = wet_west * wet_centre
    face_north = wet_centre * wet_north
    face_south = wet_south * wet_centre
    upwind_east = face_east * (
        jnp.maximum(speed_centre, 0.0) * value_centre + jnp.minimum(speed_centre, 0.0) * value_east
    )
    upwind_west = face_west * (
        jnp.maximum(speed_west, 0.0) * value_west + jnp.minimum(speed_west, 0.0) * value_centre
    )
    upwind_north = face_north * (
        jnp.maximum(flow_centre, 0.0) * value_centre + jnp.minimum(flow_centre, 0.0) * value_north
    )
    upwind_south = face_south * (
        jnp.maximum(flow_south, 0.0) * value_south + jnp.minimum(flow_south, 0.0) * value_centre
    )
    anti_east = face_east * speed_centre * (value_centre + value_east) * 0.5 - upwind_east
    anti_west = face_west * speed_west * (value_west + value_centre) * 0.5 - upwind_west
    anti_north = face_north * flow_centre * (value_centre + value_north) * 0.5 - upwind_north
    anti_south = face_south * flow_south * (value_south + value_centre) * 0.5 - upwind_south
    upwind = value_centre - wet_centre * (upwind_east - upwind_west + upwind_north - upwind_south)
    inflow = (
        jnp.maximum(anti_west, 0.0)
        - jnp.minimum(anti_east, 0.0)
        + jnp.maximum(anti_south, 0.0)
        - jnp.minimum(anti_north, 0.0)
    )
    outflow = (
        jnp.maximum(anti_east, 0.0)
        - jnp.minimum(anti_west, 0.0)
        + jnp.maximum(anti_north, 0.0)
        - jnp.minimum(anti_south, 0.0)
    )
    anti = (anti_east, anti_west, anti_north, anti_south)
    return (upwind, anti, inflow, outflow)


def ratios(upwind_sides, wet_sides, inflow, outflow):
    value_centre, value_east, value_west, value_north, value_south = upwind_sides
    _, wet_east, wet_west, wet_north, wet_south = wet_sides
    pairs = (
        (value_east, wet_east),
        (value_west, wet_west),
        (value_north, wet_north),
        (value_south, wet_south),
    )
    candidates = [value_centre] + [
        jnp.where(beside_wet > 0.5, beside, value_centre) for beside, beside_wet in pairs
    ]
    highest = reduce(jnp.maximum, candidates)
    lowest = reduce(jnp.minimum, candidates)
    ratio_plus = jnp.minimum(1.0, (highest - value_centre) / jnp.maximum(inflow, RATIO_FLOOR))
    ratio_minus = jnp.minimum(1.0, (value_centre - lowest) / jnp.maximum(outflow, RATIO_FLOOR))
    return jnp.concatenate([ratio_plus, ratio_minus], axis=0)


def limited(ratio_sides, upwind, anti, wet_centre):
    plus_centre, plus_east, plus_west, plus_north, plus_south = [side[:2] for side in ratio_sides]
    minus_centre, minus_east, minus_west, minus_north, minus_south = [
        side[2:] for side in ratio_sides
    ]
    anti_east, anti_west, anti_north, anti_south = anti
    coef_east = jnp.where(
        anti_east >= 0.0, jnp.minimum(plus_east, minus_centre), jnp.minimum(plus_centre, minus_east)
    )
    coef_west = jnp.where(
        anti_west >= 0.0, jnp.minimum(plus_centre, minus_west), jnp.minimum(plus_west, minus_centre)
    )
    coef_north = jnp.where(
        anti_north >= 0.0,
        jnp.minimum(plus_north, minus_centre),
        jnp.minimum(plus_centre, minus_north),
    )
    coef_south = jnp.where(
        anti_south >= 0.0,
        jnp.minimum(plus_centre, minus_south),
        jnp.minimum(plus_south, minus_centre),
    )
    return upwind - wet_centre * (
        coef_east * anti_east
        - coef_west * anti_west
        + coef_north * anti_north
        - coef_south * anti_south
    )


def vertical_of(tracer, wet):
    stacked_wet = wet[:-1] * wet[1:]
    vertical = (tracer[:, 1:] - tracer[:, :-1]) * stacked_wet
    return jnp.concatenate([vertical, jnp.zeros_like(tracer[:, :1])], axis=1)


def isopycnal(values, wet_sides):
    verticals = tuple((vertical_of(tracer, wet) for tracer, wet in zip(values, wet_sides)))
    densities = tuple((HALINE_COEF * tracer[1] - THERMAL_COEF * tracer[0] for tracer in values))
    stratas = tuple(
        (HALINE_COEF * vertical[1] - THERMAL_COEF * vertical[0] for vertical in verticals)
    )

    def face_flux(first, second):
        face = wet_sides[first] * wet_sides[second]
        slope = jnp.clip(
            (densities[second] - densities[first])
            / jnp.maximum(0.5 * (stratas[first] + stratas[second]), SLOPE_FLOOR),
            -SLOPE_LIMIT,
            SLOPE_LIMIT,
        )
        return (
            DIFFUSIVITY
            * face
            * (
                values[second]
                - values[first]
                - slope * 0.5 * (verticals[first] + verticals[second])
            )
        )

    east_flux = face_flux(0, 1)
    west_flux = face_flux(2, 0)
    north_flux = face_flux(0, 3)
    south_flux = face_flux(4, 0)
    return values[0] + wet_sides[0] * (east_flux - west_flux + north_flux - south_flux)


def advance(state, sides):
    state_sides = sides(state, sign_column(STATE_SIGNS), 0)
    tracer = tuple((side[:2] for side in state_sides))
    zonal = tuple((side[2] for side in state_sides))
    meridional = tuple((side[3] for side in state_sides))
    wet_sides = tuple((side[4] for side in state_sides))
    upwind, anti, inflow, outflow = low_order(tracer, zonal, meridional, wet_sides)
    upwind_sides = sides(upwind, sign_column((1.0, 1.0)), 1)
    ratio = ratios(upwind_sides, wet_sides, inflow, outflow)
    ratio_sides = sides(ratio, sign_column((1.0, 1.0, 1.0, 1.0)), 2)
    advected = limited(ratio_sides, upwind, anti, wet_sides[0])
    advected_sides = sides(advected, sign_column((1.0, 1.0)), 3)
    return isopycnal(advected_sides, wet_sides)


def local(
    heat_content_field,
    saltiness_field,
    eastward_cfl_number,
    northward_cfl_number,
    seawater_indicator,
    submerged_layer_total,
    seam_partner_index,
):
    span = heat_content_field.shape[2]
    anchor = lax.axis_index("lon") * span
    on_top = lax.axis_index("lat") == lax.axis_size("lat") - 1
    vertical_layer = jnp.arange(heat_content_field.shape[0], dtype=jnp.int32)[:, None, None]
    submerged_indicator = (
        (seawater_indicator[None] == 1) & (vertical_layer < submerged_layer_total[None])
    ).astype(jnp.float32)
    state = jnp.stack(
        [
            heat_content_field,
            saltiness_field,
            eastward_cfl_number,
            northward_cfl_number,
            submerged_indicator,
        ]
    )
    own_columns = anchor + jnp.arange(span, dtype=jnp.int32)
    facing = jnp.take(seam_partner_index, own_columns)

    def rim_sides(stack, fold_row):
        columns = jnp.concatenate([stack[..., :1], stack[..., -1:]], axis=3)
        column_rim = extended(columns, (("lon", 3),), 1, True)
        rows = jnp.concatenate([stack[:, :, :1, :], stack[:, :, -1:, :]], axis=2)
        row_rim = extended(rows, (("lat", 2),), 1, False)
        north_row = jnp.where(on_top, fold_row, row_rim[:, :, 3:4, :])
        return sided(
            stack, column_rim[..., 0:1], column_rim[..., 3:4], row_rim[:, :, 0:1, :], north_row
        )

    def device_sides(stack, signs, segment):
        top_row = lax.all_gather(stack[:, :, -1:, :], "lon", axis=3, tiled=True)
        fold_row = jnp.take(top_row, facing, axis=3) * signs
        return rim_sides(stack, fold_row)

    final = advance(state, device_sides)
    return (final[0], final[1])


def solution(mesh):
    in_specs = (
        P(None, "lat", "lon"),
        P(None, "lat", "lon"),
        P(None, "lat", "lon"),
        P(None, "lat", "lon"),
        P("lat", "lon"),
        P("lat", "lon"),
        P(),
    )
    out_specs = (P(None, "lat", "lon"), P(None, "lat", "lon"))
    return jax.shard_map(local, mesh=mesh, in_specs=in_specs, out_specs=out_specs, check_vma=False)
```

profile of v0, /device:TPU:97, one launch (start us, length us, event | category | flops | bytes accessed | tf_op | source)
XLA Modules:
  0.0 285.5 jit_solution(14750292049172549492)
XLA Ops:
  4.7 4.7 %collective-permute-start.2 = (f32[5,12,1,128]{3,2,1,0:T(1,128)}, f32[5,12,1,128]{3,2,1,0:T(1,128)}, u32[]{:S(2)}, u32[]{:S(2)}) collective-permute-start(f32[5,12,1,128]{3,2,1,0:T(1,128)} %get-tuple-element.45), channel_id=1, source_target_pairs={{1,0},{2,1},{3,2},{4,3},{5,4},{6,5},{7,6},{9,8},{10,9},{11,10},{12... | collective-permute-start | bytes 92168 | tf_op jit(solution)/shard_map/ppermute | solution.py:27
  9.3 2.7 collective-permute-start.3
  12.0 3.7 %fusion.105 = (f32[5,12,96,1]{3,2,1,0:T(8,128)}, f32[5,12,96,1]{3,2,1,0:T(8,128)}) fusion(f32[5,12,96,128]{3,2,1,0:T(8,128)S(1)} %convert_dynamic-update-slice_fusion), kind=kLoop, calls=%fused_computation.255 | loop fusion | bytes 92160 | tf_op jit(solution)/shard_map/slice | solution.py:223
  15.7 2.9 %copy.952 = f32[5,12,96,1]{2,3,1,0:T(1,128)} copy(f32[5,12,96,1]{3,2,1,0:T(8,128)} %get-tuple-element.41) | data formatting | bytes 46080 | tf_op jit(solution)/shard_map/slice | solution.py:223
  19.9 2.9 %copy.953 = f32[5,12,96,1]{2,3,1,0:T(1,128)} copy(f32[5,12,96,1]{3,2,1,0:T(8,128)} %get-tuple-element.42) | data formatting | bytes 46080 | tf_op jit(solution)/shard_map/slice | solution.py:223
  23.9 22.0 %all_gather.12 = f32[5,12,1,2048]{3,2,1,0:T(1,128)} all-gather(f32[5,12,1,128]{3,2,1,0:T(1,128)} %get-tuple-element.46), channel_id=1, replica_groups=mesh['lon'=16,'lat'=8] {'lon'}, dimensions={3}, use_global_device_ids=true | all-gather | bytes 522240 | tf_op jit(solution)/shard_map/all_gather | solution.py:233
  47.8 3.0 %fusion.106 = (f32[5,12,95,128]{3,2,1,0:T(8,128)}, f32[5,12,95,128]{3,2,1,0:T(8,128)}) fusion(f32[5,12,96,128]{3,2,1,0:T(8,128)S(1)} %convert_dynamic-update-slice_fusion), kind=kLoop, calls=%fused_computation.256 | loop fusion | bytes 11673600 | tf_op jit(solution)/shard_map/jit(_roll_static)/slice | solution.py:45
  50.8 3.6 %fusion.104 = (f32[5,12,96,127]{3,2,1,0:T(8,128)}, f32[5,12,96,127]{3,2,1,0:T(8,128)}) fusion(f32[5,12,96,128]{3,2,1,0:T(8,128)S(1)} %convert_dynamic-update-slice_fusion), kind=kLoop, calls=%fused_computation.254 | loop fusion | bytes 11704320 | tf_op jit(solution)/shard_map/jit(_roll_static)/slice | solution.py:43
  56.6 6.0 %copy.954 = f32[5,12,1,2048]{1,0,3,2:T(8,128)} copy(f32[5,12,1,2048]{3,2,1,0:T(1,128)} %all_gather.12) | data formatting | bytes 983040 | tf_op jit(solution)/shard_map/all_gather | solution.py:233
  62.6 4.9 %gather_fusion.1 = f32[128,5,12]{2,1,0:T(8,128)} fusion(f32[5,12,2048]{1,0,2:T(8,128)} %bitcast.128, s32[1024]{0:T(1024)} %pad_clamp_fusion.1), kind=kCustom, calls=%fused_computation.3 | custom fusion | bytes 61952 | tf_op jit(solution)/shard_map/jit(_take)/gather | solution.py:234
  70.2 3.2 %maximum_select_fusion = f32[5,12,96,128]{3,2,1,0:T(8,128)S(1)} fusion(f32[5,12,96,1]{3,2,1,0:T(8,128)S(1)} %copy-done.5, f32[5,12,96,127]{3,2,1,0:T(8,128)} %get-tuple-element.39, f32[5,12,96]{2,1,0:T(8,128)S(1)} %bitcast.143, pred[128]{0:T(512)(128)(4,1)S(1)} %get-tuple-element.98), kind=kLoop, calls=%fused_computation.19 | loop fusion | flops 1474560 | bytes 5921408 | tf_op jit(solution)/shard_map/jit(_where)/select_n | solution.py:43
  83.3 2.4 copy.1012
  103.3 5.8 %collective-permute-start.6 = (f32[2,12,1,128]{3,2,1,0:T(1,128)}, f32[2,12,1,128]{3,2,1,0:T(1,128)}, u32[]{:S(2)}, u32[]{:S(2)}) collective-permute-start(f32[2,12,1,128]{3,2,1,0:T(1,128)} %get-tuple-element.73), channel_id=1, source_target_pairs={{1,0},{2,1},{3,2},{4,3},{5,4},{6,5},{7,6},{9,8},{10,9},{11,10},{12... | collective-permute-start | bytes 36872 | tf_op jit(solution)/shard_map/ppermute | solution.py:27
  112.8 17.1 %all_gather.13 = f32[2,12,1,2048]{3,0,2,1:T(2,128)S(1)} all-gather(f32[2,12,1,128]{3,0,2,1:T(2,128)} %copy.960), channel_id=1, replica_groups=mesh['lon'=16,'lat'=8] {'lon'}, dimensions={3}, use_global_device_ids=true | all-gather | bytes 208896 | tf_op jit(solution)/shard_map/all_gather | solution.py:233
  129.9 2.3 copy.961
  132.3 2.5 gather_fusion.3
  137.2 10.3 %fusion.12 = (f32[2,12,96,128]{3,2,1,0:T(8,128)S(1)}, f32[2,12,96,128]{3,2,1,0:T(8,128)S(1)}, f32[2,12,96,128]{3,2,1,0:T(8,128)S(1)}, f32[2,12,96,128]{3,2,1,0:T(8,128)S(1)}, f32[2,12,96,128]{3,2,1,0:T(8,128)S(1)}) fusion(f32[2,12,96,128]{3,2,1,0:T(8,128)S(1)} %multiply_subtract_fusion.4, f32[2,12,1,128]{3,2,1,0:T(1,128)} %get-tuple-element.73, ...), kind=kLoop, calls=%fused_computation.41 | loop fusion | flops 17694720 | bytes 27765184 | tf_op jit(solution)/shard_map/min | solution.py:106
  147.6 4.2 %fusion.18 = f32[2,12,96,128]{3,2,1,0:T(8,128)S(1)} fusion(f32[2,12,96,128]{3,2,1,0:T(8,128)S(1)} %multiply_subtract_fusion.4, f32[2,12,1,128]{3,2,1,0:T(1,128)} %get-tuple-element.73, f32[2,12,95,128]{3,2,1,0:T(8,128)S(1)} %copy-done.35, f32[2,12,1,128]{3,2,1,0:T(1,128)} %get-tuple-element.72, f32[2,12,96,128]{3,2,1,0:T(8,128)S(1)} %get-tuple-element.22, ...), kind=kLoop, calls=%fused_computation.47 | loop fusion | flops 7962624 | bytes 12429760 | tf_op jit(solution)/shard_map/min | solution.py:107
  151.8 3.0 %fusion.1 = (f32[4,12,96,1]{3,2,1,0:T(8,128)}, f32[4,12,96,1]{3,2,1,0:T(8,128)}) fusion(f32[2,12,96,128]{3,2,1,0:T(8,128)S(1)} %get-tuple-element.18, f32[2,12,96,128]{3,2,1,0:T(8,128)S(1)} %fusion.18), kind=kLoop, calls=%fused_computation.24 | loop fusion | flops 9216 | bytes 2396160 | tf_op jit(solution)/shard_map/concatenate | solution.py:108
  154.8 3.0 %fusion.2 = (f32[4,12,96,127]{3,2,1,0:T(8,128)}, f32[4,12,96,127]{3,2,1,0:T(8,128)}) fusion(f32[2,12,96,128]{3,2,1,0:T(8,128)S(1)} %get-tuple-element.18, f32[2,12,96,128]{3,2,1,0:T(8,128)S(1)} %fusion.18), kind=kLoop, calls=%fused_computation.25 | loop fusion | flops 1170432 | bytes 7041024 | tf_op jit(solution)/shard_map/concatenate | solution.py:108
  163.4 3.0 %copy.968 = f32[4,12,96,1]{2,0,3,1:T(4,128)} copy(f32[4,12,96,1]{3,2,1,0:T(8,128)} %get-tuple-element.49) | data formatting | bytes 36864 | tf_op jit(solution)/shard_map/slice | solution.py:223
  166.6 3.0 %copy.970 = f32[4,12,96,1]{2,0,3,1:T(4,128)} copy(f32[4,12,96,1]{3,2,1,0:T(8,128)} %get-tuple-element.50) | data formatting | bytes 36864 | tf_op jit(solution)/shard_map/slice | solution.py:223
  171.1 19.1 %all_gather.14 = f32[4,12,1,2048]{3,0,2,1:T(4,128)} all-gather(f32[4,12,1,128]{3,0,2,1:T(4,128)} %copy.972), channel_id=1, replica_groups=mesh['lon'=16,'lat'=8] {'lon'}, dimensions={3}, use_global_device_ids=true | all-gather | bytes 417792 | tf_op jit(solution)/shard_map/all_gather | solution.py:233
  190.3 4.6 %copy.973 = f32[4,12,1,2048]{1,0,3,2:T(4,128)} copy(f32[4,12,1,2048]{3,0,2,1:T(4,128)} %all_gather.14) | data formatting | bytes 786432 | tf_op jit(solution)/shard_map/all_gather | solution.py:233
  194.8 3.8 %gather_fusion.2 = f32[128,4,12]{2,1,0:T(4,128)} fusion(f32[4,12,2048]{1,0,2:T(4,128)} %bitcast.133, s32[1024]{0:T(1024)} %pad_clamp_fusion.1), kind=kCustom, calls=%fused_computation.4 | custom fusion | bytes 49664 | tf_op jit(solution)/shard_map/jit(_take)/gather | solution.py:234
  200.3 6.1 %collective-permute-start.10 = (f32[4,12,1,128]{3,2,1,0:T(1,128)}, f32[4,12,1,128]{3,2,1,0:T(1,128)S(1)}, u32[]{:S(2)}, u32[]{:S(2)}) collective-permute-start(f32[4,12,1,128]{3,2,1,0:T(1,128)} %get-tuple-element.51), channel_id=1, source_target_pairs={{1,0},{2,1},{3,2},{4,3},{5,4},{6,5},{7,6},{9,8},{10,9},{11,10},{12... | collective-permute-start | bytes 73736 | tf_op jit(solution)/shard_map/ppermute | solution.py:27
  207.9 3.2 %maximum_select_fusion.4 = f32[4,12,96,128]{3,2,1,0:T(8,128)S(1)} fusion(f32[4,12,96,1]{3,2,1,0:T(8,128)} %get-tuple-element.49, f32[4,12,96,127]{3,2,1,0:T(8,128)} %get-tuple-element.47, f32[4,12,96]{2,1,0:T(8,128)S(1)} %copy.969, pred[128]{0:T(512)(128)(4,1)S(1)} %get-tuple-element.98), kind=kLoop, calls=%fused_computation.31 | loop fusion | flops 1179648 | bytes 4737152 | tf_op jit(solution)/shard_map/jit(_where)/select_n | solution.py:43
  233.7 18.5 %all_gather.15 = f32[2,12,1,2048]{3,0,2,1:T(2,128)} all-gather(f32[2,12,1,128]{3,0,2,1:T(2,128)} %copy.984), channel_id=1, replica_groups=mesh['lon'=16,'lat'=8] {'lon'}, dimensions={3}, use_global_device_ids=true | all-gather | bytes 208896 | tf_op jit(solution)/shard_map/all_gather | solution.py:233
  252.3 3.7 %copy.985 = f32[2,12,2048]{1,0,2:T(2,128)} copy(f32[2,12,2048]{2,0,1:T(2,128)} %bitcast.135) | data formatting | bytes 393216 | tf_op jit(solution)/shard_map/jit(_take)/Arg_0.21 | solution.py:234
  255.9 3.1 %gather_fusion.4 = f32[128,2,12]{2,1,0:T(2,128)} fusion(f32[2,12,2048]{1,0,2:T(2,128)} %copy.985, s32[1024]{0:T(1024)} %pad_clamp_fusion), kind=kCustom, calls=%fused_computation.1.clone | custom fusion | bytes 25088 | tf_op jit(solution)/shard_map/jit(_take)/gather | solution.py:234
  260.6 5.8 %collective-permute-start.14 = (f32[2,12,1,128]{3,2,1,0:T(1,128)}, f32[2,12,1,128]{3,2,1,0:T(1,128)S(1)}, u32[]{:S(2)}, u32[]{:S(2)}) collective-permute-start(f32[2,12,1,128]{3,2,1,0:T(1,128)} %get-tuple-element.64), channel_id=1, source_target_pairs={{1,0},{2,1},{3,2},{4,3},{5,4},{6,5},{7,6},{9,8},{10,9},{11,10},{12... | collective-permute-start | bytes 36872 | tf_op jit(solution)/shard_map/ppermute | solution.py:27
  280.6 3.8 %multiply_add_fusion = f32[2,12,96,128]{3,2,1,0:T(8,128)S(1)} fusion(f32[2,12,96,128]{3,2,1,0:T(8,128)S(1)} %fusion.23, f32[2,11,96,128]{3,2,1,0:T(8,128)S(1)} %fusion.35, f32[2,11,96,128]{3,2,1,0:T(8,128)S(1)} %fusion.36, f32[2,11,96,128]{3,2,1,0:T(8,128)S(1)} %fusion.37, f32[2,11,96,128]{3,2,1,0:T(8,128)S(1)} %fusion.38, ...), kind=kLoop, calls=%fused_computation.81 | loop fusion | flops 9732096 | bytes 17836480 | tf_op jit(solution)/shard_map/add | solution.py:176
  (301 shorter events, 95.6 us)
Async XLA Ops:
  0.6 45.4 %copy-start = (s32[2048]{0:T(1024)S(1)}, s32[2048]{0:T(1024)}, u32[]{:S(2)}) copy-start(s32[2048]{0:T(1024)} %param.19) | copy-start | bytes 24580
  4.7 74.9 %collective-permute-start.2 = (f32[5,12,1,128]{3,2,1,0:T(1,128)}, f32[5,12,1,128]{3,2,1,0:T(1,128)}, u32[]{:S(2)}, u32[]{:S(2)}) collective-permute-start(f32[5,12,1,128]{3,2,1,0:T(1,128)} %get-tuple-element.45), channel_id=1, source_target_pairs={{1,0},{2,1},{3,2},{4,3},{5,4},{6,5},{7,6},{9,8},{10,9},{11,10},{12... | collective-permute-start | bytes 92168 | tf_op jit(solution)/shard_map/ppermute | solution.py:27
  9.3 74.0 %collective-permute-start.3 = (f32[5,12,1,128]{3,2,1,0:T(1,128)}, f32[5,12,1,128]{3,2,1,0:T(1,128)}, u32[]{:S(2)}, u32[]{:S(2)}) collective-permute-start(f32[5,12,1,128]{3,2,1,0:T(1,128)} %get-tuple-element.46), channel_id=1, source_target_pairs={{0,1},{1,2},{2,3},{3,4},{4,5},{5,6},{6,7},{8,9},{9,10},{10,11},{11... | collective-permute-start | bytes 92168 | tf_op jit(solution)/shard_map/ppermute | solution.py:25
  18.6 50.8 %collective-permute-start = (f32[5,12,96,1]{2,3,1,0:T(1,128)}, f32[5,12,96,1]{2,3,1,0:T(1,128)}, u32[]{:S(2)}, u32[]{:S(2)}) collective-permute-start(f32[5,12,96,1]{2,3,1,0:T(1,128)} %copy.952), channel_id=1, source_target_pairs={{8,0},{16,8},{24,16},{32,24},{40,32},{48,40},{56,48},{64,56},{72,6... | collective-permute-start | bytes 69128 | tf_op jit(solution)/shard_map/ppermute | solution.py:27
  22.7 52.5 %collective-permute-start.1 = (f32[5,12,96,1]{2,3,1,0:T(1,128)}, f32[5,12,96,1]{2,3,1,0:T(1,128)}, u32[]{:S(2)}, u32[]{:S(2)}) collective-permute-start(f32[5,12,96,1]{2,3,1,0:T(1,128)} %copy.953), channel_id=1, source_target_pairs={{0,8},{8,16},{16,24},{24,32},{32,40},{40,48},{48,56},{56,64},{64,7... | collective-permute-start | bytes 69128 | tf_op jit(solution)/shard_map/ppermute | solution.py:25
  54.5 35.1 %copy-start.11 = (f32[12,96,128]{2,1,0:T(8,128)}, f32[12,96,128]{2,1,0:T(8,128)S(1)}, u32[]{:S(2)}) copy-start(f32[12,96,128]{2,1,0:T(8,128)S(1)} %fusion.83) | copy-start | bytes 1769476
  56.6 211.3 %copy-start.83 = (pred[128]{0:T(512)(128)(4,1)}, pred[128]{0:T(512)(128)(4,1)S(1)}, u32[]{:S(2)}) copy-start(pred[128]{0:T(512)(128)(4,1)S(1)} %get-tuple-element.98) | copy-start | bytes 388
  56.6 213.4 %copy-start.81 = (pred[128]{0:T(512)(128)(4,1)}, pred[128]{0:T(512)(128)(4,1)S(1)}, u32[]{:S(2)}) copy-start(pred[128]{0:T(512)(128)(4,1)S(1)} %get-tuple-element.97) | copy-start | bytes 388
  56.6 13.5 %copy-start.5 = (f32[5,12,96,1]{3,2,1,0:T(8,128)S(1)}, f32[5,12,96,1]{3,2,1,0:T(8,128)}, u32[]{:S(2)}) copy-start(f32[5,12,96,1]{3,2,1,0:T(8,128)} %get-tuple-element.41) | copy-start | bytes 69124
  73.4 16.2 %copy-start.8 = (f32[5,12,96,128]{3,2,1,0:T(8,128)}, f32[5,12,96,128]{3,2,1,0:T(8,128)S(1)}, u32[]{:S(2)}) copy-start(f32[5,12,96,128]{3,2,1,0:T(8,128)S(1)} %maximum_select_fusion) | copy-start | bytes 8847364
  77.7 11.9 %copy-start.9 = (f32[5,12,96,128]{3,2,1,0:T(8,128)}, f32[5,12,96,128]{3,2,1,0:T(8,128)S(1)}, u32[]{:S(2)}) copy-start(f32[5,12,96,128]{3,2,1,0:T(8,128)S(1)} %maximum_select_fusion.1) | copy-start | bytes 8847364
  81.9 19.7 %copy-start.6 = (f32[5,12,96,128]{3,2,1,0:T(8,128)}, f32[5,12,96,128]{3,2,1,0:T(8,128)S(1)}, u32[]{:S(2)}) copy-start(f32[5,12,96,128]{3,2,1,0:T(8,128)S(1)} %maximum_select_fusion.2) | copy-start | bytes 8847364
  87.4 15.1 %copy-start.7 = (f32[5,12,96,128]{3,2,1,0:T(8,128)}, f32[5,12,96,128]{3,2,1,0:T(8,128)S(1)}, u32[]{:S(2)}) copy-start(f32[5,12,96,128]{3,2,1,0:T(8,128)S(1)} %maximum_select_fusion.3) | copy-start | bytes 8847364
  92.8 18.0 %copy-start.15 = (f32[2,12,96,1]{3,2,1,0:T(8,128)}, f32[2,12,96,1]{3,2,1,0:T(8,128)S(1)}, u32[]{:S(2)}) copy-start(f32[2,12,96,1]{3,2,1,0:T(8,128)S(1)} %get-tuple-element.69) | copy-start | bytes 27652
  92.8 44.3 %copy-start.14 = (f32[2,12,96,1]{3,2,1,0:T(8,128)}, f32[2,12,96,1]{3,2,1,0:T(8,128)S(1)}, u32[]{:S(2)}) copy-start(f32[2,12,96,1]{3,2,1,0:T(8,128)S(1)} %get-tuple-element.68) | copy-start | bytes 27652
  98.0 38.3 %collective-permute-start.7 = (f32[2,12,1,128]{3,2,1,0:T(1,128)}, f32[2,12,1,128]{3,2,1,0:T(1,128)}, u32[]{:S(2)}, u32[]{:S(2)}) collective-permute-start(f32[2,12,1,128]{3,2,1,0:T(1,128)} %get-tuple-element.72), channel_id=1, source_target_pairs={{0,1},{1,2},{2,3},{3,4},{4,5},{5,6},{6,7},{8,9},{9,10},{10,11},{11... | collective-permute-start | bytes 36872 | tf_op jit(solution)/shard_map/ppermute | solution.py:25
  103.3 32.2 %collective-permute-start.6 = (f32[2,12,1,128]{3,2,1,0:T(1,128)}, f32[2,12,1,128]{3,2,1,0:T(1,128)}, u32[]{:S(2)}, u32[]{:S(2)}) collective-permute-start(f32[2,12,1,128]{3,2,1,0:T(1,128)} %get-tuple-element.73), channel_id=1, source_target_pairs={{1,0},{2,1},{3,2},{4,3},{5,4},{6,5},{7,6},{9,8},{10,9},{11,10},{12... | collective-permute-start | bytes 36872 | tf_op jit(solution)/shard_map/ppermute | solution.py:27
  110.1 24.7 %collective-permute-start.4 = (f32[2,12,96,1]{2,0,3,1:T(2,128)}, f32[2,12,96,1]{2,0,3,1:T(2,128)}, u32[]{:S(2)}, u32[]{:S(2)}) collective-permute-start(f32[2,12,96,1]{2,0,3,1:T(2,128)} %copy.956), channel_id=1, source_target_pairs={{8,0},{16,8},{24,16},{32,24},{40,32},{48,40},{56,48},{64,56},{72,6... | collective-permute-start | bytes 27656 | tf_op jit(solution)/shard_map/ppermute | solution.py:27
  111.8 23.8 %collective-permute-start.5 = (f32[2,12,96,1]{2,0,3,1:T(2,128)}, f32[2,12,96,1]{2,0,3,1:T(2,128)S(1)}, u32[]{:S(2)}, u32[]{:S(2)}) collective-permute-start(f32[2,12,96,1]{2,0,3,1:T(2,128)} %copy.958), channel_id=1, source_target_pairs={{0,8},{8,16},{16,24},{24,32},{32,40},{40,48},{48,56},{56,64},{64,7... | collective-permute-start | bytes 27656 | tf_op jit(solution)/shard_map/ppermute | solution.py:25
  137.1 10.5 %copy-start.16 = (f32[2,12,96,1]{3,2,1,0:T(8,128)S(1)}, f32[2,12,96,1]{3,2,1,0:T(8,128)}, u32[]{:S(2)}) copy-start(f32[2,12,96,1]{3,2,1,0:T(8,128)} %copy-done.15) | copy-start | bytes 27652
  137.1 10.5 %copy-start.32 = (f32[2,12,96,127]{3,2,1,0:T(8,128)S(1)}, f32[2,12,96,127]{3,2,1,0:T(8,128)}, u32[]{:S(2)}) copy-start(f32[2,12,96,127]{3,2,1,0:T(8,128)} %get-tuple-element.66) | copy-start | bytes 3511300
  137.1 10.5 %copy-start.33 = (f32[2,12,96,127]{3,2,1,0:T(8,128)S(1)}, f32[2,12,96,127]{3,2,1,0:T(8,128)}, u32[]{:S(2)}) copy-start(f32[2,12,96,127]{3,2,1,0:T(8,128)} %get-tuple-element.67) | copy-start | bytes 3511300
  137.1 10.5 %copy-start.34 = (f32[2,12,95,128]{3,2,1,0:T(8,128)S(1)}, f32[2,12,95,128]{3,2,1,0:T(8,128)}, u32[]{:S(2)}) copy-start(f32[2,12,95,128]{3,2,1,0:T(8,128)} %get-tuple-element.70) | copy-start | bytes 3502084
  151.8 62.1 %copy-start.2 = (f32[2,12,96,128]{3,2,1,0:T(8,128)}, f32[2,12,96,128]{3,2,1,0:T(8,128)S(1)}, u32[]{:S(2)}) copy-start(f32[2,12,96,128]{3,2,1,0:T(8,128)S(1)} %fusion.18) | copy-start | bytes 3538948
  161.5 51.7 %collective-permute-start.11 = (f32[4,12,1,128]{3,2,1,0:T(1,128)}, f32[4,12,1,128]{3,2,1,0:T(1,128)}, u32[]{:S(2)}, u32[]{:S(2)}) collective-permute-start(f32[4,12,1,128]{3,2,1,0:T(1,128)} %get-tuple-element.52), channel_id=1, source_target_pairs={{0,1},{1,2},{2,3},{3,4},{4,5},{5,6},{6,7},{8,9},{9,10},{10,11},{11... | collective-permute-start | bytes 73736 | tf_op jit(solution)/shard_map/ppermute | solution.py:25
  166.4 40.0 %collective-permute-start.8 = (f32[4,12,96,1]{2,0,3,1:T(4,128)}, f32[4,12,96,1]{2,0,3,1:T(4,128)}, u32[]{:S(2)}, u32[]{:S(2)}) collective-permute-start(f32[4,12,96,1]{2,0,3,1:T(4,128)} %copy.968), channel_id=1, source_target_pairs={{8,0},{16,8},{24,16},{32,24},{40,32},{48,40},{56,48},{64,56},{72,6... | collective-permute-start | bytes 55304 | tf_op jit(solution)/shard_map/ppermute | solution.py:27
  169.6 37.6 %collective-permute-start.9 = (f32[4,12,96,1]{2,0,3,1:T(4,128)}, f32[4,12,96,1]{2,0,3,1:T(4,128)}, u32[]{:S(2)}, u32[]{:S(2)}) collective-permute-start(f32[4,12,96,1]{2,0,3,1:T(4,128)} %copy.970), channel_id=1, source_target_pairs={{0,8},{8,16},{16,24},{24,32},{32,40},{40,48},{48,56},{56,64},{64,7... | collective-permute-start | bytes 55304 | tf_op jit(solution)/shard_map/ppermute | solution.py:25
  200.3 12.8 %collective-permute-start.10 = (f32[4,12,1,128]{3,2,1,0:T(1,128)}, f32[4,12,1,128]{3,2,1,0:T(1,128)S(1)}, u32[]{:S(2)}, u32[]{:S(2)}) collective-permute-start(f32[4,12,1,128]{3,2,1,0:T(1,128)} %get-tuple-element.51), channel_id=1, source_target_pairs={{1,0},{2,1},{3,2},{4,3},{5,4},{6,5},{7,6},{9,8},{10,9},{11,10},{12... | collective-permute-start | bytes 73736 | tf_op jit(solution)/shard_map/ppermute | solution.py:27
  225.9 48.3 %collective-permute-start.15 = (f32[2,12,1,128]{3,2,1,0:T(1,128)}, f32[2,12,1,128]{3,2,1,0:T(1,128)}, u32[]{:S(2)}, u32[]{:S(2)}) collective-permute-start(f32[2,12,1,128]{3,2,1,0:T(1,128)} %get-tuple-element.65), channel_id=1, source_target_pairs={{0,1},{1,2},{2,3},{3,4},{4,5},{5,6},{6,7},{8,9},{9,10},{10,11},{11... | collective-permute-start | bytes 36872 | tf_op jit(solution)/shard_map/ppermute | solution.py:25
  228.8 37.6 %collective-permute-start.12 = (f32[2,12,96,1]{2,0,3,1:T(2,128)}, f32[2,12,96,1]{2,0,3,1:T(2,128)}, u32[]{:S(2)}, u32[]{:S(2)}) collective-permute-start(f32[2,12,96,1]{2,0,3,1:T(2,128)} %copy.980), channel_id=1, source_target_pairs={{8,0},{16,8},{24,16},{32,24},{40,32},{48,40},{56,48},{64,56},{72,6... | collective-permute-start | bytes 27656 | tf_op jit(solution)/shard_map/ppermute | solution.py:27
  232.4 34.7 %collective-permute-start.13 = (f32[2,12,96,1]{2,0,3,1:T(2,128)}, f32[2,12,96,1]{2,0,3,1:T(2,128)}, u32[]{:S(2)}, u32[]{:S(2)}) collective-permute-start(f32[2,12,96,1]{2,0,3,1:T(2,128)} %copy.982), channel_id=1, source_target_pairs={{0,8},{8,16},{16,24},{24,32},{32,40},{40,48},{48,56},{56,64},{64,7... | collective-permute-start | bytes 27656 | tf_op jit(solution)/shard_map/ppermute | solution.py:25
  260.6 13.4 %collective-permute-start.14 = (f32[2,12,1,128]{3,2,1,0:T(1,128)}, f32[2,12,1,128]{3,2,1,0:T(1,128)S(1)}, u32[]{:S(2)}, u32[]{:S(2)}) collective-permute-start(f32[2,12,1,128]{3,2,1,0:T(1,128)} %get-tuple-element.64), channel_id=1, source_target_pairs={{1,0},{2,1},{3,2},{4,3},{5,4},{6,5},{7,6},{9,8},{10,9},{11,10},{12... | collective-permute-start | bytes 36872 | tf_op jit(solution)/shard_map/ppermute | solution.py:27
  (74 other events, 223.3 us)
where the time goes:
time: 288 us; the launch traced here: 286 us
  local copies, waits for them, and re-layouts  99.8 us (35%)
  blocking collectives  76.8 us (27%)
  other arithmetic  68.2 us (24%)
  starting transfers between devices  38.6 us (13%)
    all_gather x4, blocking collectives, device_sides(): top_row = lax.all_gather(stack[:, :, -1:, :], 'lon', axis=3, tiled=True)  76.8 us
    ppermute x8, starting transfers between devices, extended(): lax.ppermute(head, axis, [((i + 1) % count, i) for i in range(ends)])  24.9 us
    slice x11, local copies, waits for them, and re-layouts, rim_sides(): columns = jnp.concatenate([stack[..., :1], stack[..., -1:]], axis=3)  20.1 us
    gather x8, local copies, waits for them, and re-layouts, device_sides(): fold_row = jnp.take(top_row, facing, axis=3) * signs  19.4 us
    unnamed x188, local copies, waits for them, and re-layouts  15.6 us
    ppermute x8, starting transfers between devices, extended(): lax.ppermute(tail, axis, [(i, (i + 1) % count) for i in range(ends)])  13.7 us
    all_gather x3, local copies, waits for them, and re-layouts, device_sides(): top_row = lax.all_gather(stack[:, :, -1:, :], 'lon', axis=3, tiled=True)  12.9 us
    min x1, other arithmetic, ratios(): jnp.minimum(1.0, (highest - value_centre) / jnp.maximum(inflow, RATIO_FLO...  10.3 us
  transfers between devices with their start and end apart: 16, of which 0 were waited for; matrix products, arithmetic and copies ran while one was open for 34% of the time, Pallas kernels for 0%

commit v1 on v0

v1 whole, which is shorter than its diff:
```python
import functools

import jax
import jax.numpy as jnp
from jax import lax
from jax.experimental import pallas as pl
from jax.experimental.pallas import tpu as pltpu
from jax.sharding import PartitionSpec as P

RATIO_FLOOR = 0.05
SLOPE_FLOOR = 0.5
SLOPE_LIMIT = 2.0
DIFFUSIVITY = 0.1
THERMAL_COEF = 0.2
HALINE_COEF = 0.8
STATE_SIGNS = (1.0, 1.0, -1.0, -1.0, 1.0)


def sign_column(values):
    return jnp.array(values, jnp.float32).reshape(len(values), 1, 1, 1)


def around(x, west, east, south, north):
    height, width = x.shape
    lane = lax.broadcasted_iota(jnp.int32, x.shape, 1)
    level = lax.broadcasted_iota(jnp.int32, x.shape, 0)
    at_east = jnp.where(lane == width - 1, east, pltpu.roll(x, width - 1, 1))
    at_west = jnp.where(lane == 0, west, pltpu.roll(x, 1, 1))
    at_north = jnp.where(level == height - 1, north, pltpu.roll(x, height - 1, 0))
    at_south = jnp.where(level == 0, south, pltpu.roll(x, 1, 0))
    return (x, at_east, at_west, at_north, at_south)


def sides_of(refs, f, k):
    block, west, east, south, north = refs
    return around(block[f, k], west[f, k], east[f, k], south[f, k], north[f, k])


def low_order(tracer, zonal, meridional, wet_sides):
    value_centre, value_east, value_west, value_north, value_south = tracer
    speed_centre, speed_west = (zonal[0], zonal[2])
    flow_centre, flow_south = (meridional[0], meridional[4])
    wet_centre, wet_east, wet_west, wet_north, wet_south = wet_sides
    face_east = wet_centre * wet_east
    face_west = wet_west * wet_centre
    face_north = wet_centre * wet_north
    face_south = wet_south * wet_centre
    upwind_east = face_east * (
        jnp.maximum(speed_centre, 0.0) * value_centre + jnp.minimum(speed_centre, 0.0) * value_east
    )
    upwind_west = face_west * (
        jnp.maximum(speed_west, 0.0) * value_west + jnp.minimum(speed_west, 0.0) * value_centre
    )
    upwind_north = face_north * (
        jnp.maximum(flow_centre, 0.0) * value_centre + jnp.minimum(flow_centre, 0.0) * value_north
    )
    upwind_south = face_south * (
        jnp.maximum(flow_south, 0.0) * value_south + jnp.minimum(flow_south, 0.0) * value_centre
    )
    anti_east = face_east * speed_centre * (value_centre + value_east) * 0.5 - upwind_east
    anti_west = face_west * speed_west * (value_west + value_centre) * 0.5 - upwind_west
    anti_north = face_north * flow_centre * (value_centre + value_north) * 0.5 - upwind_north
    anti_south = face_south * flow_south * (value_south + value_centre) * 0.5 - upwind_south
    upwind = value_centre - wet_centre * (upwind_east - upwind_west + upwind_north - upwind_south)
    inflow = (
        jnp.maximum(anti_west, 0.0)
        - jnp.minimum(anti_east, 0.0)
        + jnp.maximum(anti_south, 0.0)
        - jnp.minimum(anti_north, 0.0)
    )
    outflow = (
        jnp.maximum(anti_east, 0.0)
        - jnp.minimum(anti_west, 0.0)
        + jnp.maximum(anti_north, 0.0)
        - jnp.minimum(anti_south, 0.0)
    )
    anti = (anti_east, anti_west, anti_north, anti_south)
    return (upwind, anti, inflow, outflow)


def level_low_order(state_refs, k, tracer):
    zonal = sides_of(state_refs, 2, k)
    meridional = sides_of(state_refs, 3, k)
    wet_sides = sides_of(state_refs, 4, k)
    return low_order(sides_of(state_refs, tracer, k), zonal, meridional, wet_sides), wet_sides


def ratio_pair(upwind_sides, wet_sides, inflow, outflow):
    value_centre = upwind_sides[0]
    candidates = [value_centre] + [
        jnp.where(beside_wet > 0.5, beside, value_centre)
        for beside, beside_wet in zip(upwind_sides[1:], wet_sides[1:])
    ]
    highest = functools.reduce(jnp.maximum, candidates)
    lowest = functools.reduce(jnp.minimum, candidates)
    ratio_plus = jnp.minimum(1.0, (highest - value_centre) / jnp.maximum(inflow, RATIO_FLOOR))
    ratio_minus = jnp.minimum(1.0, (value_centre - lowest) / jnp.maximum(outflow, RATIO_FLOOR))
    return ratio_plus, ratio_minus


def limited(plus, minus, upwind, anti, wet_centre):
    plus_centre, plus_east, plus_west, plus_north, plus_south = plus
    minus_centre, minus_east, minus_west, minus_north, minus_south = minus
    anti_east, anti_west, anti_north, anti_south = anti
    coef_east = jnp.where(
        anti_east >= 0.0, jnp.minimum(plus_east, minus_centre), jnp.minimum(plus_centre, minus_east)
    )
    coef_west = jnp.where(
        anti_west >= 0.0, jnp.minimum(plus_centre, minus_west), jnp.minimum(plus_west, minus_centre)
    )
    coef_north = jnp.where(
        anti_north >= 0.0,
        jnp.minimum(plus_north, minus_centre),
        jnp.minimum(plus_centre, minus_north),
    )
    coef_south = jnp.where(
        anti_south >= 0.0,
        jnp.minimum(plus_centre, minus_south),
        jnp.minimum(plus_south, minus_centre),
    )
    return upwind - wet_centre * (
        coef_east * anti_east
        - coef_west * anti_west
        + coef_north * anti_north
        - coef_south * anti_south
    )


def upwind_kernel(*refs):
    state_refs, out = refs[:5], refs[5]
    levels = out.shape[1]

    def body(k, carry):
        for tracer in range(2):
            (upwind, _, _, _), _ = level_low_order(state_refs, k, tracer)
            out[tracer, k] = upwind
        return carry

    lax.fori_loop(0, levels, body, 0)


def ratio_kernel(*refs):
    state_refs, upwind_refs, out = refs[:5], refs[5:10], refs[10]
    levels = out.shape[1]

    def body(k, carry):
        for tracer in range(2):
            (_, _, inflow, outflow), wet_sides = level_low_order(state_refs, k, tracer)
            plus, minus = ratio_pair(sides_of(upwind_refs, tracer, k), wet_sides, inflow, outflow)
            out[tracer, k] = plus
            out[2 + tracer, k] = minus
        return carry

    lax.fori_loop(0, levels, body, 0)


def advected_kernel(*refs):
    state_refs, upwind_ref, ratio_refs, out = refs[:5], refs[5], refs[6:11], refs[11]
    levels = out.shape[1]

    def body(k, carry):
        for tracer in range(2):
            (_, anti, _, _), wet_sides = level_low_order(state_refs, k, tracer)
            plus = sides_of(ratio_refs, tracer, k)
            minus = sides_of(ratio_refs, 2 + tracer, k)
            out[tracer, k] = limited(plus, minus, upwind_ref[tracer, k], anti, wet_sides[0])
        return carry

    lax.fori_loop(0, levels, body, 0)


def isopycnal_kernel(*refs):
    advected_refs, state_refs, out = refs[:5], refs[5:10], refs[10]
    levels = out.shape[1]

    def body(k, carry):
        above = jnp.minimum(k + 1, levels - 1)
        values = [sides_of(advected_refs, tracer, k) for tracer in range(2)]
        uppers = [sides_of(advected_refs, tracer, above) for tracer in range(2)]
        wet_sides = sides_of(state_refs, 4, k)
        wet_above = sides_of(state_refs, 4, above)
        stacked = [w * a for w, a in zip(wet_sides, wet_above)]
        verticals = [
            [(u - v) * s for u, v, s in zip(uppers[tracer], values[tracer], stacked)]
            for tracer in range(2)
        ]
        densities = [HALINE_COEF * s - THERMAL_COEF * t for t, s in zip(values[0], values[1])]
        stratas = [HALINE_COEF * s - THERMAL_COEF * t for t, s in zip(verticals[0], verticals[1])]
        for tracer in range(2):
            value, vertical = values[tracer], verticals[tracer]

            def face_flux(first, second):
                face = wet_sides[first] * wet_sides[second]
                slope = jnp.clip(
                    (densities[second] - densities[first])
                    / jnp.maximum(0.5 * (stratas[first] + stratas[second]), SLOPE_FLOOR),
                    -SLOPE_LIMIT,
                    SLOPE_LIMIT,
                )
                return (
                    DIFFUSIVITY
                    * face
                    * (
                        value[second]
                        - value[first]
                        - slope * 0.5 * (vertical[first] + vertical[second])
                    )
                )

            east_flux = face_flux(0, 1)
            west_flux = face_flux(2, 0)
            north_flux = face_flux(0, 3)
            south_flux = face_flux(4, 0)
            out[tracer, k] = value[0] + wet_sides[0] * (
                east_flux - west_flux + north_flux - south_flux
            )
        return carry

    lax.fori_loop(0, levels, body, 0)


def stage(kernel, fields, *args):
    shape = args[0].shape
    return pl.pallas_call(
        kernel,
        out_shape=jax.ShapeDtypeStruct((fields,) + shape[1:], jnp.float32),
        in_specs=[pl.BlockSpec(memory_space=pltpu.VMEM)] * len(args),
        out_specs=pl.BlockSpec(memory_space=pltpu.VMEM),
    )(*args)


def local(
    heat_content_field,
    saltiness_field,
    eastward_cfl_number,
    northward_cfl_number,
    seawater_indicator,
    submerged_layer_total,
    seam_partner_index,
):
    span = heat_content_field.shape[2]
    anchor = lax.axis_index("lon") * span
    on_top = lax.axis_index("lat") == lax.axis_size("lat") - 1
    vertical_layer = jnp.arange(heat_content_field.shape[0], dtype=jnp.int32)[:, None, None]
    submerged_indicator = (
        (seawater_indicator[None] == 1) & (vertical_layer < submerged_layer_total[None])
    ).astype(jnp.float32)
    state = jnp.stack(
        [
            heat_content_field,
            saltiness_field,
            eastward_cfl_number,
            northward_cfl_number,
            submerged_indicator,
        ]
    )
    facing = jnp.take(seam_partner_index, anchor + jnp.arange(span, dtype=jnp.int32))

    def halos(stack, signs):
        lon = lax.axis_size("lon")
        lat = lax.axis_size("lat")
        west = lax.ppermute(stack[..., -1:], "lon", [(i, (i + 1) % lon) for i in range(lon)])
        east = lax.ppermute(stack[..., :1], "lon", [((i + 1) % lon, i) for i in range(lon)])
        south = lax.ppermute(stack[:, :, -1:, :], "lat", [(i, i + 1) for i in range(lat - 1)])
        north = lax.ppermute(stack[:, :, :1, :], "lat", [(i + 1, i) for i in range(lat - 1)])
        top_row = lax.all_gather(stack[:, :, -1:, :], "lon", axis=3, tiled=True)
        fold_row = jnp.take(top_row, facing, axis=3) * signs
        return (stack, west, east, south, jnp.where(on_top, fold_row, north))

    state_refs = halos(state, sign_column(STATE_SIGNS))
    upwind = stage(upwind_kernel, 2, *state_refs)
    upwind_refs = halos(upwind, sign_column((1.0, 1.0)))
    ratio = stage(ratio_kernel, 4, *state_refs, *upwind_refs)
    ratio_refs = halos(ratio, sign_column((1.0,) * 4))
    advected = stage(advected_kernel, 2, *state_refs, upwind, *ratio_refs)
    advected_refs = halos(advected, sign_column((1.0, 1.0)))
    final = stage(isopycnal_kernel, 2, *advected_refs, *state_refs)
    return (final[0], final[1])


def solution(mesh):
    in_specs = (
        P(None, "lat", "lon"),
        P(None, "lat", "lon"),
        P(None, "lat", "lon"),
        P(None, "lat", "lon"),
        P("lat", "lon"),
        P("lat", "lon"),
        P(),
    )
    out_specs = (P(None, "lat", "lon"), P(None, "lat", "lon"))
    return jax.shard_map(local, mesh=mesh, in_specs=in_specs, out_specs=out_specs, check_vma=False)
```

time: 288 us -> 236 us (0.82)
  the two profiles are of different devices: /device:TPU:97 before, /device:TPU:25 now
where the time goes in v1:
time: 236 us; the launch traced here: 235 us
  blocking collectives  82.7 us (35%)
  local copies, waits for them, and re-layouts  64.3 us (27%)
  Pallas kernels  48 us (20%)
  starting transfers between devices  35.9 us (15%)
  other arithmetic  3.6 us (2%)
    all_gather x4, blocking collectives, halos(): top_row = lax.all_gather(stack[:, :, -1:, :], 'lon', axis=3, tiled=True)  82.7 us
    pallas_call x4, Pallas kernels, stage(): pl.pallas_call(kernel, out_shape=jax.ShapeDtypeStruct((fields,) + shape[1...  48 us
    ppermute x4, starting transfers between devices, halos(): lax.ppermute(stack[:, :, -1:, :], 'lat', [(i, i + 1) for i in range(lat -...  22.1 us
    slice x8, local copies, waits for them, and re-layouts, halos(): stack[..., :1]  15.7 us
    gather x8, local copies, waits for them, and re-layouts, halos(): fold_row = jnp.take(top_row, facing, axis=3) * signs  8.91 us
    ppermute x4, starting transfers between devices, halos(): lax.ppermute(stack[:, :, :1, :], 'lat', [(i + 1, i) for i in range(lat -...  8.61 us
    all_gather x2, local copies, waits for them, and re-layouts, halos(): top_row = lax.all_gather(stack[:, :, -1:, :], 'lon', axis=3, tiled=True)  7.95 us
    ppermute x4, local copies, waits for them, and re-layouts, halos(): lax.ppermute(stack[..., :1], 'lon', [((i + 1) % lon, i) for i in range(lo...  7.33 us
  transfers between devices with their start and end apart: 16, of which 0 were waited for; matrix products, arithmetic and copies ran while one was open for 20% of the time, Pallas kernels for 0%

profile of v1, /device:TPU:25, one launch (start us, length us, event | category | flops | bytes accessed | tf_op | source)
XLA Modules:
  0.0 235.5 jit_solution(17964200510001804010)
XLA Ops:
  4.1 2.9 %collective-permute-start.3 = (f32[5,12,1,128]{3,2,1,0:T(1,128)S(1)}, f32[5,12,1,128]{3,2,1,0:T(1,128)S(1)}, u32[]{:S(2)}, u32[]{:S(2)}) collective-permute-start(f32[5,12,1,128]{3,2,1,0:T(1,128)S(1)} %get-tuple-element.5), channel_id=1, source_target_pairs={{1,0},{2,1},{3,2},{4,3},{5,4},{6,5},{7,6},{9,8},{10,9},{11,10},{12... | collective-permute-start | bytes 92168 | tf_op jit(solution)/shard_map/ppermute | solution.py:265
  7.0 4.8 %collective-permute-start.2 = (f32[5,12,1,128]{3,2,1,0:T(1,128)S(1)}, f32[5,12,1,128]{3,2,1,0:T(1,128)S(1)}, u32[]{:S(2)}, u32[]{:S(2)}) collective-permute-start(f32[5,12,1,128]{3,2,1,0:T(1,128)S(1)} %get-tuple-element.6), channel_id=1, source_target_pairs={{0,1},{1,2},{2,3},{3,4},{4,5},{5,6},{6,7},{8,9},{9,10},{10,11},{11... | collective-permute-start | bytes 92168 | tf_op jit(solution)/shard_map/ppermute | solution.py:264
  11.8 2.7 %fusion.5 = (f32[5,12,96,1]{3,2,1,0:T(8,128)S(1)}, f32[5,12,96,1]{3,2,1,0:T(8,128)}) fusion(f32[5,12,96,128]{3,2,1,0:T(8,128)S(1)} %convert_dynamic-update-slice_fusion.refs_0_.refs_5_), kind=kLoop, calls=%fused_computation.37 | loop fusion | bytes 92160 | tf_op jit(solution)/shard_map/slice | solution.py:263
  14.5 2.3 copy.28
  16.8 2.6 %collective-permute-start = (f32[5,12,96,1]{2,3,1,0:T(1,128)S(1)}, f32[5,12,96,1]{2,3,1,0:T(1,128)S(1)}, u32[]{:S(2)}, u32[]{:S(2)}) collective-permute-start(f32[5,12,96,1]{2,3,1,0:T(1,128)S(1)} %copy.28), channel_id=1, source_target_pairs={{0,8},{8,16},{16,24},{24,32},{32,40},{40,48},{48,56},{56,64},{64,7... | collective-permute-start | bytes 69128 | tf_op jit(solution)/shard_map/ppermute | solution.py:262
  21.8 20.4 %all_gather.12 = f32[5,12,1,2048]{3,2,1,0:T(1,128)S(1)} all-gather(f32[5,12,1,128]{3,2,1,0:T(1,128)S(1)} %get-tuple-element.6), channel_id=1, replica_groups=mesh['lon'=16,'lat'=8] {'lon'}, dimensions={3}, use_global_device_ids=true | all-gather | bytes 522240 | tf_op jit(solution)/shard_map/all_gather | solution.py:266
  42.2 4.8 %copy.64 = f32[5,12,1,2048]{1,0,3,2:T(8,128)} copy(f32[5,12,1,2048]{3,2,1,0:T(1,128)S(1)} %all_gather.12) | data formatting | bytes 983040 | tf_op jit(solution)/shard_map/all_gather | solution.py:266
  47.0 4.0 %gather_fusion.1 = f32[128,5,12]{2,1,0:T(8,128)S(1)} fusion(f32[5,12,2048]{1,0,2:T(8,128)} %bitcast.37, s32[1024]{0:T(1024)S(1)} %pad_clamp_fusion.1), kind=kCustom, calls=%fused_computation.3 | custom fusion | bytes 61952 | tf_op jit(solution)/shard_map/jit(_take)/gather | solution.py:267
  51.2 2.2 copy.51.refs_2_.refs_7_
  53.4 2.1 copy.50.refs_1_.refs_6_
  56.9 8.9 %shard_map.122.refs_5_ = f32[2,12,96,128]{3,2,1,0:T(8,128)} custom-call(f32[5,12,96,128]{3,2,1,0:T(8,128)} %copy-done.1, f32[5,12,96,1]{3,2,1,0:T(8,128)} %copy.50.refs_1_.refs_6_, f32[5,12,96,1]{3,2,1,0:T(8,128)} %copy.51.refs_2_.refs_7_, f32[5,12,1,128]{3,2,1,0:T(1,128)} %copy-done.4, f32[5,12,1,128]{3,2,1,0:T(1,128)} %broadcast_select_fusion.1.refs_4_.refs_9_), custom_call_target="tpu_custom_call" | custom-call | tf_op jit(solution)/shard_map/pallas_call | solution.py:224
  66.7 2.0 fusion.11
  68.8 1.9 collective-permute-start.7
  70.7 5.8 %collective-permute-start.6 = (f32[2,12,1,128]{3,2,1,0:T(1,128)S(1)}, f32[2,12,1,128]{3,2,1,0:T(1,128)S(1)}, u32[]{:S(2)}, u32[]{:S(2)}) collective-permute-start(f32[2,12,1,128]{3,2,1,0:T(1,128)S(1)} %get-tuple-element.20), channel_id=1, source_target_pairs={{0,1},{1,2},{2,3},{3,4},{4,5},{5,6},{6,7},{8,9},{9,10},{10,11},{11... | collective-permute-start | bytes 36872 | tf_op jit(solution)/shard_map/ppermute | solution.py:264
  78.1 21.4 %all_gather.13 = f32[2,12,1,2048]{3,2,1,0:T(1,128)S(1)} all-gather(f32[2,12,1,128]{3,2,1,0:T(1,128)S(1)} %get-tuple-element.20), channel_id=1, replica_groups=mesh['lon'=16,'lat'=8] {'lon'}, dimensions={3}, use_global_device_ids=true | all-gather | bytes 208896 | tf_op jit(solution)/shard_map/all_gather | solution.py:266
  105.6 12.3 %shard_map.123.refs_6_ = f32[4,12,96,128]{3,2,1,0:T(8,128)} custom-call(f32[5,12,96,128]{3,2,1,0:T(8,128)} %copy-done.1, f32[5,12,96,1]{3,2,1,0:T(8,128)} %copy.50.refs_1_.refs_6_, f32[5,12,96,1]{3,2,1,0:T(8,128)} %copy.51.refs_2_.refs_7_, f32[5,12,1,128]{3,2,1,0:T(1,128)} %copy-done.4, f32[5,12,1,128]{3,2,1,0:T(1,128)} %broadcast_select_fusion.1.refs_4_.refs_9_, ...), custom_call_target="tpu_custom_call" | custom-call | tf_op jit(solution)/shard_map/pallas_call | solution.py:224
  118.9 4.6 %fusion.7 = (f32[4,12,96,1]{3,2,1,0:T(8,128)}, f32[4,12,96,1]{3,2,1,0:T(8,128)S(1)}) fusion(f32[4,12,96,128]{3,2,1,0:T(8,128)} %shard_map.123.refs_6_), kind=kLoop, calls=%fused_computation.39 | loop fusion | bytes 73728 | tf_op jit(solution)/shard_map/slice | solution.py:263
  123.6 1.9 collective-permute-start.11
  125.5 5.8 %collective-permute-start.10 = (f32[4,12,1,128]{3,2,1,0:T(1,128)S(1)}, f32[4,12,1,128]{3,2,1,0:T(1,128)S(1)}, u32[]{:S(2)}, u32[]{:S(2)}) collective-permute-start(f32[4,12,1,128]{3,2,1,0:T(1,128)S(1)} %get-tuple-element.10), channel_id=1, source_target_pairs={{0,1},{1,2},{2,3},{3,4},{4,5},{5,6},{6,7},{8,9},{9,10},{10,11},{11... | collective-permute-start | bytes 73736 | tf_op jit(solution)/shard_map/ppermute | solution.py:264
  131.3 2.4 %copy.45 = f32[4,12,96,1]{2,0,3,1:T(4,128)S(1)} copy(f32[4,12,96,1]{3,2,1,0:T(8,128)} %get-tuple-element.11) | data formatting | bytes 36864 | tf_op jit(solution)/shard_map/slice | solution.py:263
  135.2 20.9 %all_gather.14 = f32[4,12,1,2048]{3,2,1,0:T(1,128)S(1)} all-gather(f32[4,12,1,128]{3,2,1,0:T(1,128)S(1)} %get-tuple-element.10), channel_id=1, replica_groups=mesh['lon'=16,'lat'=8] {'lon'}, dimensions={3}, use_global_device_ids=true | all-gather | bytes 417792 | tf_op jit(solution)/shard_map/all_gather | solution.py:266
  156.1 3.2 %copy.68 = f32[4,12,1,2048]{1,0,3,2:T(4,128)} copy(f32[4,12,1,2048]{3,2,1,0:T(1,128)S(1)} %all_gather.14) | data formatting | bytes 786432 | tf_op jit(solution)/shard_map/all_gather | solution.py:266
  159.2 2.9 %gather_fusion.2 = f32[128,4,12]{2,1,0:T(4,128)S(1)} fusion(f32[4,12,2048]{1,0,2:T(4,128)} %bitcast.38, s32[1024]{0:T(1024)S(1)} %pad_clamp_fusion.1), kind=kCustom, calls=%fused_computation.4 | custom fusion | bytes 49664 | tf_op jit(solution)/shard_map/jit(_take)/gather | solution.py:267
  162.3 2.2 copy.53.refs_8_
  164.5 2.1 copy.52.refs_7_
  167.9 14.7 %shard_map.124.refs_0_ = f32[2,12,96,128]{3,2,1,0:T(8,128)} custom-call(f32[5,12,96,128]{3,2,1,0:T(8,128)} %copy-done.1, f32[5,12,96,1]{3,2,1,0:T(8,128)} %copy.50.refs_1_.refs_6_, f32[5,12,96,1]{3,2,1,0:T(8,128)} %copy.51.refs_2_.refs_7_, f32[5,12,1,128]{3,2,1,0:T(1,128)} %copy-done.4, f32[5,12,1,128]{3,2,1,0:T(1,128)} %broadcast_select_fusion.1.refs_4_.refs_9_, ...), custom_call_target="tpu_custom_call" | custom-call | tf_op jit(solution)/shard_map/pallas_call | solution.py:224
  183.6 2.1 fusion.9
  185.6 1.9 collective-permute-start.15
  187.5 5.8 %collective-permute-start.14 = (f32[2,12,1,128]{3,2,1,0:T(1,128)S(1)}, f32[2,12,1,128]{3,2,1,0:T(1,128)S(1)}, u32[]{:S(2)}, u32[]{:S(2)}) collective-permute-start(f32[2,12,1,128]{3,2,1,0:T(1,128)S(1)} %get-tuple-element.16), channel_id=1, source_target_pairs={{0,1},{1,2},{2,3},{3,4},{4,5},{5,6},{6,7},{8,9},{9,10},{10,11},{11... | collective-permute-start | bytes 36872 | tf_op jit(solution)/shard_map/ppermute | solution.py:264
  194.9 20.1 %all_gather.15 = f32[2,12,1,2048]{3,2,1,0:T(1,128)S(1)} all-gather(f32[2,12,1,128]{3,2,1,0:T(1,128)S(1)} %get-tuple-element.16), channel_id=1, replica_groups=mesh['lon'=16,'lat'=8] {'lon'}, dimensions={3}, use_global_device_ids=true | all-gather | bytes 208896 | tf_op jit(solution)/shard_map/all_gather | solution.py:266
  221.1 12.1 %shard_map.125 = f32[2,12,96,128]{3,2,1,0:T(8,128)} custom-call(f32[2,12,96,128]{3,2,1,0:T(8,128)} %shard_map.124.refs_0_, f32[2,12,96,1]{3,2,1,0:T(8,128)} %copy.60.refs_1_, f32[2,12,96,1]{3,2,1,0:T(8,128)} %copy.61.refs_2_, f32[2,12,1,128]{3,2,1,0:T(1,128)} %copy-done.7, f32[2,12,1,128]{3,2,1,0:T(1,128)} %broadcast_select_fusion.6.refs_4_, ...), custom_call_target="tpu_custom_call" | custom-call | tf_op jit(solution)/shard_map/pallas_call | solution.py:224
  233.1 2.3 slice_bitcast_fusion
  (82 shorter events, 28.5 us)
Async XLA Ops:
  0.6 20.0 %copy-start = (s32[2048]{0:T(1024)S(1)}, s32[2048]{0:T(1024)}, u32[]{:S(2)}) copy-start(s32[2048]{0:T(1024)} %param.19) | copy-start | bytes 24580
  0.6 3.2 %copy-start.2 = (f32[12,96,128]{2,1,0:T(8,128)S(1)}, f32[12,96,128]{2,1,0:T(8,128)}, u32[]{:S(2)}) copy-start(f32[12,96,128]{2,1,0:T(8,128)} %param.15) | copy-start | bytes 1769476
  0.7 3.2 %copy-start.3 = (f32[12,96,128]{2,1,0:T(8,128)S(1)}, f32[12,96,128]{2,1,0:T(8,128)}, u32[]{:S(2)}) copy-start(f32[12,96,128]{2,1,0:T(8,128)} %param.16) | copy-start | bytes 1769476
  1.6 2.4 %copy-start.5 = (s32[96,128]{1,0:T(8,128)S(1)}, s32[96,128]{1,0:T(8,128)}, u32[]{:S(2)}) copy-start(s32[96,128]{1,0:T(8,128)} %param.18) | copy-start | bytes 147460
  4.0 10.5 %copy-start.1 = (f32[5,12,96,128]{3,2,1,0:T(8,128)}, f32[5,12,96,128]{3,2,1,0:T(8,128)S(1)}, u32[]{:S(2)}) copy-start(f32[5,12,96,128]{3,2,1,0:T(8,128)S(1)} %convert_dynamic-update-slice_fusion.refs_0_.refs_5_) | copy-start | bytes 8847364
  4.1 51.5 %collective-permute-start.3 = (f32[5,12,1,128]{3,2,1,0:T(1,128)S(1)}, f32[5,12,1,128]{3,2,1,0:T(1,128)S(1)}, u32[]{:S(2)}, u32[]{:S(2)}) collective-permute-start(f32[5,12,1,128]{3,2,1,0:T(1,128)S(1)} %get-tuple-element.5), channel_id=1, source_target_pairs={{1,0},{2,1},{3,2},{4,3},{5,4},{6,5},{7,6},{9,8},{10,9},{11,10},{12... | collective-permute-start | bytes 92168 | tf_op jit(solution)/shard_map/ppermute | solution.py:265
  7.0 49.3 %collective-permute-start.2 = (f32[5,12,1,128]{3,2,1,0:T(1,128)S(1)}, f32[5,12,1,128]{3,2,1,0:T(1,128)S(1)}, u32[]{:S(2)}, u32[]{:S(2)}) collective-permute-start(f32[5,12,1,128]{3,2,1,0:T(1,128)S(1)} %get-tuple-element.6), channel_id=1, source_target_pairs={{0,1},{1,2},{2,3},{3,4},{4,5},{5,6},{6,7},{8,9},{9,10},{10,11},{11... | collective-permute-start | bytes 92168 | tf_op jit(solution)/shard_map/ppermute | solution.py:264
  16.8 36.7 %collective-permute-start = (f32[5,12,96,1]{2,3,1,0:T(1,128)S(1)}, f32[5,12,96,1]{2,3,1,0:T(1,128)S(1)}, u32[]{:S(2)}, u32[]{:S(2)}) collective-permute-start(f32[5,12,96,1]{2,3,1,0:T(1,128)S(1)} %copy.28), channel_id=1, source_target_pairs={{0,8},{8,16},{16,24},{24,32},{32,40},{40,48},{48,56},{56,64},{64,7... | collective-permute-start | bytes 69128 | tf_op jit(solution)/shard_map/ppermute | solution.py:262
  20.5 30.7 %collective-permute-start.1 = (f32[5,12,96,1]{2,3,1,0:T(1,128)S(1)}, f32[5,12,96,1]{2,3,1,0:T(1,128)S(1)}, u32[]{:S(2)}, u32[]{:S(2)}) collective-permute-start(f32[5,12,96,1]{2,3,1,0:T(1,128)S(1)} %copy.29), channel_id=1, source_target_pairs={{8,0},{16,8},{24,16},{32,24},{40,32},{48,40},{56,48},{64,56},{72,6... | collective-permute-start | bytes 69128 | tf_op jit(solution)/shard_map/ppermute | solution.py:263
  51.2 4.3 %copy-start.9 = (f32[5]{0:T(128)S(1)}, f32[5]{0:T(128)}, u32[]{:S(2)}) copy-start(f32[5]{0:T(128)} %constant.72.clone) | copy-start | bytes 64
  56.3 0.6 copy-start.4
  68.8 35.6 %collective-permute-start.7 = (f32[2,12,1,128]{3,2,1,0:T(1,128)S(1)}, f32[2,12,1,128]{3,2,1,0:T(1,128)S(1)}, u32[]{:S(2)}, u32[]{:S(2)}) collective-permute-start(f32[2,12,1,128]{3,2,1,0:T(1,128)S(1)} %get-tuple-element.19), channel_id=1, source_target_pairs={{1,0},{2,1},{3,2},{4,3},{5,4},{6,5},{7,6},{9,8},{10,9},{11,10},{12... | collective-permute-start | bytes 36872 | tf_op jit(solution)/shard_map/ppermute | solution.py:265
  70.7 34.3 %collective-permute-start.6 = (f32[2,12,1,128]{3,2,1,0:T(1,128)S(1)}, f32[2,12,1,128]{3,2,1,0:T(1,128)S(1)}, u32[]{:S(2)}, u32[]{:S(2)}) collective-permute-start(f32[2,12,1,128]{3,2,1,0:T(1,128)S(1)} %get-tuple-element.20), channel_id=1, source_target_pairs={{0,1},{1,2},{2,3},{3,4},{4,5},{5,6},{6,7},{8,9},{9,10},{10,11},{11... | collective-permute-start | bytes 36872 | tf_op jit(solution)/shard_map/ppermute | solution.py:264
  77.3 25.7 %collective-permute-start.4 = (f32[2,12,96,1]{2,0,3,1:T(2,128)S(1)}, f32[2,12,96,1]{2,0,3,1:T(2,128)S(1)}, u32[]{:S(2)}, u32[]{:S(2)}) collective-permute-start(f32[2,12,96,1]{2,0,3,1:T(2,128)S(1)} %copy.34), channel_id=1, source_target_pairs={{0,8},{8,16},{16,24},{24,32},{32,40},{40,48},{48,56},{56,64},{64,7... | collective-permute-start | bytes 27656 | tf_op jit(solution)/shard_map/ppermute | solution.py:262
  77.8 23.7 %collective-permute-start.5 = (f32[2,12,96,1]{2,0,3,1:T(2,128)S(1)}, f32[2,12,96,1]{2,0,3,1:T(2,128)S(1)}, u32[]{:S(2)}, u32[]{:S(2)}) collective-permute-start(f32[2,12,96,1]{2,0,3,1:T(2,128)S(1)} %copy.35), channel_id=1, source_target_pairs={{8,0},{16,8},{24,16},{32,24},{40,32},{48,40},{56,48},{64,56},{72,6... | collective-permute-start | bytes 27656 | tf_op jit(solution)/shard_map/ppermute | solution.py:263
  105.0 0.6 copy-start.8
  123.6 43.0 %collective-permute-start.11 = (f32[4,12,1,128]{3,2,1,0:T(1,128)S(1)}, f32[4,12,1,128]{3,2,1,0:T(1,128)S(1)}, u32[]{:S(2)}, u32[]{:S(2)}) collective-permute-start(f32[4,12,1,128]{3,2,1,0:T(1,128)S(1)} %get-tuple-element.9), channel_id=1, source_target_pairs={{1,0},{2,1},{3,2},{4,3},{5,4},{6,5},{7,6},{9,8},{10,9},{11,10},{12... | collective-permute-start | bytes 73736 | tf_op jit(solution)/shard_map/ppermute | solution.py:265
  125.5 41.8 %collective-permute-start.10 = (f32[4,12,1,128]{3,2,1,0:T(1,128)S(1)}, f32[4,12,1,128]{3,2,1,0:T(1,128)S(1)}, u32[]{:S(2)}, u32[]{:S(2)}) collective-permute-start(f32[4,12,1,128]{3,2,1,0:T(1,128)S(1)} %get-tuple-element.10), channel_id=1, source_target_pairs={{0,1},{1,2},{2,3},{3,4},{4,5},{5,6},{6,7},{8,9},{9,10},{10,11},{11... | collective-permute-start | bytes 73736 | tf_op jit(solution)/shard_map/ppermute | solution.py:264
  134.4 30.1 %collective-permute-start.8 = (f32[4,12,96,1]{2,0,3,1:T(4,128)S(1)}, f32[4,12,96,1]{2,0,3,1:T(4,128)S(1)}, u32[]{:S(2)}, u32[]{:S(2)}) collective-permute-start(f32[4,12,96,1]{2,0,3,1:T(4,128)S(1)} %copy.44), channel_id=1, source_target_pairs={{0,8},{8,16},{16,24},{24,32},{32,40},{40,48},{48,56},{56,64},{64,7... | collective-permute-start | bytes 55304 | tf_op jit(solution)/shard_map/ppermute | solution.py:262
  134.4 27.9 %collective-permute-start.9 = (f32[4,12,96,1]{2,0,3,1:T(4,128)S(1)}, f32[4,12,96,1]{2,0,3,1:T(4,128)S(1)}, u32[]{:S(2)}, u32[]{:S(2)}) collective-permute-start(f32[4,12,96,1]{2,0,3,1:T(4,128)S(1)} %copy.45), channel_id=1, source_target_pairs={{8,0},{16,8},{24,16},{32,24},{40,32},{48,40},{56,48},{64,56},{72,6... | collective-permute-start | bytes 55304 | tf_op jit(solution)/shard_map/ppermute | solution.py:263
  167.3 0.6 copy-start.6
  185.6 34.2 %collective-permute-start.15 = (f32[2,12,1,128]{3,2,1,0:T(1,128)S(1)}, f32[2,12,1,128]{3,2,1,0:T(1,128)S(1)}, u32[]{:S(2)}, u32[]{:S(2)}) collective-permute-start(f32[2,12,1,128]{3,2,1,0:T(1,128)S(1)} %get-tuple-element.15), channel_id=1, source_target_pairs={{1,0},{2,1},{3,2},{4,3},{5,4},{6,5},{7,6},{9,8},{10,9},{11,10},{12... | collective-permute-start | bytes 36872 | tf_op jit(solution)/shard_map/ppermute | solution.py:265
  187.5 32.9 %collective-permute-start.14 = (f32[2,12,1,128]{3,2,1,0:T(1,128)S(1)}, f32[2,12,1,128]{3,2,1,0:T(1,128)S(1)}, u32[]{:S(2)}, u32[]{:S(2)}) collective-permute-start(f32[2,12,1,128]{3,2,1,0:T(1,128)S(1)} %get-tuple-element.16), channel_id=1, source_target_pairs={{0,1},{1,2},{2,3},{3,4},{4,5},{5,6},{6,7},{8,9},{9,10},{10,11},{11... | collective-permute-start | bytes 36872 | tf_op jit(solution)/shard_map/ppermute | solution.py:264
  194.1 24.3 %collective-permute-start.12 = (f32[2,12,96,1]{2,0,3,1:T(2,128)S(1)}, f32[2,12,96,1]{2,0,3,1:T(2,128)S(1)}, u32[]{:S(2)}, u32[]{:S(2)}) collective-permute-start(f32[2,12,96,1]{2,0,3,1:T(2,128)S(1)} %copy.54), channel_id=1, source_target_pairs={{0,8},{8,16},{16,24},{24,32},{32,40},{40,48},{48,56},{56,64},{64,7... | collective-permute-start | bytes 27656 | tf_op jit(solution)/shard_map/ppermute | solution.py:262
  194.1 22.8 %collective-permute-start.13 = (f32[2,12,96,1]{2,0,3,1:T(2,128)S(1)}, f32[2,12,96,1]{2,0,3,1:T(2,128)S(1)}, u32[]{:S(2)}, u32[]{:S(2)}) collective-permute-start(f32[2,12,96,1]{2,0,3,1:T(2,128)S(1)} %copy.55), channel_id=1, source_target_pairs={{8,0},{16,8},{24,16},{32,24},{40,32},{48,40},{56,48},{64,56},{72,6... | collective-permute-start | bytes 27656 | tf_op jit(solution)/shard_map/ppermute | solution.py:263
  220.5 0.6 copy-start.7

commit v2 on v1

--- a/solution.py
+++ b/solution.py
@@ -217,6 +217,140 @@
         return carry
 
     lax.fori_loop(0, levels, body, 0)
+
+
+def exchange_kernel(
+    lon,
+    lat,
+    west_col,
+    east_col,
+    south_row,
+    north_row,
+    gathered,
+    west_halo,
+    east_halo,
+    south_halo,
+    north_halo,
+    fold_send,
+    fold_recv,
+    side_send,
+    side_recv,
+):
+    mesh = pl.DeviceIdType.MESH
+    me = lax.axis_index("lon")
+    row = lax.axis_index("lat")
+    west = lax.rem(me + lon - 1, lon)
+    east = lax.rem(me + 1, lon)
+    has_south = row > 0
+    has_north = row < lat - 1
+
+    barrier = pltpu.get_barrier_semaphore()
+    for peer in range(lon):
+
+        @pl.when(me != peer)
+        def _():
+            pl.semaphore_signal(barrier, 1, device_id={"lon": peer}, device_id_type=mesh)
+
+    @pl.when(has_south)
+    def _():
+        pl.semaphore_signal(barrier, 1, device_id={"lat": row - 1}, device_id_type=mesh)
+
+    @pl.when(has_north)
+    def _():
+        pl.semaphore_signal(barrier, 1, device_id={"lat": row + 1}, device_id_type=mesh)
+
+    pl.semaphore_wait(
+        barrier, lon - 1 + has_south.astype(jnp.int32) + has_north.astype(jnp.int32)
+    )
+
+    def fold_copy(peer, slot):
+        return pltpu.make_async_remote_copy(
+            src_ref=north_row,
+            dst_ref=gathered.at[slot],
+            send_sem=fold_send.at[peer],
+            recv_sem=fold_recv.at[slot],
+            device_id={"lon": peer},
+            device_id_type=mesh,
+        )
+
+    for peer in range(lon):
+
+        @pl.when(me != peer)
+        def _():
+            fold_copy(peer, me).start()
+
+    to_west = pltpu.make_async_remote_copy(
+        src_ref=west_col,
+        dst_ref=east_halo,
+        send_sem=side_send.at[0],
+        recv_sem=side_recv.at[0],
+        device_id={"lon": west},
+        device_id_type=mesh,
+    )
+    to_east = pltpu.make_async_remote_copy(
+        src_ref=east_col,
+        dst_ref=west_halo,
+        send_sem=side_send.at[1],
+        recv_sem=side_recv.at[1],
+        device_id={"lon": east},
+        device_id_type=mesh,
+    )
+    to_west.start()
+    to_east.start()
+    to_south = pltpu.make_async_remote_copy(
+        src_ref=south_row,
+        dst_ref=north_halo,
+        send_sem=side_send.at[2],
+        recv_sem=side_recv.at[2],
+        device_id={"lat": row - 1},
+        device_id_type=mesh,
+    )
+    to_north = pltpu.make_async_remote_copy(
+        src_ref=north_row,
+        dst_ref=south_halo,
+        send_sem=side_send.at[3],
+        recv_sem=side_recv.at[3],
+        device_id={"lat": row + 1},
+        device_id_type=mesh,
+    )
+
+    @pl.when(has_south)
+    def _():
+        to_south.start()
+
+    @pl.when(has_north)
+    def _():
+        to_north.start()
+
+    gathered[me] = north_row[...]
+
+    for peer in range(lon):
+
+        @pl.when(me != peer)
+        def _():
+            fold_copy(peer, me).wait_send()
+            fold_copy(peer, peer).wait_recv()
+
+    to_west.wait()
+    to_east.wait()
+
+    @pl.when(has_south)
+    def _():
+        to_south.wait_send()
+        to_north.wait_recv()
+
+    @pl.when(has_north)
+    def _():
+        to_north.wait_send()
+        to_south.wait_recv()
+
+    @pl.when(jnp.logical_not(has_south))
+    def _():
+        south_halo[...] = jnp.zeros_like(south_halo)
+
+    @pl.when(jnp.logical_not(has_north))
+    def _():
+        north_halo[...] = jnp.zeros_like(north_halo)
 
 
 def stage(kernel, fields, *args):
@@ -256,24 +390,48 @@
     )
     facing = jnp.take(seam_partner_index, anchor + jnp.arange(span, dtype=jnp.int32))
 
-    def halos(stack, signs):
+    def halos(stack, signs, cid):
+        fields = stack.shape[0]
         lon = lax.axis_size("lon")
         lat = lax.axis_size("lat")
-        west = lax.ppermute(stack[..., -1:], "lon", [(i, (i + 1) % lon) for i in range(lon)])
-        east = lax.ppermute(stack[..., :1], "lon", [((i + 1) % lon, i) for i in range(lon)])
-        south = lax.ppermute(stack[:, :, -1:, :], "lat", [(i, i + 1) for i in range(lat - 1)])
-        north = lax.ppermute(stack[:, :, :1, :], "lat", [(i + 1, i) for i in range(lat - 1)])
-        top_row = lax.all_gather(stack[:, :, -1:, :], "lon", axis=3, tiled=True)
-        fold_row = jnp.take(top_row, facing, axis=3) * signs
-        return (stack, west, east, south, jnp.where(on_top, fold_row, north))
-
-    state_refs = halos(state, sign_column(STATE_SIGNS))
+        row_shape = jax.ShapeDtypeStruct((fields,) + stack.shape[1:2] + stack.shape[3:], jnp.float32)
+        col_shape = jax.ShapeDtypeStruct(stack.shape[:3], jnp.float32)
+        gathered, west, east, south, north = pl.pallas_call(
+            functools.partial(exchange_kernel, lon, lat),
+            out_shape=(
+                jax.ShapeDtypeStruct((lon,) + row_shape.shape, jnp.float32),
+                col_shape,
+                col_shape,
+                row_shape,
+                row_shape,
+            ),
+            in_specs=[pl.BlockSpec(memory_space=pltpu.VMEM)] * 4,
+            out_specs=[pl.BlockSpec(memory_space=pltpu.VMEM)] * 5,
+            scratch_shapes=[
+                pltpu.SemaphoreType.DMA((lon,)),
+                pltpu.SemaphoreType.DMA((lon,)),
+                pltpu.SemaphoreType.DMA((4,)),
+                pltpu.SemaphoreType.DMA((4,)),
+            ],
+            compiler_params=pltpu.CompilerParams(collective_id=cid, has_side_effects=True),
+        )(stack[..., 0], stack[..., -1], stack[:, :, 0, :], stack[:, :, -1, :])
+        top_row = jnp.moveaxis(gathered, 0, 2).reshape(row_shape.shape[:2] + (-1,))
+        fold_row = jnp.take(top_row, facing, axis=2)[:, :, None, :] * signs
+        return (
+            stack,
+            west[..., None],
+            east[..., None],
+            south[:, :, None, :],
+            jnp.where(on_top, fold_row, north[:, :, None, :]),
+        )
+
+    state_refs = halos(state, sign_column(STATE_SIGNS), 0)
     upwind = stage(upwind_kernel, 2, *state_refs)
-    upwind_refs = halos(upwind, sign_column((1.0, 1.0)))
+    upwind_refs = halos(upwind, sign_column((1.0, 1.0)), 1)
     ratio = stage(ratio_kernel, 4, *state_refs, *upwind_refs)
-    ratio_refs = halos(ratio, sign_column((1.0,) * 4))
+    ratio_refs = halos(ratio, sign_column((1.0,) * 4), 2)
     advected = stage(advected_kernel, 2, *state_refs, upwind, *ratio_refs)
-    advected_refs = halos(advected, sign_column((1.0, 1.0)))
+    advected_refs = halos(advected, sign_column((1.0, 1.0)), 3)
     final = stage(isopycnal_kernel, 2, *advected_refs, *state_refs)
     return (final[0], final[1])
 

time: 236 us -> 181 us (0.77)
  the two profiles are of different devices: /device:TPU:25 before, /device:TPU:1 now
where the time goes in v2:
time: 181 us; the launch traced here: 180 us
  Pallas kernels  99 us (55%)
  local copies, waits for them, and re-layouts  79.5 us (44%)
    pallas_call x4, Pallas kernels, halos(): pl.pallas_call(functools.partial(exchange_kernel, lon, lat), out_shape=(j...  51 us
    pallas_call x4, Pallas kernels, stage(): pl.pallas_call(kernel, out_shape=jax.ShapeDtypeStruct((fields,) + shape[1...  48 us
    unnamed x63, local copies, waits for them, and re-layouts  16 us
    reshape x4, local copies, waits for them, and re-layouts, halos(): top_row = jnp.moveaxis(gathered, 0, 2).reshape(row_shape.shape[:2] + (-1,))  15.5 us
    slice x4, local copies, waits for them, and re-layouts, halos(): stack[..., -1]  12.4 us
    gather x8, local copies, waits for them, and re-layouts, halos(): fold_row = jnp.take(top_row, facing, axis=2)[:, :, None, :] * signs  8.9 us
    broadcast_in_dim x4, local copies, waits for them, and re-layouts, halos(): east[..., None]  7.69 us
    broadcast_in_dim x4, local copies, waits for them, and re-layouts, halos(): west[..., None]  7.57 us

profile of v2, /device:TPU:1, one launch (start us, length us, event | category | flops | bytes accessed | tf_op | source)
XLA Modules:
  0.0 179.9 jit_solution(6253928245091120295)
XLA Ops:
  0.7 1.2 bitcast_dynamic-update-slice_fusion.3
  1.9 1.1 bitcast_dynamic-update-slice_fusion.2
  4.0 3.5 %slice_reduce_fusion = (f32[5,12,96]{2,1,0:T(8,128)}, f32[5,12,96]{2,1,0:T(8,128)}) fusion(f32[5,12,96,128]{3,2,1,0:T(8,128)S(1)} %convert_dynamic-update-slice_fusion.refs_0_.refs_5_), kind=kLoop, calls=%fused_computation.5 | loop fusion | bytes 92160 | tf_op jit(solution)/shard_map/slice | solution.py:417
  7.5 17.6 %shard_map.122 = (f32[16,5,12,128]{3,2,1,0:T(8,128)}, f32[5,12,96]{2,1,0:T(8,128)}, f32[5,12,96]{2,1,0:T(8,128)}, f32[5,12,128]{2,1,0:T(8,128)}, f32[5,12,128]{2,1,0:T(8,128)}) custom-call(f32[5,12,96]{2,1,0:T(8,128)} %get-tuple-element.44.west_col, f32[5,12,96]{2,1,0:T(8,128)} %get-tuple-element.43.east_col, f32[5,12,128]{2,1,0:T(8,128)} %get-tuple-element.64.south_row, ...), custom_call_target="tpu_custom_call" | custom-call | tf_op jit(solution)/shard_map/pallas_call | solution.py:399
  25.2 5.9 %copy.81 = f32[5,12,16,128]{1,0,3,2:T(8,128)} copy(f32[5,12,16,128]{3,1,0,2:T(8,128)} %bitcast.91) | data formatting | bytes 983040 | tf_op jit(solution)/shard_map/reshape | solution.py:418
  31.1 1.1 gather_fusion
  32.3 4.0 %gather_fusion.1 = f32[128,5,12]{2,1,0:T(8,128)S(1)} fusion(f32[5,12,2048]{1,0,2:T(8,128)} %bitcast.87, s32[1024]{0:T(1024)S(1)} %get-tuple-element.66), kind=kCustom, calls=%fused_computation.3 | custom fusion | bytes 61952 | tf_op jit(solution)/shard_map/jit(_take)/gather | solution.py:419
  37.3 2.5 %copy.58.refs_1_.refs_6_ = f32[5,12,96,1]{3,2,1,0:T(8,128)} copy(f32[5,12,96,1]{2,1,0,3:T(8,128)S(1)} %bitcast.108) | data formatting | bytes 46080 | tf_op jit(solution)/shard_map/broadcast_in_dim | solution.py:422
  39.8 2.6 %copy.59.refs_2_.refs_7_ = f32[5,12,96,1]{3,2,1,0:T(8,128)} copy(f32[5,12,96,1]{2,1,0,3:T(8,128)S(1)} %bitcast.107) | data formatting | bytes 46080 | tf_op jit(solution)/shard_map/broadcast_in_dim | solution.py:423
  43.0 8.9 %shard_map.123.refs_5_ = f32[2,12,96,128]{3,2,1,0:T(8,128)} custom-call(f32[5,12,96,128]{3,2,1,0:T(8,128)} %copy-done.1, f32[5,12,96,1]{3,2,1,0:T(8,128)} %copy.58.refs_1_.refs_6_, f32[5,12,96,1]{3,2,1,0:T(8,128)} %copy.59.refs_2_.refs_7_, f32[5,12,1,128]{3,2,1,0:T(1,128)} %broadcast_in_dim.86.refs_3_.refs_8_, f32[5,12,1,128]{3,2,1,0:T(1,128)} %select_n.113.refs_4_.refs_9_), custom_call_target="tpu_custom_call" | custom-call | tf_op jit(solution)/shard_map/pallas_call | solution.py:358
  51.9 2.0 %fusion.12 = (f32[2,12,96,1]{3,2,1,0:T(8,128)S(1)}, f32[2,12,96,1]{3,2,1,0:T(8,128)S(1)}) fusion(f32[2,12,96,128]{3,2,1,0:T(8,128)} %shard_map.123.refs_5_), kind=kLoop, calls=%fused_computation.50 | loop fusion | bytes 36864 | tf_op jit(solution)/shard_map/slice | solution.py:417
  58.3 9.2 %shard_map.124 = (f32[16,2,12,128]{3,2,1,0:T(8,128)}, f32[2,12,96]{2,1,0:T(8,128)}, f32[2,12,96]{2,1,0:T(8,128)}, f32[2,12,128]{2,1,0:T(8,128)}, f32[2,12,128]{2,1,0:T(8,128)}) custom-call(f32[2,12,96]{2,1,0:T(8,128)} %bitcast.99, f32[2,12,96]{2,1,0:T(8,128)} %bitcast.101, f32[2,12,128]{2,1,0:T(8,128)} %bitcast.105, f32[2,12,128]{2,1,0:T(8,128)} %bitcast.103), custom_call_target="tpu_custom_call" | custom-call | tf_op jit(solution)/shard_map/pallas_call | solution.py:399
  67.5 2.5 %copy.88 = f32[2,12,16,128]{1,0,3,2:T(2,128)S(1)} copy(f32[2,12,16,128]{3,1,0,2:T(8,128)} %bitcast.93) | data formatting | bytes 393216 | tf_op jit(solution)/shard_map/reshape | solution.py:418
  71.6 1.5 copy.43.refs_6_
  73.0 1.5 copy.44.refs_7_
  75.1 12.3 %shard_map.125.refs_6_ = f32[4,12,96,128]{3,2,1,0:T(8,128)} custom-call(f32[5,12,96,128]{3,2,1,0:T(8,128)} %copy-done.1, f32[5,12,96,1]{3,2,1,0:T(8,128)} %copy.58.refs_1_.refs_6_, f32[5,12,96,1]{3,2,1,0:T(8,128)} %copy.59.refs_2_.refs_7_, f32[5,12,1,128]{3,2,1,0:T(1,128)} %broadcast_in_dim.86.refs_3_.refs_8_, f32[5,12,1,128]{3,2,1,0:T(1,128)} %select_n.113.refs_4_.refs_9_, ...), custom_call_target="tpu_custom_call" | custom-call | tf_op jit(solution)/shard_map/pallas_call | solution.py:358
  87.5 4.8 %fusion.8 = (f32[4,12,96,1]{3,2,1,0:T(8,128)S(1)}, f32[4,12,96,1]{3,2,1,0:T(8,128)}) fusion(f32[4,12,96,128]{3,2,1,0:T(8,128)} %shard_map.125.refs_6_), kind=kLoop, calls=%fused_computation.46 | loop fusion | bytes 73728 | tf_op jit(solution)/shard_map/slice | solution.py:417
  92.3 3.2 %copy.117 = f32[4,12,96,1]{2,1,0,3:T(8,128)} copy(f32[4,12,96,1]{3,2,1,0:T(8,128)} %get-tuple-element.52) | data formatting | bytes 36864
  95.5 1.6 copy.118
  99.3 13.5 %shard_map.126 = (f32[16,4,12,128]{3,2,1,0:T(8,128)}, f32[4,12,96]{2,1,0:T(8,128)}, f32[4,12,96]{2,1,0:T(8,128)}, f32[4,12,128]{2,1,0:T(8,128)}, f32[4,12,128]{2,1,0:T(8,128)}) custom-call(f32[4,12,96]{2,1,0:T(8,128)} %bitcast.95, f32[4,12,96]{2,1,0:T(8,128)} %bitcast.96, f32[4,12,128]{2,1,0:T(8,128)} %bitcast.98, f32[4,12,128]{2,1,0:T(8,128)} %bitcast.97), custom_call_target="tpu_custom_call" | custom-call | tf_op jit(solution)/shard_map/pallas_call | solution.py:399
  112.9 4.5 %copy.95 = f32[4,12,16,128]{1,0,3,2:T(4,128)} copy(f32[4,12,16,128]{3,1,0,2:T(8,128)} %bitcast.92) | data formatting | bytes 786432 | tf_op jit(solution)/shard_map/reshape | solution.py:418
  117.4 3.0 %gather_fusion.2 = f32[128,4,12]{2,1,0:T(4,128)S(1)} fusion(f32[4,12,2048]{1,0,2:T(4,128)} %bitcast.88, s32[1024]{0:T(1024)S(1)} %get-tuple-element.66), kind=kCustom, calls=%fused_computation.4 | custom fusion | bytes 49664 | tf_op jit(solution)/shard_map/jit(_take)/gather | solution.py:419
  121.1 2.2 %copy.60.refs_7_ = f32[4,12,96,1]{3,2,1,0:T(8,128)} copy(f32[4,12,96,1]{2,1,0,3:T(8,128)S(1)} %bitcast.110) | data formatting | bytes 36864 | tf_op jit(solution)/shard_map/broadcast_in_dim | solution.py:422
  123.3 2.2 %copy.61.refs_8_ = f32[4,12,96,1]{3,2,1,0:T(8,128)} copy(f32[4,12,96,1]{2,1,0,3:T(8,128)S(1)} %bitcast.109) | data formatting | bytes 36864 | tf_op jit(solution)/shard_map/broadcast_in_dim | solution.py:423
  126.1 14.7 %shard_map.127.refs_0_ = f32[2,12,96,128]{3,2,1,0:T(8,128)} custom-call(f32[5,12,96,128]{3,2,1,0:T(8,128)} %copy-done.1, f32[5,12,96,1]{3,2,1,0:T(8,128)} %copy.58.refs_1_.refs_6_, f32[5,12,96,1]{3,2,1,0:T(8,128)} %copy.59.refs_2_.refs_7_, f32[5,12,1,128]{3,2,1,0:T(1,128)} %broadcast_in_dim.86.refs_3_.refs_8_, f32[5,12,1,128]{3,2,1,0:T(1,128)} %select_n.113.refs_4_.refs_9_, ...), custom_call_target="tpu_custom_call" | custom-call | tf_op jit(solution)/shard_map/pallas_call | solution.py:358
  140.8 2.1 %fusion.10 = (f32[2,12,96,1]{3,2,1,0:T(8,128)S(1)}, f32[2,12,96,1]{3,2,1,0:T(8,128)S(1)}) fusion(f32[2,12,96,128]{3,2,1,0:T(8,128)} %shard_map.127.refs_0_), kind=kLoop, calls=%fused_computation.48 | loop fusion | bytes 36864 | tf_op jit(solution)/shard_map/slice | solution.py:417
  147.3 10.6 %shard_map.128 = (f32[16,2,12,128]{3,2,1,0:T(8,128)}, f32[2,12,96]{2,1,0:T(8,128)}, f32[2,12,96]{2,1,0:T(8,128)}, f32[2,12,128]{2,1,0:T(8,128)}, f32[2,12,128]{2,1,0:T(8,128)}) custom-call(f32[2,12,96]{2,1,0:T(8,128)} %bitcast.100, f32[2,12,96]{2,1,0:T(8,128)} %bitcast.102, f32[2,12,128]{2,1,0:T(8,128)} %bitcast.106, f32[2,12,128]{2,1,0:T(8,128)} %bitcast.104), custom_call_target="tpu_custom_call" | custom-call | tf_op jit(solution)/shard_map/pallas_call | solution.py:399
  158.0 2.5 %copy.104 = f32[2,12,16,128]{1,0,3,2:T(2,128)S(1)} copy(f32[2,12,16,128]{3,1,0,2:T(8,128)} %bitcast.94) | data formatting | bytes 393216 | tf_op jit(solution)/shard_map/reshape | solution.py:418
  162.0 1.4 copy.75.refs_1_
  163.4 1.5 copy.76.refs_2_
  165.5 12.1 %shard_map.129 = f32[2,12,96,128]{3,2,1,0:T(8,128)} custom-call(f32[2,12,96,128]{3,2,1,0:T(8,128)} %shard_map.127.refs_0_, f32[2,12,96,1]{3,2,1,0:T(8,128)} %copy.75.refs_1_, f32[2,12,96,1]{3,2,1,0:T(8,128)} %copy.76.refs_2_, f32[2,12,1,128]{3,2,1,0:T(1,128)} %copy.77.refs_3_, f32[2,12,1,128]{3,2,1,0:T(1,128)} %copy.78.refs_4_, ...), custom_call_target="tpu_custom_call" | custom-call | tf_op jit(solution)/shard_map/pallas_call | solution.py:358
  177.6 2.3 %slice_bitcast_fusion = (f32[12,96,128]{2,1,0:T(8,128)}, f32[12,96,128]{2,1,0:T(8,128)}) fusion(f32[2,12,96,128]{3,2,1,0:T(8,128)} %shard_map.129), kind=kLoop, calls=%fused_computation.7 | loop fusion | bytes 2359296 | tf_op jit(solution)/shard_map/squeeze | solution.py:436
  (88 shorter events, 19.1 us)
Async XLA Ops:
  0.6 30.5 %copy-start = (s32[2048]{0:T(1024)S(1)}, s32[2048]{0:T(1024)}, u32[]{:S(2)}) copy-start(s32[2048]{0:T(1024)} %param.19) | copy-start | bytes 24580
  0.6 2.4 %copy-start.2 = (f32[12,96,128]{2,1,0:T(8,128)S(1)}, f32[12,96,128]{2,1,0:T(8,128)}, u32[]{:S(2)}) copy-start(f32[12,96,128]{2,1,0:T(8,128)} %param.15) | copy-start | bytes 1769476
  0.7 2.4 %copy-start.3 = (f32[12,96,128]{2,1,0:T(8,128)S(1)}, f32[12,96,128]{2,1,0:T(8,128)}, u32[]{:S(2)}) copy-start(f32[12,96,128]{2,1,0:T(8,128)} %param.16) | copy-start | bytes 1769476
  0.7 2.5 %copy-start.5 = (s32[96,128]{1,0:T(8,128)S(1)}, s32[96,128]{1,0:T(8,128)}, u32[]{:S(2)}) copy-start(s32[96,128]{1,0:T(8,128)} %param.17) | copy-start | bytes 147460
  0.7 2.5 %copy-start.4 = (s32[96,128]{1,0:T(8,128)S(1)}, s32[96,128]{1,0:T(8,128)}, u32[]{:S(2)}) copy-start(s32[96,128]{1,0:T(8,128)} %param.18) | copy-start | bytes 147460
  3.2 4.3 %copy-start.1 = (f32[5,12,96,128]{3,2,1,0:T(8,128)}, f32[5,12,96,128]{3,2,1,0:T(8,128)S(1)}, u32[]{:S(2)}) copy-start(f32[5,12,96,128]{3,2,1,0:T(8,128)S(1)} %convert_dynamic-update-slice_fusion.refs_0_.refs_5_) | copy-start | bytes 8847364
  25.2 11.4 %copy-start.7 = (f32[5,12,128]{2,1,0:T(8,128)S(1)}, f32[5,12,128]{2,1,0:T(8,128)}, u32[]{:S(2)}) copy-start(f32[5,12,128]{2,1,0:T(8,128)} %get-tuple-element.27) | copy-start | bytes 92164
  25.2 11.4 %copy-start.22 = (f32[5]{0:T(128)S(1)}, f32[5]{0:T(128)}, u32[]{:S(2)}) copy-start(f32[5]{0:T(128)} %constant.72.clone) | copy-start | bytes 64
  25.2 12.1 %copy-start.9 = (f32[5,12,96]{2,1,0:T(8,128)S(1)}, f32[5,12,96]{2,1,0:T(8,128)}, u32[]{:S(2)}) copy-start(f32[5,12,96]{2,1,0:T(8,128)} %get-tuple-element.23) | copy-start | bytes 69124
  31.1 8.7 %copy-start.8 = (f32[5,12,96]{2,1,0:T(8,128)S(1)}, f32[5,12,96]{2,1,0:T(8,128)}, u32[]{:S(2)}) copy-start(f32[5,12,96]{2,1,0:T(8,128)} %get-tuple-element.24) | copy-start | bytes 69124
  37.3 5.1 %copy-start.6 = (f32[5,12,128]{2,1,0:T(8,128)S(1)}, f32[5,12,128]{2,1,0:T(8,128)}, u32[]{:S(2)}) copy-start(f32[5,12,128]{2,1,0:T(8,128)} %get-tuple-element.25) | copy-start | bytes 92164
  67.5 3.4 %copy-start.19 = (f32[2,12,128]{2,1,0:T(8,128)S(1)}, f32[2,12,128]{2,1,0:T(8,128)}, u32[]{:S(2)}) copy-start(f32[2,12,128]{2,1,0:T(8,128)} %get-tuple-element.32) | copy-start | bytes 36868
  67.5 4.0 %copy-start.17 = (f32[2,12,96]{2,1,0:T(8,128)S(1)}, f32[2,12,96]{2,1,0:T(8,128)}, u32[]{:S(2)}) copy-start(f32[2,12,96]{2,1,0:T(8,128)} %get-tuple-element.28) | copy-start | bytes 27652
  67.5 5.5 %copy-start.16 = (f32[2,12,96]{2,1,0:T(8,128)S(1)}, f32[2,12,96]{2,1,0:T(8,128)}, u32[]{:S(2)}) copy-start(f32[2,12,96]{2,1,0:T(8,128)} %get-tuple-element.29) | copy-start | bytes 27652
  67.5 7.0 %copy-start.21 = (f32[2,12,128]{2,1,0:T(8,128)S(1)}, f32[2,12,128]{2,1,0:T(8,128)}, u32[]{:S(2)}) copy-start(f32[2,12,128]{2,1,0:T(8,128)} %get-tuple-element.30) | copy-start | bytes 36868
  112.9 7.6 %copy-start.12 = (f32[4,12,128]{2,1,0:T(8,128)S(1)}, f32[4,12,128]{2,1,0:T(8,128)}, u32[]{:S(2)}) copy-start(f32[4,12,128]{2,1,0:T(8,128)} %get-tuple-element.37) | copy-start | bytes 73732
  112.9 8.3 %copy-start.11 = (f32[4,12,96]{2,1,0:T(8,128)S(1)}, f32[4,12,96]{2,1,0:T(8,128)}, u32[]{:S(2)}) copy-start(f32[4,12,96]{2,1,0:T(8,128)} %get-tuple-element.33) | copy-start | bytes 55300
  117.4 5.9 %copy-start.10 = (f32[4,12,96]{2,1,0:T(8,128)S(1)}, f32[4,12,96]{2,1,0:T(8,128)}, u32[]{:S(2)}) copy-start(f32[4,12,96]{2,1,0:T(8,128)} %get-tuple-element.34) | copy-start | bytes 55300
  121.1 4.3 %copy-start.13 = (f32[4,12,128]{2,1,0:T(8,128)S(1)}, f32[4,12,128]{2,1,0:T(8,128)}, u32[]{:S(2)}) copy-start(f32[4,12,128]{2,1,0:T(8,128)} %get-tuple-element.35) | copy-start | bytes 73732
  157.9 3.4 %copy-start.18 = (f32[2,12,128]{2,1,0:T(8,128)S(1)}, f32[2,12,128]{2,1,0:T(8,128)}, u32[]{:S(2)}) copy-start(f32[2,12,128]{2,1,0:T(8,128)} %get-tuple-element.42) | copy-start | bytes 36868
  157.9 4.0 %copy-start.15 = (f32[2,12,96]{2,1,0:T(8,128)S(1)}, f32[2,12,96]{2,1,0:T(8,128)}, u32[]{:S(2)}) copy-start(f32[2,12,96]{2,1,0:T(8,128)} %get-tuple-element.38) | copy-start | bytes 27652
  157.9 5.5 %copy-start.14 = (f32[2,12,96]{2,1,0:T(8,128)S(1)}, f32[2,12,96]{2,1,0:T(8,128)}, u32[]{:S(2)}) copy-start(f32[2,12,96]{2,1,0:T(8,128)} %get-tuple-element.39) | copy-start | bytes 27652
  158.0 6.9 %copy-start.20 = (f32[2,12,128]{2,1,0:T(8,128)S(1)}, f32[2,12,128]{2,1,0:T(8,128)}, u32[]{:S(2)}) copy-start(f32[2,12,128]{2,1,0:T(8,128)} %get-tuple-element.40) | copy-start | bytes 36868

commit v3 on v1

--- a/solution.py
+++ b/solution.py
@@ -33,7 +33,9 @@
 
 def sides_of(refs, f, k):
     block, west, east, south, north = refs
-    return around(block[f, k], west[f, k], east[f, k], south[f, k], north[f, k])
+    return around(
+        block[f, k], west[f, k], east[f, k], south[f, pl.ds(k, 1), :], north[f, pl.ds(k, 1), :]
+    )
 
 
 def low_order(tracer, zonal, meridional, wet_sides):
@@ -219,14 +221,225 @@
     lax.fori_loop(0, levels, body, 0)
 
 
-def stage(kernel, fields, *args):
-    shape = args[0].shape
+class Pair:
+    def __init__(self, first, second):
+        self.refs = (first, second)
+        self.shape = (2,) + first.shape
+
+    def __setitem__(self, index, value):
+        self.refs[index[0]][index[1]] = value
+
+
+def buffers_for(fields, levels, height, width, lon):
+    columns = pltpu.VMEM((fields, 16, height), jnp.float32)
+    rows = pltpu.VMEM((fields, levels, width), jnp.float32)
+    halo = pltpu.VMEM((fields, levels, height, 1), jnp.float32)
+    return [
+        columns,
+        columns,
+        rows,
+        rows,
+        columns,
+        columns,
+        rows,
+        rows,
+        pltpu.VMEM((lon, fields, levels, width), jnp.float32),
+        halo,
+        halo,
+        rows,
+    ]
+
+
+STAGE_FIELDS = (5, 2, 4, 2)
+
+
+def fused_kernel(lon, lat, signs, blocks, reverse, state, first_out, second_out, *scratch):
+    mesh = pl.DeviceIdType.MESH
+    upwind, ratio, advected = scratch[:3]
+    count = len(STAGE_FIELDS)
+    per_stage = [scratch[3 + 12 * s : 15 + 12 * s] for s in range(count)]
+    fold_send, fold_recv, side_send, side_recv = scratch[3 + 12 * count :]
+    me = lax.axis_index("lon")
+    row = lax.axis_index("lat")
+    west = lax.rem(me + lon - 1, lon)
+    east = lax.rem(me + 1, lon)
+    has_south = row > 0
+    has_north = row < lat - 1
+    on_top = row == lat - 1
+    levels, height, width = state.shape[1:]
+
+    barrier = pltpu.get_barrier_semaphore()
+    for peer in range(lon):
+
+        @pl.when(me != peer)
+        def _():
+            pl.semaphore_signal(barrier, 1, device_id={"lon": peer}, device_id_type=mesh)
+
+    @pl.when(has_south)
+    def _():
+        pl.semaphore_signal(barrier, 1, device_id={"lat": row - 1}, device_id_type=mesh)
+
+    @pl.when(has_north)
+    def _():
+        pl.semaphore_signal(barrier, 1, device_id={"lat": row + 1}, device_id_type=mesh)
+
+    pl.semaphore_wait(
+        barrier, lon - 1 + has_south.astype(jnp.int32) + has_north.astype(jnp.int32)
+    )
+
+    def exchange(s, source):
+        wsend, esend, ssend, nsend, whalo, ehalo, shalo, nhalo, gathered, wcol, ecol, north = (
+            per_stage[s]
+        )
+        fields = source.shape[0]
+        lane = lax.broadcasted_iota(jnp.int32, (height, width), 1)
+        for f in range(fields):
+            packed = jnp.zeros((height, width), jnp.float32)
+            for k in range(levels):
+                tile = source[f, k]
+                packed = jnp.where(lane == k, tile[:, 0:1], packed)
+                packed = jnp.where(lane == 16 + k, tile[:, width - 1 : width], packed)
+                ssend[f, pl.ds(k, 1), :] = tile[0:1, :]
+                nsend[f, pl.ds(k, 1), :] = tile[height - 1 : height, :]
+            flipped = packed.T
+            wsend[f] = flipped[0:16, :]
+            esend[f] = flipped[16:32, :]
+
+        def fold_copy(peer, slot):
+            return pltpu.make_async_remote_copy(
+                src_ref=nsend,
+                dst_ref=gathered.at[slot],
+                send_sem=fold_send.at[s, peer],
+                recv_sem=fold_recv.at[s, slot],
+                device_id={"lon": peer},
+                device_id_type=mesh,
+            )
+
+        for peer in range(lon):
+
+            @pl.when(me != peer)
+            def _():
+                fold_copy(peer, me).start()
+
+        def side(i, src, dst, device):
+            return pltpu.make_async_remote_copy(
+                src_ref=src,
+                dst_ref=dst,
+                send_sem=side_send.at[s, i],
+                recv_sem=side_recv.at[s, i],
+                device_id=device,
+                device_id_type=mesh,
+            )
+
+        to_west = side(0, wsend, ehalo, {"lon": west})
+        to_east = side(1, esend, whalo, {"lon": east})
+        to_south = side(2, ssend, nhalo, {"lat": row - 1})
+        to_north = side(3, nsend, shalo, {"lat": row + 1})
+        to_west.start()
+        to_east.start()
+
+        @pl.when(has_south)
+        def _():
+            to_south.start()
+
+        @pl.when(has_north)
+        def _():
+            to_north.start()
+
+        gathered[me] = nsend[...]
+
+        for peer in range(lon):
+
+            @pl.when(me != peer)
+            def _():
+                fold_copy(peer, me).wait_send()
+                fold_copy(peer, peer).wait_recv()
+
+        to_west.wait()
+        to_east.wait()
+
+        @pl.when(has_south)
+        def _():
+            to_south.wait_send()
+            to_north.wait_recv()
+
+        @pl.when(has_north)
+        def _():
+            to_north.wait_send()
+            to_south.wait_recv()
+
+        @pl.when(jnp.logical_not(has_south))
+        def _():
+            shalo[...] = jnp.zeros_like(shalo)
+
+        @pl.when(jnp.logical_not(has_north))
+        def _():
+            nhalo[...] = jnp.zeros_like(nhalo)
+
+        lower, upper = blocks[0], blocks[1]
+        for f in range(fields):
+            both = jnp.concatenate([whalo[f], ehalo[f]], axis=0).T
+            for k in range(levels):
+                wcol[f, k] = both[:, k : k + 1]
+                ecol[f, k] = both[:, 16 + k : 17 + k]
+            ghost = jnp.dot(
+                gathered[lower, f],
+                reverse[0],
+                precision=lax.Precision.HIGHEST,
+                preferred_element_type=jnp.float32,
+            ) + jnp.dot(
+                gathered[upper, f],
+                reverse[1],
+                precision=lax.Precision.HIGHEST,
+                preferred_element_type=jnp.float32,
+            )
+            sign = signs[f] if s == 0 else 1.0
+            north[f] = jnp.where(on_top, ghost * sign, nhalo[f])
+        return (source, wcol, ecol, shalo, north)
+
+    state_refs = exchange(0, state)
+    upwind_kernel(*state_refs, upwind)
+    upwind_refs = exchange(1, upwind)
+    ratio_kernel(*state_refs, *upwind_refs, ratio)
+    ratio_refs = exchange(2, ratio)
+    advected_kernel(*state_refs, upwind, *ratio_refs, advected)
+    advected_refs = exchange(3, advected)
+    isopycnal_kernel(*advected_refs, *state_refs, Pair(first_out, second_out))
+
+
+def fused(state, blocks, reverse):
+    lon = lax.axis_size("lon")
+    lat = lax.axis_size("lat")
+    levels, height, width = state.shape[1:]
+    block = jax.ShapeDtypeStruct((levels, height, width), jnp.float32)
+    scratch = [
+        pltpu.VMEM((2, levels, height, width), jnp.float32),
+        pltpu.VMEM((4, levels, height, width), jnp.float32),
+        pltpu.VMEM((2, levels, height, width), jnp.float32),
+    ]
+    for fields in STAGE_FIELDS:
+        scratch += buffers_for(fields, levels, height, width, lon)
+    count = len(STAGE_FIELDS)
+    scratch += [
+        pltpu.SemaphoreType.DMA((count, lon)),
+        pltpu.SemaphoreType.DMA((count, lon)),
+        pltpu.SemaphoreType.DMA((count, 4)),
+        pltpu.SemaphoreType.DMA((count, 4)),
+    ]
     return pl.pallas_call(
-        kernel,
-        out_shape=jax.ShapeDtypeStruct((fields,) + shape[1:], jnp.float32),
-        in_specs=[pl.BlockSpec(memory_space=pltpu.VMEM)] * len(args),
-        out_specs=pl.BlockSpec(memory_space=pltpu.VMEM),
-    )(*args)
+        functools.partial(fused_kernel, lon, lat, STATE_SIGNS),
+        out_shape=(block, block),
+        in_specs=[
+            pl.BlockSpec(memory_space=pltpu.SMEM),
+            pl.BlockSpec(memory_space=pltpu.VMEM),
+            pl.BlockSpec(memory_space=pltpu.VMEM),
+        ],
+        out_specs=[pl.BlockSpec(memory_space=pltpu.VMEM)] * 2,
+        scratch_shapes=scratch,
+        compiler_params=pltpu.CompilerParams(
+            collective_id=0, has_side_effects=True, vmem_limit_bytes=60 * 1024 * 1024
+        ),
+    )(blocks, reverse, state)
 
 
 def local(
@@ -239,8 +452,7 @@
     seam_partner_index,
 ):
     span = heat_content_field.shape[2]
-    anchor = lax.axis_index("lon") * span
-    on_top = lax.axis_index("lat") == lax.axis_size("lat") - 1
+    lon = lax.axis_size("lon")
     vertical_layer = jnp.arange(heat_content_field.shape[0], dtype=jnp.int32)[:, None, None]
     submerged_indicator = (
         (seawater_indicator[None] == 1) & (vertical_layer < submerged_layer_total[None])
@@ -254,28 +466,16 @@
             submerged_indicator,
         ]
     )
-    facing = jnp.take(seam_partner_index, anchor + jnp.arange(span, dtype=jnp.int32))
-
-    def halos(stack, signs):
-        lon = lax.axis_size("lon")
-        lat = lax.axis_size("lat")
-        west = lax.ppermute(stack[..., -1:], "lon", [(i, (i + 1) % lon) for i in range(lon)])
-        east = lax.ppermute(stack[..., :1], "lon", [((i + 1) % lon, i) for i in range(lon)])
-        south = lax.ppermute(stack[:, :, -1:, :], "lat", [(i, i + 1) for i in range(lat - 1)])
-        north = lax.ppermute(stack[:, :, :1, :], "lat", [(i + 1, i) for i in range(lat - 1)])
-        top_row = lax.all_gather(stack[:, :, -1:, :], "lon", axis=3, tiled=True)
-        fold_row = jnp.take(top_row, facing, axis=3) * signs
-        return (stack, west, east, south, jnp.where(on_top, fold_row, north))
-
-    state_refs = halos(state, sign_column(STATE_SIGNS))
-    upwind = stage(upwind_kernel, 2, *state_refs)
-    upwind_refs = halos(upwind, sign_column((1.0, 1.0)))
-    ratio = stage(ratio_kernel, 4, *state_refs, *upwind_refs)
-    ratio_refs = halos(ratio, sign_column((1.0,) * 4))
-    advected = stage(advected_kernel, 2, *state_refs, upwind, *ratio_refs)
-    advected_refs = halos(advected, sign_column((1.0, 1.0)))
-    final = stage(isopycnal_kernel, 2, *advected_refs, *state_refs)
-    return (final[0], final[1])
+    pivot = seam_partner_index[0]
+    pivot_block, pivot_offset = pivot // span, pivot % span
+    me = lax.axis_index("lon")
+    blocks = jnp.stack([(pivot_block - me - 1) % lon, (pivot_block - me) % lon]).astype(jnp.int32)
+    source = lax.broadcasted_iota(jnp.int32, (span, span), 0)
+    target = lax.broadcasted_iota(jnp.int32, (span, span), 1)
+    reverse = jnp.stack(
+        [source == span + pivot_offset - target, source == pivot_offset - target]
+    ).astype(jnp.float32)
+    return fused(state, blocks, reverse)
 
 
 def solution(mesh):

time: 236 us -> 88 us (0.37)
  the two profiles are of different devices: /device:TPU:25 before, /device:TPU:32 now
where the time goes in v3:
time: 88 us; the launch traced here: 87.6 us
  Pallas kernels  72.9 us (83%)
  local copies, waits for them, and re-layouts  9.02 us (10%)
  between operations  3.39 us (4%)
  other arithmetic  2.25 us (3%)
    pallas_call x1, Pallas kernels, fused(): pl.pallas_call(functools.partial(fused_kernel, lon, lat, STATE_SIGNS), ou...  72.9 us
    unnamed x14, local copies, waits for them, and re-layouts  7.73 us

profile of v3, /device:TPU:32, one launch (start us, length us, event | category | flops | bytes accessed | tf_op | source)
XLA Modules:
  0.0 87.6 jit_solution(12501432354493011889)
XLA Ops:
  0.6 0.0 copy-start.2
  0.6 0.0 copy-start.1
  0.7 1.3 %slice.3 = s32[1]{0:T(128)} slice(s32[2048]{0:T(1024)} %param.13), slice={[0:1]} | slice | bytes 8 | tf_op jit(solution)/shard_map/slice | solution.py:469
  4.6 0.0 copy-start.3
  4.6 0.7 pad_add_fusion.blocks
  5.3 0.8 broadcast_compare_fusion
  6.1 0.7 add_convert_fusion.reverse
  6.8 1.1 %bitcast_dynamic-update-slice_fusion.3 = f32[5,12,96,128]{3,2,1,0:T(8,128)S(1)} fusion(f32[12,96,128]{2,1,0:T(8,128)} %param.7), kind=kLoop, calls=%fused_computation.3 | loop fusion | bytes 1179648
  7.9 1.1 %bitcast_dynamic-update-slice_fusion.2 = f32[5,12,96,128]{3,2,1,0:T(8,128)S(1)} fusion(f32[5,12,96,128]{3,2,1,0:T(8,128)S(1)} %bitcast_dynamic-update-slice_fusion.3, f32[12,96,128]{2,1,0:T(8,128)} %param.8), kind=kLoop, calls=%fused_computation.2 | loop fusion | bytes 1179648
  9.0 0.0 copy-done.1
  9.1 0.0 copy-done.2
  9.1 0.0 copy-done.3
  9.1 0.1 convert_dynamic-update-slice_fusion.state
  9.2 0.0 copy-start
  9.2 1.6 %copy-done = f32[5,12,96,128]{3,2,1,0:T(8,128)} copy-done((f32[5,12,96,128]{3,2,1,0:T(8,128)}, f32[5,12,96,128]{3,2,1,0:T(8,128)S(1)}, u32[]{:S(2)}) %copy-start) | copy-done | bytes 2949144
  10.8 72.9 %shard_map.86 = (f32[12,96,128]{2,1,0:T(8,128)}, f32[12,96,128]{2,1,0:T(8,128)}) custom-call(s32[2]{0:T(128)} %pad_add_fusion.blocks, f32[2,128,128]{2,1,0:T(8,128)} %add_convert_fusion.reverse, f32[5,12,96,128]{3,2,1,0:T(8,128)} %copy-done), custom_call_target="tpu_custom_call" | custom-call | tf_op jit(solution)/shard_map/pallas_call | solution.py:429
  83.7 1.9 %copy.15 = f32[12,96,128]{2,1,0:T(8,128)} copy(f32[12,96,128]{2,1,0:T(8,128)} %get-tuple-element.6) | data formatting | bytes 1179648
  85.7 1.9 %copy.16 = f32[12,96,128]{2,1,0:T(8,128)} copy(f32[12,96,128]{2,1,0:T(8,128)} %get-tuple-element.7) | data formatting | bytes 1179648
  (5 shorter events, 0.1 us)
Async XLA Ops:
  0.6 8.4 %copy-start.2 = (f32[12,96,128]{2,1,0:T(8,128)S(1)}, f32[12,96,128]{2,1,0:T(8,128)}, u32[]{:S(2)}) copy-start(f32[12,96,128]{2,1,0:T(8,128)} %param.10) | copy-start | bytes 1769476
  0.6 8.4 %copy-start.1 = (f32[12,96,128]{2,1,0:T(8,128)S(1)}, f32[12,96,128]{2,1,0:T(8,128)}, u32[]{:S(2)}) copy-start(f32[12,96,128]{2,1,0:T(8,128)} %param.9) | copy-start | bytes 1769476
  4.6 4.5 %copy-start.3 = (s32[96,128]{1,0:T(8,128)S(1)}, s32[96,128]{1,0:T(8,128)}, u32[]{:S(2)}) copy-start(s32[96,128]{1,0:T(8,128)} %param.12) | copy-start | bytes 147460
  9.2 1.6 %copy-start = (f32[5,12,96,128]{3,2,1,0:T(8,128)}, f32[5,12,96,128]{3,2,1,0:T(8,128)S(1)}, u32[]{:S(2)}) copy-start(f32[5,12,96,128]{3,2,1,0:T(8,128)S(1)} %convert_dynamic-update-slice_fusion.state) | copy-start | bytes 8847364

commit v4 on v3

--- a/solution.py
+++ b/solution.py
@@ -128,27 +128,31 @@
     )
 
 
-def upwind_kernel(*refs):
-    state_refs, out = refs[:5], refs[5]
+def upwind_kernel(state_refs, out, anti_out, flow_out):
     levels = out.shape[1]
 
     def body(k, carry):
         for tracer in range(2):
-            (upwind, _, _, _), _ = level_low_order(state_refs, k, tracer)
+            (upwind, anti, inflow, outflow), _ = level_low_order(state_refs, k, tracer)
             out[tracer, k] = upwind
+            for face in range(4):
+                anti_out[4 * tracer + face, k] = anti[face]
+            flow_out[tracer, k] = inflow
+            flow_out[2 + tracer, k] = outflow
         return carry
 
     lax.fori_loop(0, levels, body, 0)
 
 
-def ratio_kernel(*refs):
-    state_refs, upwind_refs, out = refs[:5], refs[5:10], refs[10]
+def ratio_kernel(state_refs, upwind_refs, flow, out):
     levels = out.shape[1]
 
     def body(k, carry):
+        wet_sides = sides_of(state_refs, 4, k)
         for tracer in range(2):
-            (_, _, inflow, outflow), wet_sides = level_low_order(state_refs, k, tracer)
-            plus, minus = ratio_pair(sides_of(upwind_refs, tracer, k), wet_sides, inflow, outflow)
+            plus, minus = ratio_pair(
+                sides_of(upwind_refs, tracer, k), wet_sides, flow[tracer, k], flow[2 + tracer, k]
+            )
             out[tracer, k] = plus
             out[2 + tracer, k] = minus
         return carry
@@ -156,16 +160,16 @@
     lax.fori_loop(0, levels, body, 0)
 
 
-def advected_kernel(*refs):
-    state_refs, upwind_ref, ratio_refs, out = refs[:5], refs[5], refs[6:11], refs[11]
+def advected_kernel(wet, upwind_ref, anti_ref, ratio_refs, out):
     levels = out.shape[1]
 
     def body(k, carry):
+        wet_centre = wet[k]
         for tracer in range(2):
-            (_, anti, _, _), wet_sides = level_low_order(state_refs, k, tracer)
+            anti = tuple(anti_ref[4 * tracer + face, k] for face in range(4))
             plus = sides_of(ratio_refs, tracer, k)
             minus = sides_of(ratio_refs, 2 + tracer, k)
-            out[tracer, k] = limited(plus, minus, upwind_ref[tracer, k], anti, wet_sides[0])
+            out[tracer, k] = limited(plus, minus, upwind_ref[tracer, k], anti, wet_centre)
         return carry
 
     lax.fori_loop(0, levels, body, 0)
@@ -219,6 +223,15 @@
         return carry
 
     lax.fori_loop(0, levels, body, 0)
+
+
+class Stack:
+    def __init__(self, *refs):
+        self.refs = refs
+        self.shape = (len(refs),) + refs[0].shape
+
+    def __getitem__(self, index):
+        return self.refs[index[0]][index[1:]]
 
 
 class Pair:
@@ -253,12 +266,14 @@
 STAGE_FIELDS = (5, 2, 4, 2)
 
 
-def fused_kernel(lon, lat, signs, blocks, reverse, state, first_out, second_out, *scratch):
+def fused_kernel(
+    lon, lat, signs, seam, heat, salt, zonal, meridional, sea, depth, first_out, second_out, *scratch
+):
     mesh = pl.DeviceIdType.MESH
-    upwind, ratio, advected = scratch[:3]
+    upwind, ratio, advected, anti, flow, wet = scratch[:6]
     count = len(STAGE_FIELDS)
-    per_stage = [scratch[3 + 12 * s : 15 + 12 * s] for s in range(count)]
-    fold_send, fold_recv, side_send, side_recv = scratch[3 + 12 * count :]
+    per_stage = [scratch[6 + 12 * s : 18 + 12 * s] for s in range(count)]
+    fold_send, fold_recv, side_send, side_recv = scratch[6 + 12 * count :]
     me = lax.axis_index("lon")
     row = lax.axis_index("lat")
     west = lax.rem(me + lon - 1, lon)
@@ -266,7 +281,21 @@
     has_south = row > 0
     has_north = row < lat - 1
     on_top = row == lat - 1
-    levels, height, width = state.shape[1:]
+    levels, height, width = heat.shape
+    wet_column = sea[...] == 1
+    for k in range(levels):
+        wet[k] = jnp.where(wet_column & (k < depth[...]), 1.0, 0.0).astype(jnp.float32)
+    state = Stack(heat, salt, zonal, meridional, wet)
+    pivot = seam[0]
+    pivot_block, pivot_offset = pivot // width, pivot % width
+    lower = lax.rem(pivot_block - me - 1 + 2 * lon, lon)
+    upper = lax.rem(pivot_block - me + 2 * lon, lon)
+    source_lane = lax.broadcasted_iota(jnp.int32, (width, width), 0)
+    target_lane = lax.broadcasted_iota(jnp.int32, (width, width), 1)
+    reverse = (
+        jnp.where(source_lane == width + pivot_offset - target_lane, 1.0, 0.0).astype(jnp.float32),
+        jnp.where(source_lane == pivot_offset - target_lane, 1.0, 0.0).astype(jnp.float32),
+    )
 
     barrier = pltpu.get_barrier_semaphore()
     for peer in range(lon):
@@ -376,7 +405,6 @@
         def _():
             nhalo[...] = jnp.zeros_like(nhalo)
 
-        lower, upper = blocks[0], blocks[1]
         for f in range(fields):
             both = jnp.concatenate([whalo[f], ehalo[f]], axis=0).T
             for k in range(levels):
@@ -398,48 +426,48 @@
         return (source, wcol, ecol, shalo, north)
 
     state_refs = exchange(0, state)
-    upwind_kernel(*state_refs, upwind)
+    upwind_kernel(state_refs, upwind, anti, flow)
     upwind_refs = exchange(1, upwind)
-    ratio_kernel(*state_refs, *upwind_refs, ratio)
+    ratio_kernel(state_refs, upwind_refs, flow, ratio)
     ratio_refs = exchange(2, ratio)
-    advected_kernel(*state_refs, upwind, *ratio_refs, advected)
+    advected_kernel(wet, upwind, anti, ratio_refs, advected)
     advected_refs = exchange(3, advected)
     isopycnal_kernel(*advected_refs, *state_refs, Pair(first_out, second_out))
 
 
-def fused(state, blocks, reverse):
+def fused(fields, seam):
     lon = lax.axis_size("lon")
     lat = lax.axis_size("lat")
-    levels, height, width = state.shape[1:]
+    levels, height, width = fields[0].shape
     block = jax.ShapeDtypeStruct((levels, height, width), jnp.float32)
     scratch = [
         pltpu.VMEM((2, levels, height, width), jnp.float32),
         pltpu.VMEM((4, levels, height, width), jnp.float32),
         pltpu.VMEM((2, levels, height, width), jnp.float32),
+        pltpu.VMEM((8, levels, height, width), jnp.float32),
+        pltpu.VMEM((4, levels, height, width), jnp.float32),
+        pltpu.VMEM((levels, height, width), jnp.float32),
     ]
-    for fields in STAGE_FIELDS:
-        scratch += buffers_for(fields, levels, height, width, lon)
-    count = len(STAGE_FIELDS)
+    for count in STAGE_FIELDS:
+        scratch += buffers_for(count, levels, height, width, lon)
+    stages = len(STAGE_FIELDS)
     scratch += [
-        pltpu.SemaphoreType.DMA((count, lon)),
-        pltpu.SemaphoreType.DMA((count, lon)),
-        pltpu.SemaphoreType.DMA((count, 4)),
-        pltpu.SemaphoreType.DMA((count, 4)),
+        pltpu.SemaphoreType.DMA((stages, lon)),
+        pltpu.SemaphoreType.DMA((stages, lon)),
+        pltpu.SemaphoreType.DMA((stages, 4)),
+        pltpu.SemaphoreType.DMA((stages, 4)),
     ]
     return pl.pallas_call(
         functools.partial(fused_kernel, lon, lat, STATE_SIGNS),
         out_shape=(block, block),
-        in_specs=[
-            pl.BlockSpec(memory_space=pltpu.SMEM),
-            pl.BlockSpec(memory_space=pltpu.VMEM),
-            pl.BlockSpec(memory_space=pltpu.VMEM),
-        ],
+        in_specs=[pl.BlockSpec(memory_space=pltpu.SMEM)]
+        + [pl.BlockSpec(memory_space=pltpu.VMEM)] * len(fields),
         out_specs=[pl.BlockSpec(memory_space=pltpu.VMEM)] * 2,
         scratch_shapes=scratch,
         compiler_params=pltpu.CompilerParams(
             collective_id=0, has_side_effects=True, vmem_limit_bytes=60 * 1024 * 1024
         ),
-    )(blocks, reverse, state)
+    )(seam, *fields)
 
 
 def local(
@@ -451,31 +479,17 @@
     submerged_layer_total,
     seam_partner_index,
 ):
-    span = heat_content_field.shape[2]
-    lon = lax.axis_size("lon")
-    vertical_layer = jnp.arange(heat_content_field.shape[0], dtype=jnp.int32)[:, None, None]
-    submerged_indicator = (
-        (seawater_indicator[None] == 1) & (vertical_layer < submerged_layer_total[None])
-    ).astype(jnp.float32)
-    state = jnp.stack(
-        [
+    return fused(
+        (
             heat_content_field,
             saltiness_field,
             eastward_cfl_number,
             northward_cfl_number,
-            submerged_indicator,
-        ]
-    )
-    pivot = seam_partner_index[0]
-    pivot_block, pivot_offset = pivot // span, pivot % span
-    me = lax.axis_index("lon")
-    blocks = jnp.stack([(pivot_block - me - 1) % lon, (pivot_block - me) % lon]).astype(jnp.int32)
-    source = lax.broadcasted_iota(jnp.int32, (span, span), 0)
-    target = lax.broadcasted_iota(jnp.int32, (span, span), 1)
-    reverse = jnp.stack(
-        [source == span + pivot_offset - target, source == pivot_offset - target]
-    ).astype(jnp.float32)
-    return fused(state, blocks, reverse)
+            seawater_indicator,
+            submerged_layer_total,
+        ),
+        seam_partner_index,
+    )
 
 
 def solution(mesh):

time: 88 us -> 70 us (0.80)
  Pallas kernels: 72.9 us -> 66.4 us
  local copies, waits for them, and re-layouts: 9.02 us -> 2.8 us
  between operations: 3.39 us -> 0.65 us
  other arithmetic: 2.25 us -> 0 us
    pallas_call x1, Pallas kernels: 72.9 us -> 66.4 us  [fused(): pl.pallas_call(functools.partial(fused_kernel, lon, lat, STATE_SIGNS), ou...]
    unnamed x14 -> x4, local copies, waits for them, and re-layouts: 7.73 us -> 2.8 us
    slice x1 -> x0, local copies, waits for them, and re-layouts: 1.29 us -> none  [local(): pivot = seam_partner_index[0]]
where the time goes in v4:
time: 70 us; the launch traced here: 69.9 us
  Pallas kernels  66.4 us (95%)
  local copies, waits for them, and re-layouts  2.8 us (4%)
    pallas_call x1, Pallas kernels, fused(): pl.pallas_call(functools.partial(fused_kernel, lon, lat, STATE_SIGNS), ou...  66.4 us
    unnamed x4, local copies, waits for them, and re-layouts  2.8 us

profile of v4, /device:TPU:32, one launch (start us, length us, event | category | flops | bytes accessed | tf_op | source)
XLA Modules:
  0.0 69.9 jit_solution(3611390989556474814)
XLA Ops:
  0.6 66.4 %shard_map.86 = (f32[12,96,128]{2,1,0:T(8,128)}, f32[12,96,128]{2,1,0:T(8,128)}) custom-call(s32[2048]{0:T(1024)} %seam.1, f32[12,96,128]{2,1,0:T(8,128)} %heat.1, f32[12,96,128]{2,1,0:T(8,128)} %salt.1, f32[12,96,128]{2,1,0:T(8,128)} %zonal.1, f32[12,96,128]{2,1,0:T(8,128)} %meridional.1, s32[96,128]{1,0:T(8,128)} %sea.1, s32[96,128]{1,0:T(8,128)} %depth.1), custom_call_target="tpu_custom_call" | custom-call | tf_op jit(solution)/shard_map/pallas_call | solution.py:460
  67.1 0.0 copy-start
  67.1 2.0 %copy.11 = f32[12,96,128]{2,1,0:T(8,128)} copy(f32[12,96,128]{2,1,0:T(8,128)} %get-tuple-element.4) | data formatting | bytes 1179648
  69.0 0.0 copy-done
  69.0 0.8 %copy.12 = f32[12,96,128]{2,1,0:T(8,128)} copy(f32[12,96,128]{2,1,0:T(8,128)S(1)} %copy-done) | data formatting | bytes 1179648
Async XLA Ops:
  67.1 2.0 %copy-start = (f32[12,96,128]{2,1,0:T(8,128)S(1)}, f32[12,96,128]{2,1,0:T(8,128)}, u32[]{:S(2)}) copy-start(f32[12,96,128]{2,1,0:T(8,128)} %get-tuple-element.5) | copy-start | bytes 1769476

commit v5 on v4

--- a/solution.py
+++ b/solution.py
@@ -132,8 +132,12 @@
     levels = out.shape[1]
 
     def body(k, carry):
+        zonal = sides_of(state_refs, 2, k)
+        meridional = sides_of(state_refs, 3, k)
+        wet_sides = sides_of(state_refs, 4, k)
         for tracer in range(2):
-            (upwind, anti, inflow, outflow), _ = level_low_order(state_refs, k, tracer)
+            tracer_sides = sides_of(state_refs, tracer, k)
+            upwind, anti, inflow, outflow = low_order(tracer_sides, zonal, meridional, wet_sides)
             out[tracer, k] = upwind
             for face in range(4):
                 anti_out[4 * tracer + face, k] = anti[face]
@@ -300,7 +304,7 @@
     barrier = pltpu.get_barrier_semaphore()
     for peer in range(lon):
 
-        @pl.when(me != peer)
+        @pl.when((me != peer) & (on_top | (peer == west) | (peer == east)))
         def _():
             pl.semaphore_signal(barrier, 1, device_id={"lon": peer}, device_id_type=mesh)
 
@@ -312,8 +316,12 @@
     def _():
         pl.semaphore_signal(barrier, 1, device_id={"lat": row + 1}, device_id_type=mesh)
 
+    beside = 1 if lon == 2 else 2
     pl.semaphore_wait(
-        barrier, lon - 1 + has_south.astype(jnp.int32) + has_north.astype(jnp.int32)
+        barrier,
+        jnp.where(on_top, lon - 1, beside)
+        + has_south.astype(jnp.int32)
+        + has_north.astype(jnp.int32),
     )
 
     def exchange(s, source):
@@ -344,12 +352,6 @@
                 device_id_type=mesh,
             )
 
-        for peer in range(lon):
-
-            @pl.when(me != peer)
-            def _():
-                fold_copy(peer, me).start()
-
         def side(i, src, dst, device):
             return pltpu.make_async_remote_copy(
                 src_ref=src,
@@ -375,11 +377,19 @@
         def _():
             to_north.start()
 
-        gathered[me] = nsend[...]
-
         for peer in range(lon):
 
-            @pl.when(me != peer)
+            @pl.when((me != peer) & on_top)
+            def _():
+                fold_copy(peer, me).start()
+
+        @pl.when(on_top)
+        def _():
+            gathered[me] = nsend[...]
+
+        for peer in range(lon):
+
+            @pl.when((me != peer) & on_top)
             def _():
                 fold_copy(peer, me).wait_send()
                 fold_copy(peer, peer).wait_recv()
@@ -410,19 +420,26 @@
             for k in range(levels):
                 wcol[f, k] = both[:, k : k + 1]
                 ecol[f, k] = both[:, 16 + k : 17 + k]
-            ghost = jnp.dot(
-                gathered[lower, f],
-                reverse[0],
-                precision=lax.Precision.HIGHEST,
-                preferred_element_type=jnp.float32,
-            ) + jnp.dot(
-                gathered[upper, f],
-                reverse[1],
-                precision=lax.Precision.HIGHEST,
-                preferred_element_type=jnp.float32,
-            )
             sign = signs[f] if s == 0 else 1.0
-            north[f] = jnp.where(on_top, ghost * sign, nhalo[f])
+
+            @pl.when(on_top)
+            def _():
+                ghost = jnp.dot(
+                    gathered[lower, f],
+                    reverse[0],
+                    precision=lax.Precision.HIGHEST,
+                    preferred_element_type=jnp.float32,
+                ) + jnp.dot(
+                    gathered[upper, f],
+                    reverse[1],
+                    precision=lax.Precision.HIGHEST,
+                    preferred_element_type=jnp.float32,
+                )
+                north[f] = ghost * sign
+
+            @pl.when(jnp.logical_not(on_top))
+            def _():
+                north[f] = nhalo[f]
         return (source, wcol, ecol, shalo, north)
 
     state_refs = exchange(0, state)

time: 70 us -> 69.6 us (level)
  the two profiles are of different devices: /device:TPU:32 before, /device:TPU:113 now
where the time goes in v5:
time: 69.6 us; the launch traced here: 69.4 us
  Pallas kernels  66 us (95%)
  local copies, waits for them, and re-layouts  2.8 us (4%)
    pallas_call x1, Pallas kernels, fused(): pl.pallas_call(functools.partial(fused_kernel, lon, lat, STATE_SIGNS), ou...  66 us
    unnamed x4, local copies, waits for them, and re-layouts  2.8 us

profile of v5, /device:TPU:113, one launch (start us, length us, event | category | flops | bytes accessed | tf_op | source)
XLA Modules:
  0.0 69.4 jit_solution(9138718507642915223)
XLA Ops:
  0.6 66.0 %shard_map.86 = (f32[12,96,128]{2,1,0:T(8,128)}, f32[12,96,128]{2,1,0:T(8,128)}) custom-call(s32[2048]{0:T(1024)} %seam.1, f32[12,96,128]{2,1,0:T(8,128)} %heat.1, f32[12,96,128]{2,1,0:T(8,128)} %salt.1, f32[12,96,128]{2,1,0:T(8,128)} %zonal.1, f32[12,96,128]{2,1,0:T(8,128)} %meridional.1, s32[96,128]{1,0:T(8,128)} %sea.1, s32[96,128]{1,0:T(8,128)} %depth.1), custom_call_target="tpu_custom_call" | custom-call | tf_op jit(solution)/shard_map/pallas_call | solution.py:477
  66.6 0.0 copy-start
  66.6 2.0 %copy.11 = f32[12,96,128]{2,1,0:T(8,128)} copy(f32[12,96,128]{2,1,0:T(8,128)} %get-tuple-element.4) | data formatting | bytes 1179648
  68.6 0.0 copy-done
  68.6 0.8 %copy.12 = f32[12,96,128]{2,1,0:T(8,128)} copy(f32[12,96,128]{2,1,0:T(8,128)S(1)} %copy-done) | data formatting | bytes 1179648
Async XLA Ops:
  66.6 2.0 %copy-start = (f32[12,96,128]{2,1,0:T(8,128)S(1)}, f32[12,96,128]{2,1,0:T(8,128)}, u32[]{:S(2)}) copy-start(f32[12,96,128]{2,1,0:T(8,128)} %get-tuple-element.5) | copy-start | bytes 1769476

commit v6 on v5

--- a/solution.py
+++ b/solution.py
@@ -31,11 +31,32 @@
     return (x, at_east, at_west, at_north, at_south)
 
 
-def sides_of(refs, f, k):
+def around_top(pair, west, east, north):
+    x = pair[1:2]
+    width = x.shape[1]
+    lane = lax.broadcasted_iota(jnp.int32, x.shape, 1)
+    at_east = jnp.where(lane == width - 1, east, pltpu.roll(x, width - 1, 1))
+    at_west = jnp.where(lane == 0, west, pltpu.roll(x, 1, 1))
+    return (x, at_east, at_west, north, pair[0:1])
+
+
+def sides_of(refs, f, k, top=False):
     block, west, east, south, north = refs
+    if top:
+        height = west.shape[2]
+        return around_top(
+            block[f, k, pl.ds(height - 2, 2), :],
+            west[f, k, pl.ds(height - 1, 1), :],
+            east[f, k, pl.ds(height - 1, 1), :],
+            north[f, pl.ds(k, 1), :],
+        )
     return around(
         block[f, k], west[f, k], east[f, k], south[f, pl.ds(k, 1), :], north[f, pl.ds(k, 1), :]
     )
+
+
+def tail_of(shape, top):
+    return (pl.ds(shape[-2] - 1, 1), slice(None)) if top else ()
 
 
 def low_order(tracer, zonal, meridional, wet_sides):
@@ -128,67 +149,75 @@
     )
 
 
-def upwind_kernel(state_refs, out, anti_out, flow_out):
+def upwind_kernel(state_refs, out, anti_out, flow_out, top=False):
     levels = out.shape[1]
+    tail = tail_of(out.shape, top)
 
     def body(k, carry):
-        zonal = sides_of(state_refs, 2, k)
-        meridional = sides_of(state_refs, 3, k)
-        wet_sides = sides_of(state_refs, 4, k)
+        zonal = sides_of(state_refs, 2, k, top)
+        meridional = sides_of(state_refs, 3, k, top)
+        wet_sides = sides_of(state_refs, 4, k, top)
         for tracer in range(2):
-            tracer_sides = sides_of(state_refs, tracer, k)
+            tracer_sides = sides_of(state_refs, tracer, k, top)
             upwind, anti, inflow, outflow = low_order(tracer_sides, zonal, meridional, wet_sides)
-            out[tracer, k] = upwind
+            out[(tracer, k) + tail] = upwind
             for face in range(4):
-                anti_out[4 * tracer + face, k] = anti[face]
-            flow_out[tracer, k] = inflow
-            flow_out[2 + tracer, k] = outflow
+                anti_out[(4 * tracer + face, k) + tail] = anti[face]
+            flow_out[(tracer, k) + tail] = inflow
+            flow_out[(2 + tracer, k) + tail] = outflow
         return carry
 
     lax.fori_loop(0, levels, body, 0)
 
 
-def ratio_kernel(state_refs, upwind_refs, flow, out):
+def ratio_kernel(state_refs, upwind_refs, flow, out, top=False):
     levels = out.shape[1]
+    tail = tail_of(out.shape, top)
 
     def body(k, carry):
-        wet_sides = sides_of(state_refs, 4, k)
+        wet_sides = sides_of(state_refs, 4, k, top)
         for tracer in range(2):
             plus, minus = ratio_pair(
-                sides_of(upwind_refs, tracer, k), wet_sides, flow[tracer, k], flow[2 + tracer, k]
+                sides_of(upwind_refs, tracer, k, top),
+                wet_sides,
+                flow[(tracer, k) + tail],
+                flow[(2 + tracer, k) + tail],
             )
-            out[tracer, k] = plus
-            out[2 + tracer, k] = minus
+            out[(tracer, k) + tail] = plus
+            out[(2 + tracer, k) + tail] = minus
         return carry
 
     lax.fori_loop(0, levels, body, 0)
 
 
-def advected_kernel(wet, upwind_ref, anti_ref, ratio_refs, out):
+def advected_kernel(wet, upwind_ref, anti_ref, ratio_refs, out, top=False):
     levels = out.shape[1]
+    tail = tail_of(out.shape, top)
 
     def body(k, carry):
-        wet_centre = wet[k]
+        wet_centre = wet[(k,) + tail]
         for tracer in range(2):
-            anti = tuple(anti_ref[4 * tracer + face, k] for face in range(4))
-            plus = sides_of(ratio_refs, tracer, k)
-            minus = sides_of(ratio_refs, 2 + tracer, k)
-            out[tracer, k] = limited(plus, minus, upwind_ref[tracer, k], anti, wet_centre)
+            anti = tuple(anti_ref[(4 * tracer + face, k) + tail] for face in range(4))
+            plus = sides_of(ratio_refs, tracer, k, top)
+            minus = sides_of(ratio_refs, 2 + tracer, k, top)
+            out[(tracer, k) + tail] = limited(
+                plus, minus, upwind_ref[(tracer, k) + tail], anti, wet_centre
+            )
         return carry
 
     lax.fori_loop(0, levels, body, 0)
 
 
-def isopycnal_kernel(*refs):
-    advected_refs, state_refs, out = refs[:5], refs[5:10], refs[10]
+def isopycnal_kernel(advected_refs, state_refs, out, top=False):
     levels = out.shape[1]
+    tail = tail_of(out.shape, top)
 
     def body(k, carry):
         above = jnp.minimum(k + 1, levels - 1)
-        values = [sides_of(advected_refs, tracer, k) for tracer in range(2)]
-        uppers = [sides_of(advected_refs, tracer, above) for tracer in range(2)]
-        wet_sides = sides_of(state_refs, 4, k)
-        wet_above = sides_of(state_refs, 4, above)
+        values = [sides_of(advected_refs, tracer, k, top) for tracer in range(2)]
+        uppers = [sides_of(advected_refs, tracer, above, top) for tracer in range(2)]
+        wet_sides = sides_of(state_refs, 4, k, top)
+        wet_above = sides_of(state_refs, 4, above, top)
         stacked = [w * a for w, a in zip(wet_sides, wet_above)]
         verticals = [
             [(u - v) * s for u, v, s in zip(uppers[tracer], values[tracer], stacked)]
@@ -221,7 +250,7 @@
             west_flux = face_flux(2, 0)
             north_flux = face_flux(0, 3)
             south_flux = face_flux(4, 0)
-            out[tracer, k] = value[0] + wet_sides[0] * (
+            out[(tracer, k) + tail] = value[0] + wet_sides[0] * (
                 east_flux - west_flux + north_flux - south_flux
             )
         return carry
@@ -244,7 +273,7 @@
         self.shape = (2,) + first.shape
 
     def __setitem__(self, index, value):
-        self.refs[index[0]][index[1]] = value
+        self.refs[index[0]][index[1:]] = value
 
 
 def buffers_for(fields, levels, height, width, lon):
@@ -387,13 +416,6 @@
         def _():
             gathered[me] = nsend[...]
 
-        for peer in range(lon):
-
-            @pl.when((me != peer) & on_top)
-            def _():
-                fold_copy(peer, me).wait_send()
-                fold_copy(peer, peer).wait_recv()
-
         to_west.wait()
         to_east.wait()
 
@@ -420,36 +442,48 @@
             for k in range(levels):
                 wcol[f, k] = both[:, k : k + 1]
                 ecol[f, k] = both[:, 16 + k : 17 + k]
-            sign = signs[f] if s == 0 else 1.0
+            north[f] = nhalo[f]
+
+        def finish():
+            for peer in range(lon):
+
+                @pl.when((me != peer) & on_top)
+                def _():
+                    fold_copy(peer, me).wait_send()
+                    fold_copy(peer, peer).wait_recv()
 
             @pl.when(on_top)
             def _():
-                ghost = jnp.dot(
-                    gathered[lower, f],
-                    reverse[0],
-                    precision=lax.Precision.HIGHEST,
-                    preferred_element_type=jnp.float32,
-                ) + jnp.dot(
-                    gathered[upper, f],
-                    reverse[1],
-                    precision=lax.Precision.HIGHEST,
-                    preferred_element_type=jnp.float32,
-                )
-                north[f] = ghost * sign
-
-            @pl.when(jnp.logical_not(on_top))
-            def _():
-                north[f] = nhalo[f]
-        return (source, wcol, ecol, shalo, north)
-
-    state_refs = exchange(0, state)
-    upwind_kernel(state_refs, upwind, anti, flow)
-    upwind_refs = exchange(1, upwind)
-    ratio_kernel(state_refs, upwind_refs, flow, ratio)
-    ratio_refs = exchange(2, ratio)
-    advected_kernel(wet, upwind, anti, ratio_refs, advected)
-    advected_refs = exchange(3, advected)
-    isopycnal_kernel(*advected_refs, *state_refs, Pair(first_out, second_out))
+                for f in range(fields):
+                    ghost = jnp.dot(
+                        gathered[lower, f],
+                        reverse[0],
+                        precision=lax.Precision.HIGHEST,
+                        preferred_element_type=jnp.float32,
+                    ) + jnp.dot(
+                        gathered[upper, f],
+                        reverse[1],
+                        precision=lax.Precision.HIGHEST,
+                        preferred_element_type=jnp.float32,
+                    )
+                    north[f] = ghost * (signs[f] if s == 0 else 1.0)
+
+        return (source, wcol, ecol, shalo, north), finish
+
+    def run(stage, finish):
+        stage(False)
+        finish()
+        pl.when(on_top)(lambda: stage(True))
+
+    state_refs, finish = exchange(0, state)
+    run(lambda top: upwind_kernel(state_refs, upwind, anti, flow, top), finish)
+    upwind_refs, finish = exchange(1, upwind)
+    run(lambda top: ratio_kernel(state_refs, upwind_refs, flow, ratio, top), finish)
+    ratio_refs, finish = exchange(2, ratio)
+    run(lambda top: advected_kernel(wet, upwind, anti, ratio_refs, advected, top), finish)
+    advected_refs, finish = exchange(3, advected)
+    final = Pair(first_out, second_out)
+    run(lambda top: isopycnal_kernel(advected_refs, state_refs, final, top), finish)
 
 
 def fused(fields, seam):

time: 69.6 us -> 64 us (0.920)
  Pallas kernels: 66 us -> 60.4 us
    pallas_call x1, Pallas kernels: 66 us -> 60.4 us  [fused(): pl.pallas_call(functools.partial(fused_kernel, lon, lat, STATE_SIGNS), ou...]
where the time goes in v6:
time: 64 us; the launch traced here: 63.8 us
  Pallas kernels  60.4 us (94%)
  local copies, waits for them, and re-layouts  2.8 us (4%)
  between operations  0.65 us (1%)
    pallas_call x1, Pallas kernels, fused(): pl.pallas_call(functools.partial(fused_kernel, lon, lat, STATE_SIGNS), ou...  60.4 us
    unnamed x4, local copies, waits for them, and re-layouts  2.8 us

profile of v6, /device:TPU:113, one launch (start us, length us, event | category | flops | bytes accessed | tf_op | source)
XLA Modules:
  0.0 63.8 jit_solution(16207167913806823001)
XLA Ops:
  0.6 60.4 %shard_map.86 = (f32[12,96,128]{2,1,0:T(8,128)}, f32[12,96,128]{2,1,0:T(8,128)}) custom-call(s32[2048]{0:T(1024)} %seam.1, f32[12,96,128]{2,1,0:T(8,128)} %heat.1, f32[12,96,128]{2,1,0:T(8,128)} %salt.1, f32[12,96,128]{2,1,0:T(8,128)} %zonal.1, f32[12,96,128]{2,1,0:T(8,128)} %meridional.1, s32[96,128]{1,0:T(8,128)} %sea.1, s32[96,128]{1,0:T(8,128)} %depth.1), custom_call_target="tpu_custom_call" | custom-call | tf_op jit(solution)/shard_map/pallas_call | solution.py:511
  61.0 0.0 copy-start
  61.0 2.0 %copy.11 = f32[12,96,128]{2,1,0:T(8,128)} copy(f32[12,96,128]{2,1,0:T(8,128)} %get-tuple-element.4) | data formatting | bytes 1179648
  63.0 0.0 copy-done
  63.0 0.8 %copy.12 = f32[12,96,128]{2,1,0:T(8,128)} copy(f32[12,96,128]{2,1,0:T(8,128)S(1)} %copy-done) | data formatting | bytes 1179648
Async XLA Ops:
  61.0 2.0 %copy-start = (f32[12,96,128]{2,1,0:T(8,128)S(1)}, f32[12,96,128]{2,1,0:T(8,128)}, u32[]{:S(2)}) copy-start(f32[12,96,128]{2,1,0:T(8,128)} %get-tuple-element.5) | copy-start | bytes 1769476

commit v7 on v6

--- a/solution.py
+++ b/solution.py
@@ -31,32 +31,48 @@
     return (x, at_east, at_west, at_north, at_south)
 
 
-def around_top(pair, west, east, north):
-    x = pair[1:2]
-    width = x.shape[1]
-    lane = lax.broadcasted_iota(jnp.int32, x.shape, 1)
-    at_east = jnp.where(lane == width - 1, east, pltpu.roll(x, width - 1, 1))
-    at_west = jnp.where(lane == 0, west, pltpu.roll(x, 1, 1))
-    return (x, at_east, at_west, north, pair[0:1])
-
-
-def sides_of(refs, f, k, top=False):
+def pick_rows(low, high):
+    level = lax.broadcasted_iota(jnp.int32, (2, high.shape[-1]), 0)
+    return jnp.where(level == 0, low, high)
+
+
+def load_view(ref, index, rows):
+    if not rows:
+        return ref[index]
+    height = ref.shape[-2]
+    return pick_rows(
+        ref[index + (pl.ds(0, 1), slice(None))], ref[index + (pl.ds(height - 1, 1), slice(None))]
+    )
+
+
+def store_view(ref, index, value, rows):
+    if not rows:
+        ref[index] = value
+        return
+    height = ref.shape[-2]
+    ref[index + (pl.ds(0, 1), slice(None))] = value[0:1]
+    ref[index + (pl.ds(height - 1, 1), slice(None))] = value[1:2]
+
+
+def sides_of(refs, f, k, rows=False):
     block, west, east, south, north = refs
-    if top:
-        height = west.shape[2]
-        return around_top(
-            block[f, k, pl.ds(height - 2, 2), :],
-            west[f, k, pl.ds(height - 1, 1), :],
-            east[f, k, pl.ds(height - 1, 1), :],
-            north[f, pl.ds(k, 1), :],
+    if not rows:
+        return around(
+            block[f, k], west[f, k], east[f, k], south[f, pl.ds(k, 1), :], north[f, pl.ds(k, 1), :]
         )
-    return around(
-        block[f, k], west[f, k], east[f, k], south[f, pl.ds(k, 1), :], north[f, pl.ds(k, 1), :]
-    )
-
-
-def tail_of(shape, top):
-    return (pl.ds(shape[-2] - 1, 1), slice(None)) if top else ()
+    height = west.shape[2]
+    low = block[f, k, pl.ds(0, 2), :]
+    high = block[f, k, pl.ds(height - 2, 2), :]
+    centre = pick_rows(low[0:1], high[1:2])
+    at_north = pick_rows(low[1:2], north[f, pl.ds(k, 1), :])
+    at_south = pick_rows(south[f, pl.ds(k, 1), :], high[0:1])
+    west_end = pick_rows(west[f, k, pl.ds(0, 1), :], west[f, k, pl.ds(height - 1, 1), :])
+    east_end = pick_rows(east[f, k, pl.ds(0, 1), :], east[f, k, pl.ds(height - 1, 1), :])
+    width = centre.shape[1]
+    lane = lax.broadcasted_iota(jnp.int32, centre.shape, 1)
+    at_east = jnp.where(lane == width - 1, east_end, pltpu.roll(centre, width - 1, 1))
+    at_west = jnp.where(lane == 0, west_end, pltpu.roll(centre, 1, 1))
+    return (centre, at_east, at_west, at_north, at_south)
 
 
 def low_order(tracer, zonal, meridional, wet_sides):
@@ -149,75 +165,70 @@
     )
 
 
-def upwind_kernel(state_refs, out, anti_out, flow_out, top=False):
+def upwind_kernel(state_refs, out, anti_out, flow_out, rows=False):
     levels = out.shape[1]
-    tail = tail_of(out.shape, top)
 
     def body(k, carry):
-        zonal = sides_of(state_refs, 2, k, top)
-        meridional = sides_of(state_refs, 3, k, top)
-        wet_sides = sides_of(state_refs, 4, k, top)
+        zonal = sides_of(state_refs, 2, k, rows)
+        meridional = sides_of(state_refs, 3, k, rows)
+        wet_sides = sides_of(state_refs, 4, k, rows)
         for tracer in range(2):
-            tracer_sides = sides_of(state_refs, tracer, k, top)
+            tracer_sides = sides_of(state_refs, tracer, k, rows)
             upwind, anti, inflow, outflow = low_order(tracer_sides, zonal, meridional, wet_sides)
-            out[(tracer, k) + tail] = upwind
+            store_view(out, (tracer, k), upwind, rows)
             for face in range(4):
-                anti_out[(4 * tracer + face, k) + tail] = anti[face]
-            flow_out[(tracer, k) + tail] = inflow
-            flow_out[(2 + tracer, k) + tail] = outflow
+                store_view(anti_out, (4 * tracer + face, k), anti[face], rows)
+            store_view(flow_out, (tracer, k), inflow, rows)
+            store_view(flow_out, (2 + tracer, k), outflow, rows)
         return carry
 
     lax.fori_loop(0, levels, body, 0)
 
 
-def ratio_kernel(state_refs, upwind_refs, flow, out, top=False):
+def ratio_kernel(state_refs, upwind_refs, flow, out, rows=False):
     levels = out.shape[1]
-    tail = tail_of(out.shape, top)
 
     def body(k, carry):
-        wet_sides = sides_of(state_refs, 4, k, top)
+        wet_sides = sides_of(state_refs, 4, k, rows)
         for tracer in range(2):
             plus, minus = ratio_pair(
-                sides_of(upwind_refs, tracer, k, top),
+                sides_of(upwind_refs, tracer, k, rows),
                 wet_sides,
-                flow[(tracer, k) + tail],
-                flow[(2 + tracer, k) + tail],
+                load_view(flow, (tracer, k), rows),
+                load_view(flow, (2 + tracer, k), rows),
             )
-            out[(tracer, k) + tail] = plus
-            out[(2 + tracer, k) + tail] = minus
+            store_view(out, (tracer, k), plus, rows)
+            store_view(out, (2 + tracer, k), minus, rows)
         return carry
 
     lax.fori_loop(0, levels, body, 0)
 
 
-def advected_kernel(wet, upwind_ref, anti_ref, ratio_refs, out, top=False):
+def advected_kernel(wet, upwind_ref, anti_ref, ratio_refs, out, rows=False):
     levels = out.shape[1]
-    tail = tail_of(out.shape, top)
 
     def body(k, carry):
-        wet_centre = wet[(k,) + tail]
+        wet_centre = load_view(wet, (k,), rows)
         for tracer in range(2):
-            anti = tuple(anti_ref[(4 * tracer + face, k) + tail] for face in range(4))
-            plus = sides_of(ratio_refs, tracer, k, top)
-            minus = sides_of(ratio_refs, 2 + tracer, k, top)
-            out[(tracer, k) + tail] = limited(
-                plus, minus, upwind_ref[(tracer, k) + tail], anti, wet_centre
-            )
+            anti = tuple(load_view(anti_ref, (4 * tracer + face, k), rows) for face in range(4))
+            plus = sides_of(ratio_refs, tracer, k, rows)
+            minus = sides_of(ratio_refs, 2 + tracer, k, rows)
+            upwind = load_view(upwind_ref, (tracer, k), rows)
+            store_view(out, (tracer, k), limited(plus, minus, upwind, anti, wet_centre), rows)
         return carry
 
     lax.fori_loop(0, levels, body, 0)
 
 
-def isopycnal_kernel(advected_refs, state_refs, out, top=False):
+def isopycnal_kernel(advected_refs, state_refs, out, rows=False):
     levels = out.shape[1]
-    tail = tail_of(out.shape, top)
 
     def body(k, carry):
         above = jnp.minimum(k + 1, levels - 1)
-        values = [sides_of(advected_refs, tracer, k, top) for tracer in range(2)]
-        uppers = [sides_of(advected_refs, tracer, above, top) for tracer in range(2)]
-        wet_sides = sides_of(state_refs, 4, k, top)
-        wet_above = sides_of(state_refs, 4, above, top)
+        values = [sides_of(advected_refs, tracer, k, rows) for tracer in range(2)]
+        uppers = [sides_of(advected_refs, tracer, above, rows) for tracer in range(2)]
+        wet_sides = sides_of(state_refs, 4, k, rows)
+        wet_above = sides_of(state_refs, 4, above, rows)
         stacked = [w * a for w, a in zip(wet_sides, wet_above)]
         verticals = [
             [(u - v) * s for u, v, s in zip(uppers[tracer], values[tracer], stacked)]
@@ -250,9 +261,8 @@
             west_flux = face_flux(2, 0)
             north_flux = face_flux(0, 3)
             south_flux = face_flux(4, 0)
-            out[(tracer, k) + tail] = value[0] + wet_sides[0] * (
-                east_flux - west_flux + north_flux - south_flux
-            )
+            result = value[0] + wet_sides[0] * (east_flux - west_flux + north_flux - south_flux)
+            store_view(out, (tracer, k), result, rows)
         return carry
 
     lax.fori_loop(0, levels, body, 0)
@@ -419,32 +429,35 @@
         to_west.wait()
         to_east.wait()
 
-        @pl.when(has_south)
-        def _():
-            to_south.wait_send()
-            to_north.wait_recv()
-
-        @pl.when(has_north)
-        def _():
-            to_north.wait_send()
-            to_south.wait_recv()
-
-        @pl.when(jnp.logical_not(has_south))
-        def _():
-            shalo[...] = jnp.zeros_like(shalo)
-
-        @pl.when(jnp.logical_not(has_north))
-        def _():
-            nhalo[...] = jnp.zeros_like(nhalo)
-
         for f in range(fields):
             both = jnp.concatenate([whalo[f], ehalo[f]], axis=0).T
             for k in range(levels):
                 wcol[f, k] = both[:, k : k + 1]
                 ecol[f, k] = both[:, 16 + k : 17 + k]
-            north[f] = nhalo[f]
 
         def finish():
+            @pl.when(has_south)
+            def _():
+                to_south.wait_send()
+                to_north.wait_recv()
+
+            @pl.when(has_north)
+            def _():
+                to_north.wait_send()
+                to_south.wait_recv()
+
+            @pl.when(jnp.logical_not(has_south))
+            def _():
+                shalo[...] = jnp.zeros_like(shalo)
+
+            @pl.when(jnp.logical_not(has_north))
+            def _():
+                nhalo[...] = jnp.zeros_like(nhalo)
+
+            @pl.when(jnp.logical_not(on_top))
+            def _():
+                north[...] = nhalo[...]
+
             for peer in range(lon):
 
                 @pl.when((me != peer) & on_top)
@@ -468,22 +481,40 @@
                     )
                     north[f] = ghost * (signs[f] if s == 0 else 1.0)
 
-        return (source, wcol, ecol, shalo, north), finish
+        return (source, wcol, ecol, ssend, nsend), (source, wcol, ecol, shalo, north), finish
 
     def run(stage, finish):
         stage(False)
         finish()
-        pl.when(on_top)(lambda: stage(True))
-
-    state_refs, finish = exchange(0, state)
-    run(lambda top: upwind_kernel(state_refs, upwind, anti, flow, top), finish)
-    upwind_refs, finish = exchange(1, upwind)
-    run(lambda top: ratio_kernel(state_refs, upwind_refs, flow, ratio, top), finish)
-    ratio_refs, finish = exchange(2, ratio)
-    run(lambda top: advected_kernel(wet, upwind, anti, ratio_refs, advected, top), finish)
-    advected_refs, finish = exchange(3, advected)
+        stage(True)
+
+    state_early, state_refs, finish = exchange(0, state)
+    run(
+        lambda rows: upwind_kernel(state_refs if rows else state_early, upwind, anti, flow, rows),
+        finish,
+    )
+    upwind_early, upwind_refs, finish = exchange(1, upwind)
+    run(
+        lambda rows: ratio_kernel(
+            state_refs, upwind_refs if rows else upwind_early, flow, ratio, rows
+        ),
+        finish,
+    )
+    ratio_early, ratio_refs, finish = exchange(2, ratio)
+    run(
+        lambda rows: advected_kernel(
+            wet, upwind, anti, ratio_refs if rows else ratio_early, advected, rows
+        ),
+        finish,
+    )
+    advected_early, advected_refs, finish = exchange(3, advected)
     final = Pair(first_out, second_out)
-    run(lambda top: isopycnal_kernel(advected_refs, state_refs, final, top), finish)
+    run(
+        lambda rows: isopycnal_kernel(
+            advected_refs if rows else advected_early, state_refs, final, rows
+        ),
+        finish,
+    )
 
 
 def fused(fields, seam):

time: 64 us -> 61.8 us (0.966)
  Pallas kernels: 60.4 us -> 58.2 us
    pallas_call x1, Pallas kernels: 60.4 us -> 58.2 us  [fused(): pl.pallas_call(functools.partial(fused_kernel, lon, lat, STATE_SIGNS), ou...]
where the time goes in v7:
time: 61.8 us; the launch traced here: 61.6 us
  Pallas kernels  58.2 us (94%)
  local copies, waits for them, and re-layouts  2.8 us (5%)
  between operations  0.65 us (1%)
    pallas_call x1, Pallas kernels, fused(): pl.pallas_call(functools.partial(fused_kernel, lon, lat, STATE_SIGNS), ou...  58.2 us
    unnamed x4, local copies, waits for them, and re-layouts  2.8 us

profile of v7, /device:TPU:113, one launch (start us, length us, event | category | flops | bytes accessed | tf_op | source)
XLA Modules:
  0.0 61.6 jit_solution(17313325804829538777)
XLA Ops:
  0.6 58.2 %shard_map.86 = (f32[12,96,128]{2,1,0:T(8,128)}, f32[12,96,128]{2,1,0:T(8,128)}) custom-call(s32[2048]{0:T(1024)} %seam.1, f32[12,96,128]{2,1,0:T(8,128)} %heat.1, f32[12,96,128]{2,1,0:T(8,128)} %salt.1, f32[12,96,128]{2,1,0:T(8,128)} %zonal.1, f32[12,96,128]{2,1,0:T(8,128)} %meridional.1, s32[96,128]{1,0:T(8,128)} %sea.1, s32[96,128]{1,0:T(8,128)} %depth.1), custom_call_target="tpu_custom_call" | custom-call | tf_op jit(solution)/shard_map/pallas_call | solution.py:542
  58.8 0.0 copy-start
  58.8 2.0 %copy.11 = f32[12,96,128]{2,1,0:T(8,128)} copy(f32[12,96,128]{2,1,0:T(8,128)} %get-tuple-element.4) | data formatting | bytes 1179648
  60.8 0.0 copy-done
  60.8 0.8 %copy.12 = f32[12,96,128]{2,1,0:T(8,128)} copy(f32[12,96,128]{2,1,0:T(8,128)S(1)} %copy-done) | data formatting | bytes 1179648
Async XLA Ops:
  58.8 2.0 %copy-start = (f32[12,96,128]{2,1,0:T(8,128)S(1)}, f32[12,96,128]{2,1,0:T(8,128)}, u32[]{:S(2)}) copy-start(f32[12,96,128]{2,1,0:T(8,128)} %get-tuple-element.5) | copy-start | bytes 1769476

commit v8 on v7

--- a/solution.py
+++ b/solution.py
@@ -368,18 +368,17 @@
             per_stage[s]
         )
         fields = source.shape[0]
-        lane = lax.broadcasted_iota(jnp.int32, (height, width), 1)
         for f in range(fields):
-            packed = jnp.zeros((height, width), jnp.float32)
             for k in range(levels):
                 tile = source[f, k]
-                packed = jnp.where(lane == k, tile[:, 0:1], packed)
-                packed = jnp.where(lane == 16 + k, tile[:, width - 1 : width], packed)
+                flipped = tile.T
+                wsend[f, pl.ds(k, 1), :] = flipped[0:1, :]
+                esend[f, pl.ds(k, 1), :] = flipped[width - 1 : width, :]
                 ssend[f, pl.ds(k, 1), :] = tile[0:1, :]
                 nsend[f, pl.ds(k, 1), :] = tile[height - 1 : height, :]
-            flipped = packed.T
-            wsend[f] = flipped[0:16, :]
-            esend[f] = flipped[16:32, :]
+            spare = wsend.shape[1] - levels
+            wsend[f, pl.ds(levels, spare), :] = jnp.zeros((spare, height), jnp.float32)
+            esend[f, pl.ds(levels, spare), :] = jnp.zeros((spare, height), jnp.float32)
 
         def fold_copy(peer, slot):
             return pltpu.make_async_remote_copy(

time: 61.8 us -> 59.2 us (0.958)
  Pallas kernels: 58.2 us -> 55.2 us
    pallas_call x1, Pallas kernels: 58.2 us -> 55.2 us  [fused(): pl.pallas_call(functools.partial(fused_kernel, lon, lat, STATE_SIGNS), ou...]
where the time goes in v8:
time: 59.2 us; the launch traced here: 58.7 us
  Pallas kernels  55.2 us (93%)
  local copies, waits for them, and re-layouts  2.8 us (5%)
  between operations  0.65 us (1%)
    pallas_call x1, Pallas kernels, fused(): pl.pallas_call(functools.partial(fused_kernel, lon, lat, STATE_SIGNS), ou...  55.2 us
    unnamed x4, local copies, waits for them, and re-layouts  2.8 us

profile of v8, /device:TPU:113, one launch (start us, length us, event | category | flops | bytes accessed | tf_op | source)
XLA Modules:
  0.0 58.7 jit_solution(2211519361688595231)
XLA Ops:
  0.6 55.2 %shard_map.86 = (f32[12,96,128]{2,1,0:T(8,128)}, f32[12,96,128]{2,1,0:T(8,128)}) custom-call(s32[2048]{0:T(1024)} %seam.1, f32[12,96,128]{2,1,0:T(8,128)} %heat.1, f32[12,96,128]{2,1,0:T(8,128)} %salt.1, f32[12,96,128]{2,1,0:T(8,128)} %zonal.1, f32[12,96,128]{2,1,0:T(8,128)} %meridional.1, s32[96,128]{1,0:T(8,128)} %sea.1, s32[96,128]{1,0:T(8,128)} %depth.1), custom_call_target="tpu_custom_call" | custom-call | tf_op jit(solution)/shard_map/pallas_call | solution.py:541
  55.9 0.0 copy-start
  55.9 2.0 %copy.11 = f32[12,96,128]{2,1,0:T(8,128)} copy(f32[12,96,128]{2,1,0:T(8,128)} %get-tuple-element.4) | data formatting | bytes 1179648
  57.9 0.0 copy-done
  57.9 0.8 %copy.12 = f32[12,96,128]{2,1,0:T(8,128)} copy(f32[12,96,128]{2,1,0:T(8,128)S(1)} %copy-done) | data formatting | bytes 1179648
Async XLA Ops:
  55.9 2.0 %copy-start = (f32[12,96,128]{2,1,0:T(8,128)S(1)}, f32[12,96,128]{2,1,0:T(8,128)}, u32[]{:S(2)}) copy-start(f32[12,96,128]{2,1,0:T(8,128)} %get-tuple-element.5) | copy-start | bytes 1769476

commit v9 on v8

--- a/solution.py
+++ b/solution.py
@@ -289,7 +289,7 @@
 def buffers_for(fields, levels, height, width, lon):
     columns = pltpu.VMEM((fields, 16, height), jnp.float32)
     rows = pltpu.VMEM((fields, levels, width), jnp.float32)
-    halo = pltpu.VMEM((fields, levels, height, 1), jnp.float32)
+    halo = pltpu.VMEM((fields, levels, height, width), jnp.float32)
     return [
         columns,
         columns,
@@ -428,11 +428,16 @@
         to_west.wait()
         to_east.wait()
 
+        edge = lax.broadcasted_iota(jnp.int32, (height, width), 1)
         for f in range(fields):
-            both = jnp.concatenate([whalo[f], ehalo[f]], axis=0).T
+            rows = whalo.shape[1]
+            spread = jnp.concatenate(
+                [whalo[f], ehalo[f], jnp.zeros((width - 2 * rows, height), jnp.float32)], axis=0
+            ).T
             for k in range(levels):
-                wcol[f, k] = both[:, k : k + 1]
-                ecol[f, k] = both[:, 16 + k : 17 + k]
+                west_lane = spread if k == 0 else pltpu.roll(spread, width - k, 1)
+                east_lane = pltpu.roll(spread, width - 1 - rows - k, 1)
+                wcol[f, k] = jnp.where(edge == 0, west_lane, east_lane)
 
         def finish():
             @pl.when(has_south)
@@ -480,7 +485,7 @@
                     )
                     north[f] = ghost * (signs[f] if s == 0 else 1.0)
 
-        return (source, wcol, ecol, ssend, nsend), (source, wcol, ecol, shalo, north), finish
+        return (source, wcol, wcol, ssend, nsend), (source, wcol, wcol, shalo, north), finish
 
     def run(stage, finish):
         stage(False)

time: 59.2 us -> 55.5 us (0.938)
  Pallas kernels: 55.2 us -> 51.3 us
    pallas_call x1, Pallas kernels: 55.2 us -> 51.3 us  [fused(): pl.pallas_call(functools.partial(fused_kernel, lon, lat, STATE_SIGNS), ou...]
where the time goes in v9:
time: 55.5 us; the launch traced here: 54.8 us
  Pallas kernels  51.3 us (92%)
  local copies, waits for them, and re-layouts  2.8 us (5%)
  between operations  0.65 us (1%)
    pallas_call x1, Pallas kernels, fused(): pl.pallas_call(functools.partial(fused_kernel, lon, lat, STATE_SIGNS), ou...  51.3 us
    unnamed x4, local copies, waits for them, and re-layouts  2.8 us

profile of v9, /device:TPU:113, one launch (start us, length us, event | category | flops | bytes accessed | tf_op | source)
XLA Modules:
  0.0 54.8 jit_solution(11681406307145199474)
XLA Ops:
  0.6 51.3 %shard_map.86 = (f32[12,96,128]{2,1,0:T(8,128)}, f32[12,96,128]{2,1,0:T(8,128)}) custom-call(s32[2048]{0:T(1024)} %seam.1, f32[12,96,128]{2,1,0:T(8,128)} %heat.1, f32[12,96,128]{2,1,0:T(8,128)} %salt.1, f32[12,96,128]{2,1,0:T(8,128)} %zonal.1, f32[12,96,128]{2,1,0:T(8,128)} %meridional.1, s32[96,128]{1,0:T(8,128)} %sea.1, s32[96,128]{1,0:T(8,128)} %depth.1), custom_call_target="tpu_custom_call" | custom-call | tf_op jit(solution)/shard_map/pallas_call | solution.py:546
  52.0 0.0 copy-start
  52.0 2.0 %copy.11 = f32[12,96,128]{2,1,0:T(8,128)} copy(f32[12,96,128]{2,1,0:T(8,128)} %get-tuple-element.4) | data formatting | bytes 1179648
  54.0 0.0 copy-done
  54.0 0.8 %copy.12 = f32[12,96,128]{2,1,0:T(8,128)} copy(f32[12,96,128]{2,1,0:T(8,128)S(1)} %copy-done) | data formatting | bytes 1179648
Async XLA Ops:
  52.0 2.0 %copy-start = (f32[12,96,128]{2,1,0:T(8,128)S(1)}, f32[12,96,128]{2,1,0:T(8,128)}, u32[]{:S(2)}) copy-start(f32[12,96,128]{2,1,0:T(8,128)} %get-tuple-element.5) | copy-start | bytes 1769476

commit v10 on v9

--- a/solution.py
+++ b/solution.py
@@ -56,16 +56,15 @@
 
 def sides_of(refs, f, k, rows=False):
     block, west, east, south, north = refs
+    line = pl.ds(f * block.shape[1] + k, 1)
     if not rows:
-        return around(
-            block[f, k], west[f, k], east[f, k], south[f, pl.ds(k, 1), :], north[f, pl.ds(k, 1), :]
-        )
+        return around(block[f, k], west[f, k], east[f, k], south[line, :], north[line, :])
     height = west.shape[2]
     low = block[f, k, pl.ds(0, 2), :]
     high = block[f, k, pl.ds(height - 2, 2), :]
     centre = pick_rows(low[0:1], high[1:2])
-    at_north = pick_rows(low[1:2], north[f, pl.ds(k, 1), :])
-    at_south = pick_rows(south[f, pl.ds(k, 1), :], high[0:1])
+    at_north = pick_rows(low[1:2], north[line, :])
+    at_south = pick_rows(south[line, :], high[0:1])
     west_end = pick_rows(west[f, k, pl.ds(0, 1), :], west[f, k, pl.ds(height - 1, 1), :])
     east_end = pick_rows(east[f, k, pl.ds(0, 1), :], east[f, k, pl.ds(height - 1, 1), :])
     width = centre.shape[1]
@@ -288,7 +287,7 @@
 
 def buffers_for(fields, levels, height, width, lon):
     columns = pltpu.VMEM((fields, 16, height), jnp.float32)
-    rows = pltpu.VMEM((fields, levels, width), jnp.float32)
+    rows = pltpu.VMEM((fields * levels, width), jnp.float32)
     halo = pltpu.VMEM((fields, levels, height, width), jnp.float32)
     return [
         columns,
@@ -299,7 +298,7 @@
         columns,
         rows,
         rows,
-        pltpu.VMEM((lon, fields, levels, width), jnp.float32),
+        pltpu.VMEM((lon, fields * levels, width), jnp.float32),
         halo,
         halo,
         rows,
@@ -374,8 +373,8 @@
                 flipped = tile.T
                 wsend[f, pl.ds(k, 1), :] = flipped[0:1, :]
                 esend[f, pl.ds(k, 1), :] = flipped[width - 1 : width, :]
-                ssend[f, pl.ds(k, 1), :] = tile[0:1, :]
-                nsend[f, pl.ds(k, 1), :] = tile[height - 1 : height, :]
+                ssend[pl.ds(f * levels + k, 1), :] = tile[0:1, :]
+                nsend[pl.ds(f * levels + k, 1), :] = tile[height - 1 : height, :]
             spare = wsend.shape[1] - levels
             wsend[f, pl.ds(levels, spare), :] = jnp.zeros((spare, height), jnp.float32)
             esend[f, pl.ds(levels, spare), :] = jnp.zeros((spare, height), jnp.float32)
@@ -471,19 +470,25 @@
 
             @pl.when(on_top)
             def _():
-                for f in range(fields):
-                    ghost = jnp.dot(
-                        gathered[lower, f],
-                        reverse[0],
-                        precision=lax.Precision.HIGHEST,
-                        preferred_element_type=jnp.float32,
-                    ) + jnp.dot(
-                        gathered[upper, f],
-                        reverse[1],
-                        precision=lax.Precision.HIGHEST,
-                        preferred_element_type=jnp.float32,
-                    )
-                    north[f] = ghost * (signs[f] if s == 0 else 1.0)
+                ghost = jnp.dot(
+                    gathered[lower],
+                    reverse[0],
+                    precision=lax.Precision.HIGHEST,
+                    preferred_element_type=jnp.float32,
+                ) + jnp.dot(
+                    gathered[upper],
+                    reverse[1],
+                    precision=lax.Precision.HIGHEST,
+                    preferred_element_type=jnp.float32,
+                )
+                if s == 0:
+                    line = lax.broadcasted_iota(jnp.int32, ghost.shape, 0)
+                    sign = jnp.ones(ghost.shape, jnp.float32)
+                    for f in range(fields):
+                        owned = (line >= f * levels) & (line < (f + 1) * levels)
+                        sign = jnp.where(owned, signs[f], sign)
+                    ghost = ghost * sign
+                north[...] = ghost
 
         return (source, wcol, wcol, ssend, nsend), (source, wcol, wcol, shalo, north), finish
 

time: 55.5 us -> 54.5 us (0.982)
  Pallas kernels: 51.3 us -> 50.4 us
    pallas_call x1, Pallas kernels: 51.3 us -> 50.4 us  [fused(): pl.pallas_call(functools.partial(fused_kernel, lon, lat, STATE_SIGNS), ou...]
where the time goes in v10:
time: 54.5 us; the launch traced here: 53.8 us
  Pallas kernels  50.4 us (92%)
  local copies, waits for them, and re-layouts  2.8 us (5%)
  between operations  0.65 us (1%)
    pallas_call x1, Pallas kernels, fused(): pl.pallas_call(functools.partial(fused_kernel, lon, lat, STATE_SIGNS), ou...  50.4 us
    unnamed x4, local copies, waits for them, and re-layouts  2.8 us

profile of v10, /device:TPU:113, one launch (start us, length us, event | category | flops | bytes accessed | tf_op | source)
XLA Modules:
  0.0 53.8 jit_solution(5555807164195192996)
XLA Ops:
  0.6 50.4 %shard_map.86 = (f32[12,96,128]{2,1,0:T(8,128)}, f32[12,96,128]{2,1,0:T(8,128)}) custom-call(s32[2048]{0:T(1024)} %seam.1, f32[12,96,128]{2,1,0:T(8,128)} %heat.1, f32[12,96,128]{2,1,0:T(8,128)} %salt.1, f32[12,96,128]{2,1,0:T(8,128)} %zonal.1, f32[12,96,128]{2,1,0:T(8,128)} %meridional.1, s32[96,128]{1,0:T(8,128)} %sea.1, s32[96,128]{1,0:T(8,128)} %depth.1), custom_call_target="tpu_custom_call" | custom-call | tf_op jit(solution)/shard_map/pallas_call | solution.py:551
  51.0 0.0 copy-start
  51.0 2.0 %copy.11 = f32[12,96,128]{2,1,0:T(8,128)} copy(f32[12,96,128]{2,1,0:T(8,128)} %get-tuple-element.4) | data formatting | bytes 1179648
  53.0 0.0 copy-done
  53.0 0.8 %copy.12 = f32[12,96,128]{2,1,0:T(8,128)} copy(f32[12,96,128]{2,1,0:T(8,128)S(1)} %copy-done) | data formatting | bytes 1179648
Async XLA Ops:
  51.0 2.0 %copy-start = (f32[12,96,128]{2,1,0:T(8,128)S(1)}, f32[12,96,128]{2,1,0:T(8,128)}, u32[]{:S(2)}) copy-start(f32[12,96,128]{2,1,0:T(8,128)} %get-tuple-element.5) | copy-start | bytes 1769476

commit v11 on v10

--- a/solution.py
+++ b/solution.py
@@ -370,9 +370,13 @@
         for f in range(fields):
             for k in range(levels):
                 tile = source[f, k]
-                flipped = tile.T
-                wsend[f, pl.ds(k, 1), :] = flipped[0:1, :]
-                esend[f, pl.ds(k, 1), :] = flipped[width - 1 : width, :]
+                if s == 0 and f == 3:
+                    wsend[f, pl.ds(k, 1), :] = jnp.zeros((1, height), jnp.float32)
+                    esend[f, pl.ds(k, 1), :] = jnp.zeros((1, height), jnp.float32)
+                else:
+                    flipped = tile.T
+                    wsend[f, pl.ds(k, 1), :] = flipped[0:1, :]
+                    esend[f, pl.ds(k, 1), :] = flipped[width - 1 : width, :]
                 ssend[pl.ds(f * levels + k, 1), :] = tile[0:1, :]
                 nsend[pl.ds(f * levels + k, 1), :] = tile[height - 1 : height, :]
             spare = wsend.shape[1] - levels
@@ -429,6 +433,9 @@
 
         edge = lax.broadcasted_iota(jnp.int32, (height, width), 1)
         for f in range(fields):
+            if s == 0 and f == 3:
+                wcol[f] = jnp.zeros(wcol.shape[1:], jnp.float32)
+                continue
             rows = whalo.shape[1]
             spread = jnp.concatenate(
                 [whalo[f], ehalo[f], jnp.zeros((width - 2 * rows, height), jnp.float32)], axis=0

time: 54.5 us -> 54.1 us (level)
  no operation moved by 1% of the time
where the time goes in v11:
time: 54.1 us; the launch traced here: 53.5 us
  Pallas kernels  50 us (92%)
  local copies, waits for them, and re-layouts  2.8 us (5%)
  between operations  0.65 us (1%)
    pallas_call x1, Pallas kernels, fused(): pl.pallas_call(functools.partial(fused_kernel, lon, lat, STATE_SIGNS), ou...  50 us
    unnamed x4, local copies, waits for them, and re-layouts  2.8 us

profile of v11, /device:TPU:113, one launch (start us, length us, event | category | flops | bytes accessed | tf_op | source)
XLA Modules:
  0.0 53.5 jit_solution(15650455725452611176)
XLA Ops:
  0.6 50.0 %shard_map.86 = (f32[12,96,128]{2,1,0:T(8,128)}, f32[12,96,128]{2,1,0:T(8,128)}) custom-call(s32[2048]{0:T(1024)} %seam.1, f32[12,96,128]{2,1,0:T(8,128)} %heat.1, f32[12,96,128]{2,1,0:T(8,128)} %salt.1, f32[12,96,128]{2,1,0:T(8,128)} %zonal.1, f32[12,96,128]{2,1,0:T(8,128)} %meridional.1, s32[96,128]{1,0:T(8,128)} %sea.1, s32[96,128]{1,0:T(8,128)} %depth.1), custom_call_target="tpu_custom_call" | custom-call | tf_op jit(solution)/shard_map/pallas_call | solution.py:558
  50.6 0.0 copy-start
  50.7 2.0 %copy.11 = f32[12,96,128]{2,1,0:T(8,128)} copy(f32[12,96,128]{2,1,0:T(8,128)} %get-tuple-element.4) | data formatting | bytes 1179648
  52.6 0.0 copy-done
  52.6 0.8 %copy.12 = f32[12,96,128]{2,1,0:T(8,128)} copy(f32[12,96,128]{2,1,0:T(8,128)S(1)} %copy-done) | data formatting | bytes 1179648
Async XLA Ops:
  50.6 2.0 %copy-start = (f32[12,96,128]{2,1,0:T(8,128)S(1)}, f32[12,96,128]{2,1,0:T(8,128)}, u32[]{:S(2)}) copy-start(f32[12,96,128]{2,1,0:T(8,128)} %get-tuple-element.5) | copy-start | bytes 1769476

commit v12 on v11

--- a/solution.py
+++ b/solution.py
@@ -222,12 +222,21 @@
 def isopycnal_kernel(advected_refs, state_refs, out, rows=False):
     levels = out.shape[1]
 
-    def body(k, carry):
-        above = jnp.minimum(k + 1, levels - 1)
+    def level(k):
         values = [sides_of(advected_refs, tracer, k, rows) for tracer in range(2)]
-        uppers = [sides_of(advected_refs, tracer, above, rows) for tracer in range(2)]
-        wet_sides = sides_of(state_refs, 4, k, rows)
-        wet_above = sides_of(state_refs, 4, above, rows)
+        return values, sides_of(state_refs, 4, k, rows)
+
+    def body(pair, carry):
+        k = 2 * pair
+        lower, middle = level(k), level(k + 1)
+        upper = level(jnp.minimum(k + 2, levels - 1))
+        emit(k, lower, middle)
+        emit(k + 1, middle, upper)
+        return carry
+
+    def emit(k, here, there):
+        values, wet_sides = here
+        uppers, wet_above = there
         stacked = [w * a for w, a in zip(wet_sides, wet_above)]
         verticals = [
             [(u - v) * s for u, v, s in zip(uppers[tracer], values[tracer], stacked)]
@@ -262,9 +271,8 @@
             south_flux = face_flux(4, 0)
             result = value[0] + wet_sides[0] * (east_flux - west_flux + north_flux - south_flux)
             store_view(out, (tracer, k), result, rows)
-        return carry
-
-    lax.fori_loop(0, levels, body, 0)
+
+    lax.fori_loop(0, levels // 2, body, 0)
 
 
 class Stack:

time: 54.1 us -> 53.4 us (0.987)
  Pallas kernels: 50 us -> 49.2 us
    pallas_call x1, Pallas kernels: 50 us -> 49.2 us  [fused(): pl.pallas_call(functools.partial(fused_kernel, lon, lat, STATE_SIGNS), ou...]
where the time goes in v12:
time: 53.4 us; the launch traced here: 52.7 us
  Pallas kernels  49.2 us (92%)
  local copies, waits for them, and re-layouts  2.8 us (5%)
  between operations  0.65 us (1%)
    pallas_call x1, Pallas kernels, fused(): pl.pallas_call(functools.partial(fused_kernel, lon, lat, STATE_SIGNS), ou...  49.2 us
    unnamed x4, local copies, waits for them, and re-layouts  2.8 us

profile of v12, /device:TPU:113, one launch (start us, length us, event | category | flops | bytes accessed | tf_op | source)
XLA Modules:
  0.0 52.7 jit_solution(13617227409586601457)
XLA Ops:
  0.6 49.2 %shard_map.86 = (f32[12,96,128]{2,1,0:T(8,128)}, f32[12,96,128]{2,1,0:T(8,128)}) custom-call(s32[2048]{0:T(1024)} %seam.1, f32[12,96,128]{2,1,0:T(8,128)} %heat.1, f32[12,96,128]{2,1,0:T(8,128)} %salt.1, f32[12,96,128]{2,1,0:T(8,128)} %zonal.1, f32[12,96,128]{2,1,0:T(8,128)} %meridional.1, s32[96,128]{1,0:T(8,128)} %sea.1, s32[96,128]{1,0:T(8,128)} %depth.1), custom_call_target="tpu_custom_call" | custom-call | tf_op jit(solution)/shard_map/pallas_call | solution.py:566
  49.9 0.0 copy-start
  49.9 2.0 %copy.11 = f32[12,96,128]{2,1,0:T(8,128)} copy(f32[12,96,128]{2,1,0:T(8,128)} %get-tuple-element.4) | data formatting | bytes 1179648
  51.9 0.0 copy-done
  51.9 0.8 %copy.12 = f32[12,96,128]{2,1,0:T(8,128)} copy(f32[12,96,128]{2,1,0:T(8,128)S(1)} %copy-done) | data formatting | bytes 1179648
Async XLA Ops:
  49.9 2.0 %copy-start = (f32[12,96,128]{2,1,0:T(8,128)S(1)}, f32[12,96,128]{2,1,0:T(8,128)}, u32[]{:S(2)}) copy-start(f32[12,96,128]{2,1,0:T(8,128)} %get-tuple-element.5) | copy-start | bytes 1769476

commit v13 on v12

--- a/solution.py
+++ b/solution.py
@@ -181,7 +181,7 @@
             store_view(flow_out, (2 + tracer, k), outflow, rows)
         return carry
 
-    lax.fori_loop(0, levels, body, 0)
+    lax.fori_loop(0, levels, body, 0, unroll=2)
 
 
 def ratio_kernel(state_refs, upwind_refs, flow, out, rows=False):
@@ -200,7 +200,7 @@
             store_view(out, (2 + tracer, k), minus, rows)
         return carry
 
-    lax.fori_loop(0, levels, body, 0)
+    lax.fori_loop(0, levels, body, 0, unroll=2)
 
 
 def advected_kernel(wet, upwind_ref, anti_ref, ratio_refs, out, rows=False):
@@ -216,7 +216,7 @@
             store_view(out, (tracer, k), limited(plus, minus, upwind, anti, wet_centre), rows)
         return carry
 
-    lax.fori_loop(0, levels, body, 0)
+    lax.fori_loop(0, levels, body, 0, unroll=2)
 
 
 def isopycnal_kernel(advected_refs, state_refs, out, rows=False):

time: 53.4 us -> 51.4 us (0.963)
  Pallas kernels: 49.2 us -> 47.8 us
    pallas_call x1, Pallas kernels: 49.2 us -> 47.8 us  [fused(): pl.pallas_call(functools.partial(fused_kernel, lon, lat, STATE_SIGNS), ou...]
where the time goes in v13:
time: 51.4 us; the launch traced here: 51.2 us
  Pallas kernels  47.8 us (93%)
  local copies, waits for them, and re-layouts  2.8 us (5%)
  between operations  0.65 us (1%)
    pallas_call x1, Pallas kernels, fused(): pl.pallas_call(functools.partial(fused_kernel, lon, lat, STATE_SIGNS), ou...  47.8 us
    unnamed x4, local copies, waits for them, and re-layouts  2.8 us

profile of v13, /device:TPU:113, one launch (start us, length us, event | category | flops | bytes accessed | tf_op | source)
XLA Modules:
  0.0 51.2 jit_solution(9580292353240983585)
XLA Ops:
  0.6 47.8 %shard_map.86 = (f32[12,96,128]{2,1,0:T(8,128)}, f32[12,96,128]{2,1,0:T(8,128)}) custom-call(s32[2048]{0:T(1024)} %seam.1, f32[12,96,128]{2,1,0:T(8,128)} %heat.1, f32[12,96,128]{2,1,0:T(8,128)} %salt.1, f32[12,96,128]{2,1,0:T(8,128)} %zonal.1, f32[12,96,128]{2,1,0:T(8,128)} %meridional.1, s32[96,128]{1,0:T(8,128)} %sea.1, s32[96,128]{1,0:T(8,128)} %depth.1), custom_call_target="tpu_custom_call" | custom-call | tf_op jit(solution)/shard_map/pallas_call | solution.py:566
  48.4 0.0 copy-start
  48.4 2.0 %copy.11 = f32[12,96,128]{2,1,0:T(8,128)} copy(f32[12,96,128]{2,1,0:T(8,128)} %get-tuple-element.4) | data formatting | bytes 1179648
  50.4 0.0 copy-done
  50.4 0.8 %copy.12 = f32[12,96,128]{2,1,0:T(8,128)} copy(f32[12,96,128]{2,1,0:T(8,128)S(1)} %copy-done) | data formatting | bytes 1179648
Async XLA Ops:
  48.4 2.0 %copy-start = (f32[12,96,128]{2,1,0:T(8,128)S(1)}, f32[12,96,128]{2,1,0:T(8,128)}, u32[]{:S(2)}) copy-start(f32[12,96,128]{2,1,0:T(8,128)} %get-tuple-element.5) | copy-start | bytes 1769476

commit v14 on v13

--- a/solution.py
+++ b/solution.py
@@ -181,7 +181,7 @@
             store_view(flow_out, (2 + tracer, k), outflow, rows)
         return carry
 
-    lax.fori_loop(0, levels, body, 0, unroll=2)
+    lax.fori_loop(0, levels, body, 0, unroll=3)
 
 
 def ratio_kernel(state_refs, upwind_refs, flow, out, rows=False):
@@ -200,7 +200,7 @@
             store_view(out, (2 + tracer, k), minus, rows)
         return carry
 
-    lax.fori_loop(0, levels, body, 0, unroll=2)
+    lax.fori_loop(0, levels, body, 0, unroll=3)
 
 
 def advected_kernel(wet, upwind_ref, anti_ref, ratio_refs, out, rows=False):
@@ -216,7 +216,7 @@
             store_view(out, (tracer, k), limited(plus, minus, upwind, anti, wet_centre), rows)
         return carry
 
-    lax.fori_loop(0, levels, body, 0, unroll=2)
+    lax.fori_loop(0, levels, body, 0, unroll=3)
 
 
 def isopycnal_kernel(advected_refs, state_refs, out, rows=False):

time: 51.4 us -> 50.7 us (0.986)
  Pallas kernels: 47.8 us -> 47.1 us
    pallas_call x1, Pallas kernels: 47.8 us -> 47.1 us  [fused(): pl.pallas_call(functools.partial(fused_kernel, lon, lat, STATE_SIGNS), ou...]
where the time goes in v14:
time: 50.7 us; the launch traced here: 50.6 us
  Pallas kernels  47.1 us (93%)
  local copies, waits for them, and re-layouts  2.8 us (6%)
  between operations  0.65 us (1%)
    pallas_call x1, Pallas kernels, fused(): pl.pallas_call(functools.partial(fused_kernel, lon, lat, STATE_SIGNS), ou...  47.1 us
    unnamed x4, local copies, waits for them, and re-layouts  2.8 us

profile of v14, /device:TPU:113, one launch (start us, length us, event | category | flops | bytes accessed | tf_op | source)
XLA Modules:
  0.0 50.6 jit_solution(15489967268057103209)
XLA Ops:
  0.6 47.1 %shard_map.86 = (f32[12,96,128]{2,1,0:T(8,128)}, f32[12,96,128]{2,1,0:T(8,128)}) custom-call(s32[2048]{0:T(1024)} %seam.1, f32[12,96,128]{2,1,0:T(8,128)} %heat.1, f32[12,96,128]{2,1,0:T(8,128)} %salt.1, f32[12,96,128]{2,1,0:T(8,128)} %zonal.1, f32[12,96,128]{2,1,0:T(8,128)} %meridional.1, s32[96,128]{1,0:T(8,128)} %sea.1, s32[96,128]{1,0:T(8,128)} %depth.1), custom_call_target="tpu_custom_call" | custom-call | tf_op jit(solution)/shard_map/pallas_call | solution.py:566
  47.8 0.0 copy-start
  47.8 2.0 %copy.11 = f32[12,96,128]{2,1,0:T(8,128)} copy(f32[12,96,128]{2,1,0:T(8,128)} %get-tuple-element.4) | data formatting | bytes 1179648
  49.8 0.0 copy-done
  49.8 0.8 %copy.12 = f32[12,96,128]{2,1,0:T(8,128)} copy(f32[12,96,128]{2,1,0:T(8,128)S(1)} %copy-done) | data formatting | bytes 1179648
Async XLA Ops:
  47.8 2.0 %copy-start = (f32[12,96,128]{2,1,0:T(8,128)S(1)}, f32[12,96,128]{2,1,0:T(8,128)}, u32[]{:S(2)}) copy-start(f32[12,96,128]{2,1,0:T(8,128)} %get-tuple-element.5) | copy-start | bytes 1769476

commit v15 on v14

--- a/solution.py
+++ b/solution.py
@@ -181,7 +181,7 @@
             store_view(flow_out, (2 + tracer, k), outflow, rows)
         return carry
 
-    lax.fori_loop(0, levels, body, 0, unroll=3)
+    lax.fori_loop(0, levels, body, 0, unroll=4)
 
 
 def ratio_kernel(state_refs, upwind_refs, flow, out, rows=False):
@@ -200,7 +200,7 @@
             store_view(out, (2 + tracer, k), minus, rows)
         return carry
 
-    lax.fori_loop(0, levels, body, 0, unroll=3)
+    lax.fori_loop(0, levels, body, 0, unroll=4)
 
 
 def advected_kernel(wet, upwind_ref, anti_ref, ratio_refs, out, rows=False):
@@ -216,7 +216,7 @@
             store_view(out, (tracer, k), limited(plus, minus, upwind, anti, wet_centre), rows)
         return carry
 
-    lax.fori_loop(0, levels, body, 0, unroll=3)
+    lax.fori_loop(0, levels, body, 0, unroll=4)
 
 
 def isopycnal_kernel(advected_refs, state_refs, out, rows=False):

time: 50.7 us -> 50.5 us (level)
  no operation moved by 1% of the time
where the time goes in v15:
time: 50.5 us; the launch traced here: 50.2 us
  Pallas kernels  46.7 us (92%)
  local copies, waits for them, and re-layouts  2.8 us (6%)
  between operations  0.65 us (1%)
    pallas_call x1, Pallas kernels, fused(): pl.pallas_call(functools.partial(fused_kernel, lon, lat, STATE_SIGNS), ou...  46.7 us
    unnamed x4, local copies, waits for them, and re-layouts  2.8 us

profile of v15, /device:TPU:113, one launch (start us, length us, event | category | flops | bytes accessed | tf_op | source)
XLA Modules:
  0.0 50.2 jit_solution(18391845229425918655)
XLA Ops:
  0.6 46.7 %shard_map.86 = (f32[12,96,128]{2,1,0:T(8,128)}, f32[12,96,128]{2,1,0:T(8,128)}) custom-call(s32[2048]{0:T(1024)} %seam.1, f32[12,96,128]{2,1,0:T(8,128)} %heat.1, f32[12,96,128]{2,1,0:T(8,128)} %salt.1, f32[12,96,128]{2,1,0:T(8,128)} %zonal.1, f32[12,96,128]{2,1,0:T(8,128)} %meridional.1, s32[96,128]{1,0:T(8,128)} %sea.1, s32[96,128]{1,0:T(8,128)} %depth.1), custom_call_target="tpu_custom_call" | custom-call | tf_op jit(solution)/shard_map/pallas_call | solution.py:566
  47.4 0.0 copy-start
  47.4 2.0 %copy.11 = f32[12,96,128]{2,1,0:T(8,128)} copy(f32[12,96,128]{2,1,0:T(8,128)} %get-tuple-element.4) | data formatting | bytes 1179648
  49.4 0.0 copy-done
  49.4 0.8 %copy.12 = f32[12,96,128]{2,1,0:T(8,128)} copy(f32[12,96,128]{2,1,0:T(8,128)S(1)} %copy-done) | data formatting | bytes 1179648
Async XLA Ops:
  47.4 2.0 %copy-start = (f32[12,96,128]{2,1,0:T(8,128)S(1)}, f32[12,96,128]{2,1,0:T(8,128)}, u32[]{:S(2)}) copy-start(f32[12,96,128]{2,1,0:T(8,128)} %get-tuple-element.5) | copy-start | bytes 1769476
